TPU v7x, 32 devices: a whole 2x2x4 slice. The times are simulated.
32 devices in a mesh: dp: 4 (over y, x), expert: 8 (over z, core).
Axes of the slice: x: 2, y: 2, z: 4, core: 2. Of those that a mesh axis runs over, the one named last changes fastest.
Arguments:
- hidden_in: bfloat16 [4096, 2048], P(('dp', 'expert')), may hold values from -6 to 6
- out_grad: bfloat16 [4096, 2048], P(('dp', 'expert')), may hold values from -6 to 6
- lengths: int32 [4, 5], P('dp'), may hold values from 1 to 512, 1024 in all within a row
- routes: int32 [4096, 4], P(('dp', 'expert')), may hold values from 0 to 7, all different within a row; in each aligned block of 128 rows (0 to 127, 128 to 255, ...) at most 128 rows name the same one
- norm1_gain: bfloat16 [2048], P(('dp', 'expert')), may hold values from 0.5 to 1.5
- qkv_weight: bfloat16 [2048, 6144], P(('dp', 'expert')), may hold values from -0.125 to 0.125
- qkv_bias: bfloat16 [6144], P(('dp', 'expert')), may hold values from -0.625 to 0.625
- out_weight: bfloat16 [2048, 2048], P(('dp', 'expert')), may hold values from -1 to 1
- norm2_gain: bfloat16 [2048], P(('dp', 'expert')), may hold values from 0.5 to 1.5
- router_weight: bfloat16 [2048, 8], P(('dp', 'expert')), may hold values from -0.0625 to 0.0625
- shared_gate: bfloat16 [2048], P(('dp', 'expert')), may hold values from -0.125 to 0.125
- shared_in: bfloat16 [2048, 11264], P(('dp', 'expert')), may hold values from -0.125 to 0.125
- shared_out: bfloat16 [5632, 2048], P(('dp', 'expert')), may hold values from -0.15625 to 0.15625
- expert_in: bfloat16 [8, 2048, 2816], P('expert', 'dp'), may hold values from -0.125 to 0.125
- expert_out: bfloat16 [8, 1408, 2048], P('expert', 'dp'), may hold values from -0.5 to 0.5
Outputs:
- output: bfloat16 [4096, 2048], P(('dp', 'expert'))
- input_grad: bfloat16 [4096, 2048], P(('dp', 'expert'))
- grad_norm1: float32 [2048], P(('dp', 'expert'))
- grad_qkv: float32 [2048, 6144], P(('dp', 'expert'))
- grad_bias: float32 [6144], P(('dp', 'expert'))
- grad_out_weight: float32 [2048, 2048], P(('dp', 'expert'))
- grad_norm2: float32 [2048], P(('dp', 'expert'))
- grad_router: float32 [2048, 8], P(('dp', 'expert'))
- grad_shared_gate: float32 [2048], P(('dp', 'expert'))
- grad_shared_in: float32 [2048, 11264], P(('dp', 'expert'))
- grad_shared_out: float32 [5632, 2048], P(('dp', 'expert'))
- grad_expert_in: float32 [8, 2048, 2816], P('expert', 'dp')
- grad_expert_out: float32 [8, 1408, 2048], P('expert', 'dp')
Inputs may be any that keep to these rules, and one draw needn't show every extreme that they name: `routes`: each row names 4 different experts. Among the 128 rows of one device, no expert is named more than 128 times, a bound that some block reaches. Row g belongs to data group g and sums to 1024: its first 4 entries are the group's sequence lengths in order, the last is the padding after them. Some entry equals 512.
All inputs are finite; a program needn't handle non-finite values.
Results may differ from a plain program's by a relative error of at most 0.015.
Values may be sent and summed in bfloat16 or wider, within the bound.
A program may use at most 448 MiB of HBM per device.

v0:
```python
import jax
import jax.numpy as jnp
from jax import lax
from jax.sharding import PartitionSpec as P

HD = 128


EPSILON = 1e-06
THETA = 1000000.0
NEG_FILL = -1e30


def rms_scale(values):
    return lax.rsqrt(jnp.mean(values * values, axis=-1, keepdims=True) + EPSILON)


def rotary_tables(positions, head_size):
    half_size = head_size // 2
    steps_up = jnp.arange(half_size, dtype=jnp.float32) * (2.0 / head_size)
    inverse = THETA ** (-steps_up)
    angles = positions.astype(jnp.float32)[:, None] * inverse[None, :]
    angles = jnp.concatenate([angles, angles], axis=-1)
    return (jnp.cos(angles)[:, None, :], jnp.sin(angles)[:, None, :])


def rotate(values, cosine, sine):
    half_size = values.shape[-1] // 2
    turned = jnp.concatenate([-values[..., half_size:], values[..., :half_size]], axis=-1)
    return values * cosine + turned * sine


def rotate_back(grad_values, cosine, sine):
    half_size = grad_values.shape[-1] // 2
    scaled = grad_values * sine
    turned = jnp.concatenate([scaled[..., half_size:], -scaled[..., :half_size]], axis=-1)
    return grad_values * cosine + turned


def swiglu(gate_up):
    half_size = gate_up.shape[-1] // 2
    return jax.nn.silu(gate_up[..., :half_size]) * gate_up[..., half_size:]


def swiglu_back(gate_up, grad_hidden):
    half_size = gate_up.shape[-1] // 2
    gate_part = gate_up[..., :half_size]
    up_part = gate_up[..., half_size:]
    sigmoid_gate = jax.nn.sigmoid(gate_part)
    grad_gate = grad_hidden * up_part * sigmoid_gate * (1.0 + gate_part * (1.0 - sigmoid_gate))
    grad_up = grad_hidden * gate_part * sigmoid_gate
    return jnp.concatenate([grad_gate, grad_up], axis=-1)


def norm_back(values, scale_rows, gain, grad_normed):
    weighted = grad_normed * gain
    inner = jnp.mean(weighted * values, axis=-1, keepdims=True)
    grad_values = scale_rows * weighted - values * scale_rows * scale_rows * scale_rows * inner
    grad_gain = jnp.sum(grad_normed * values * scale_rows, axis=0)
    return (grad_values, grad_gain)


def segment_table(length_row, count):
    ends = jnp.cumsum(length_row, dtype=jnp.int32)
    starts = ends - length_row
    places = jnp.arange(count, dtype=jnp.int32)
    segment = jnp.sum(
        (places[:, None] >= ends[None, :-1]).astype(jnp.int32), axis=1, dtype=jnp.int32
    )
    owners = segment[:, None] == jnp.arange(length_row.shape[0], dtype=jnp.int32)[None, :]
    first = jnp.sum(jnp.where(owners, starts[None, :], 0), axis=1, dtype=jnp.int32)
    return (segment, places - first)


def per_device(
    hidden_in,
    out_grad,
    lengths,
    routes,
    norm1_gain,
    qkv_weight,
    qkv_bias,
    out_weight,
    norm2_gain,
    router_weight,
    shared_gate,
    shared_in,
    shared_out,
    expert_in,
    expert_out,
):
    highest = lax.Precision.HIGHEST
    row_count, model_width = hidden_in.shape
    head_count = model_width // HD
    group_size = lax.axis_size("expert")
    group_rows = row_count * group_size
    top_count = routes.shape[1]
    expert_count = router_weight.shape[1]
    local_count = expert_in.shape[0]
    capacity = max(2, 2 * row_count * top_count // expert_count)
    slot_count = expert_count * capacity
    score_scale = HD ** (-0.5)
    dense = (
        lax.all_gather(norm1_gain, ("dp", "expert"), axis=0, tiled=True),
        lax.all_gather(qkv_weight, ("dp", "expert"), axis=0, tiled=True),
        lax.all_gather(qkv_bias, ("dp", "expert"), axis=0, tiled=True),
        lax.all_gather(out_weight, ("dp", "expert"), axis=0, tiled=True),
        lax.all_gather(norm2_gain, ("dp", "expert"), axis=0, tiled=True),
        lax.all_gather(router_weight, ("dp", "expert"), axis=0, tiled=True),
        lax.all_gather(shared_gate, ("dp", "expert"), axis=0, tiled=True),
        lax.all_gather(shared_in, ("dp", "expert"), axis=0, tiled=True),
        lax.all_gather(shared_out, ("dp", "expert"), axis=0, tiled=True),
    )
    (
        gain_first,
        weight_qkv,
        bias_first,
        weight_out,
        gain_second,
        weight_router,
        weight_gate,
        weight_shared_in,
        weight_shared_out,
    ) = dense
    weight_expert_in, weight_expert_out = (
        lax.all_gather(expert_in, "dp", axis=1, tiled=True),
        lax.all_gather(expert_out, "dp", axis=1, tiled=True),
    )
    segment_all, position_all = segment_table(lengths[0], group_rows)
    first_row = lax.axis_index("expert") * row_count
    segment_mine = lax.dynamic_slice_in_dim(segment_all, first_row, row_count, 0)
    position_mine = lax.dynamic_slice_in_dim(position_all, first_row, row_count, 0)
    valid_rows = (segment_mine < lengths.shape[1] - 1).astype(jnp.float32)[:, None]
    cosine, sine = rotary_tables(position_mine, HD)
    allowed = (
        (segment_mine[:, None] == segment_all[None, :])
        & (position_mine[:, None] >= position_all[None, :])
    )[None]
    inputs = hidden_in.astype(jnp.float32)
    scale_first = rms_scale(inputs)
    gain_one = gain_first.astype(jnp.float32)
    normed_one = (inputs * scale_first * gain_one).astype(jnp.bfloat16)
    projected = jnp.dot(
        normed_one, weight_qkv, preferred_element_type=jnp.float32
    ) + bias_first.astype(jnp.float32)
    query_low = rotate(
        projected[:, :model_width].reshape(row_count, head_count, HD), cosine, sine
    ).astype(jnp.bfloat16)
    key_low = rotate(
        projected[:, model_width : 2 * model_width].reshape(row_count, head_count, HD), cosine, sine
    ).astype(jnp.bfloat16)
    value_low = (
        projected[:, 2 * model_width :].reshape(row_count, head_count, HD).astype(jnp.bfloat16)
    )
    keys_all, values_all = (
        lax.all_gather(key_low, "expert", axis=0, tiled=True),
        lax.all_gather(value_low, "expert", axis=0, tiled=True),
    )

    def score_rows(queries):
        raw = (
            jnp.einsum("qhd,khd->hqk", queries, keys_all, preferred_element_type=jnp.float32)
            * score_scale
        )
        return jnp.where(allowed, raw, NEG_FILL)

    scores = score_rows(query_low)
    peak = jnp.max(scores, axis=-1, keepdims=True)
    log_total = peak + jnp.log(jnp.sum(jnp.exp(scores - peak), axis=-1, keepdims=True))
    weights_low = jnp.exp(scores - log_total).astype(jnp.bfloat16)
    attended = (
        jnp.einsum("hqk,khd->qhd", weights_low, values_all, preferred_element_type=jnp.float32)
        .reshape(row_count, model_width)
        .astype(jnp.bfloat16)
    )
    middle = inputs + jnp.dot(attended, weight_out, preferred_element_type=jnp.float32)
    scale_second = rms_scale(middle)
    gain_two = gain_second.astype(jnp.float32)
    normed_two = (middle * scale_second * gain_two).astype(jnp.bfloat16)
    logits = jnp.dot(normed_two, weight_router, preferred_element_type=jnp.float32)
    gate_logit = jnp.dot(normed_two, weight_gate, preferred_element_type=jnp.float32)
    peak_logit = jnp.max(logits, axis=-1, keepdims=True)
    router_total = peak_logit + jnp.log(
        jnp.sum(jnp.exp(logits - peak_logit), axis=-1, keepdims=True)
    )
    router_probs = jnp.exp(logits - router_total)
    expert_ids = jnp.arange(expert_count, dtype=jnp.int32)
    chosen = routes[:, :, None] == expert_ids[None, None, :]
    chosen_float = chosen.astype(jnp.float32)
    gates = jnp.sum(chosen_float * router_probs[:, None, :], axis=2)
    flat_hits = chosen.reshape(row_count * top_count, expert_count).astype(jnp.int32)
    earlier = jnp.cumsum(flat_hits, axis=0, dtype=jnp.int32) - flat_hits
    slot_rank = jnp.sum(earlier * flat_hits, axis=1, dtype=jnp.int32)
    slot_of = routes.reshape(-1) * capacity + slot_rank
    slot_hits = (
        (slot_of[:, None] == jnp.arange(slot_count, dtype=jnp.int32)[None, :])
        .reshape(row_count, top_count, slot_count)
        .astype(jnp.float32)
    )
    placement_map = jnp.sum(slot_hits, axis=1)
    weighted_map = jnp.sum(slot_hits * gates[:, :, None], axis=1)
    send_rows = (
        jnp.einsum(
            "ts,td->sd",
            placement_map.astype(jnp.bfloat16),
            normed_two,
            preferred_element_type=jnp.float32,
        )
        .astype(jnp.bfloat16)
        .reshape(expert_count, capacity, model_width)
    )
    arrived = lax.all_to_all(send_rows, "expert", split_axis=0, concat_axis=0, tiled=True)
    item_count = arrived.shape[1]
    grouped = arrived.reshape(group_size, local_count, item_count, model_width)
    gate_up = jnp.einsum(
        "gecd,edf->gecf", grouped, weight_expert_in, preferred_element_type=jnp.float32
    )
    hidden_low = swiglu(gate_up).astype(jnp.bfloat16)
    produced = jnp.einsum(
        "gecf,efd->gecd", hidden_low, weight_expert_out, preferred_element_type=jnp.float32
    ).astype(jnp.bfloat16)
    produced_rows = produced.reshape(group_size * local_count, item_count, model_width)
    expert_gate_up = gate_up.reshape(group_size * local_count, item_count, gate_up.shape[-1])
    back_rows = lax.all_to_all(produced_rows, "expert", split_axis=0, concat_axis=0, tiled=True)
    back_float = back_rows.reshape(slot_count, model_width).astype(jnp.float32)
    routed = jnp.dot(weighted_map, back_float, precision=highest)
    shared_up = jnp.dot(normed_two, weight_shared_in, preferred_element_type=jnp.float32)
    shared_hidden = swiglu(shared_up).astype(jnp.bfloat16)
    shared_rows = jnp.dot(shared_hidden, weight_shared_out, preferred_element_type=jnp.float32)
    opener = jax.nn.sigmoid(gate_logit)[:, None]
    output = (valid_rows * (middle + routed + opener * shared_rows)).astype(jnp.bfloat16)
    held = (
        lax.all_gather(norm1_gain, ("dp", "expert"), axis=0, tiled=True),
        lax.all_gather(qkv_weight, ("dp", "expert"), axis=0, tiled=True),
        lax.all_gather(qkv_bias, ("dp", "expert"), axis=0, tiled=True),
        lax.all_gather(out_weight, ("dp", "expert"), axis=0, tiled=True),
        lax.all_gather(norm2_gain, ("dp", "expert"), axis=0, tiled=True),
        lax.all_gather(router_weight, ("dp", "expert"), axis=0, tiled=True),
        lax.all_gather(shared_gate, ("dp", "expert"), axis=0, tiled=True),
        lax.all_gather(shared_in, ("dp", "expert"), axis=0, tiled=True),
        lax.all_gather(shared_out, ("dp", "expert"), axis=0, tiled=True),
    )
    (
        gain_first,
        weight_qkv,
        bias_first,
        weight_out,
        gain_second,
        weight_router,
        weight_gate,
        weight_shared_in,
        weight_shared_out,
    ) = held
    gain_one = gain_first.astype(jnp.float32)
    gain_two = gain_second.astype(jnp.float32)
    grad_rows = out_grad.astype(jnp.float32) * valid_rows
    grad_shared_rows = (grad_rows * opener).astype(jnp.bfloat16)
    grad_gate_logit = (
        jnp.sum(grad_rows * shared_rows, axis=-1) * opener[:, 0] * (1.0 - opener[:, 0])
    ).astype(jnp.bfloat16)
    grad_shared_hidden = jnp.einsum(
        "td,fd->tf", grad_shared_rows, weight_shared_out, preferred_element_type=jnp.float32
    )
    grad_shared_up = swiglu_back(shared_up, grad_shared_hidden).astype(jnp.bfloat16)
    term_shared_out = jnp.einsum(
        "tf,td->fd", shared_hidden, grad_shared_rows, preferred_element_type=jnp.float32
    )
    term_shared_in = jnp.einsum(
        "td,tf->df", normed_two, grad_shared_up, preferred_element_type=jnp.float32
    )
    slot_product = jnp.einsum("td,sd->ts", grad_rows, back_float, precision=highest)
    grad_gates = jnp.sum(slot_hits * slot_product[:, None, :], axis=2)
    grad_probs = jnp.sum(chosen_float * grad_gates[:, :, None], axis=1)
    grad_logits = (
        router_probs * (grad_probs - jnp.sum(router_probs * grad_probs, axis=-1, keepdims=True))
    ).astype(jnp.bfloat16)
    term_router = jnp.einsum(
        "td,te->de", normed_two, grad_logits, preferred_element_type=jnp.float32
    )
    term_gate = jnp.einsum(
        "td,t->d", normed_two, grad_gate_logit, preferred_element_type=jnp.float32
    )
    grad_result = (
        jnp.einsum("ts,td->sd", weighted_map, grad_rows, precision=highest)
        .astype(jnp.bfloat16)
        .reshape(expert_count, capacity, model_width)
    )
    grad_arrived = lax.all_to_all(grad_result, "expert", split_axis=0, concat_axis=0, tiled=True)
    grad_grouped = grad_arrived.reshape(group_size, local_count, capacity, model_width)
    gate_up_grouped = expert_gate_up.reshape(
        group_size, local_count, capacity, expert_gate_up.shape[-1]
    )
    hidden_again = swiglu(gate_up_grouped).astype(jnp.bfloat16)
    grad_hidden = jnp.einsum(
        "gecd,efd->gecf", grad_grouped, weight_expert_out, preferred_element_type=jnp.float32
    )
    grad_gate_up = swiglu_back(gate_up_grouped, grad_hidden).astype(jnp.bfloat16)
    arrived_grouped = arrived.reshape(group_size, local_count, capacity, model_width)
    term_expert_in = jnp.einsum(
        "gecd,gecf->edf", arrived_grouped, grad_gate_up, preferred_element_type=jnp.float32
    )
    term_expert_out = jnp.einsum(
        "gecf,gecd->efd", hidden_again, grad_grouped, preferred_element_type=jnp.float32
    )
    grad_sent = jnp.einsum(
        "gecf,edf->gecd", grad_gate_up, weight_expert_in, preferred_element_type=jnp.float32
    ).reshape(group_size * local_count, capacity, model_width)
    grad_slots = lax.all_to_all(
        grad_sent.astype(jnp.bfloat16), "expert", split_axis=0, concat_axis=0, tiled=True
    ).astype(grad_sent.dtype)
    grad_expert_in, grad_expert_out = (
        lax.psum_scatter(
            term_expert_in.astype(jnp.bfloat16), "dp", scatter_dimension=1, tiled=True
        ).astype(jnp.float32),
        lax.psum_scatter(
            term_expert_out.astype(jnp.bfloat16), "dp", scatter_dimension=1, tiled=True
        ).astype(jnp.float32),
    )
    grad_normed_two = jnp.einsum(
        "te,de->td", grad_logits, weight_router, preferred_element_type=jnp.float32
    )
    grad_normed_two = (
        grad_normed_two
        + grad_gate_logit.astype(jnp.float32)[:, None] * weight_gate.astype(jnp.float32)[None, :]
    )
    grad_normed_two = grad_normed_two + jnp.einsum(
        "tf,df->td", grad_shared_up, weight_shared_in, preferred_element_type=jnp.float32
    )
    grad_normed_two = grad_normed_two + jnp.dot(
        placement_map, grad_slots.reshape(slot_count, model_width), precision=highest
    )
    grad_middle_norm, term_norm_two = norm_back(middle, scale_second, gain_two, grad_normed_two)
    grad_middle = grad_rows + grad_middle_norm
    grad_norm2, grad_router, grad_shared_gate, grad_shared_in, grad_shared_out = (
        lax.psum_scatter(term_norm_two, ("dp", "expert"), scatter_dimension=0, tiled=True),
        lax.psum_scatter(term_router, ("dp", "expert"), scatter_dimension=0, tiled=True),
        lax.psum_scatter(term_gate, ("dp", "expert"), scatter_dimension=0, tiled=True),
        lax.psum_scatter(term_shared_in, ("dp", "expert"), scatter_dimension=0, tiled=True),
        lax.psum_scatter(term_shared_out, ("dp", "expert"), scatter_dimension=0, tiled=True),
    )
    grad_branch = grad_middle.astype(jnp.bfloat16)
    term_out_weight = jnp.einsum(
        "td,te->de", attended, grad_branch, preferred_element_type=jnp.float32
    )
    grad_attended = (
        jnp.einsum("te,de->td", grad_branch, weight_out, preferred_element_type=jnp.float32)
        .astype(jnp.bfloat16)
        .reshape(row_count, head_count, HD)
    )
    weights_again = jnp.exp(score_rows(query_low) - log_total)
    weights_again_low = weights_again.astype(jnp.bfloat16)
    grad_weights = jnp.einsum(
        "qhd,khd->hqk", grad_attended, values_all, preferred_element_type=jnp.float32
    )
    delta_rows = jnp.sum(weights_again * grad_weights, axis=-1, keepdims=True)
    grad_scores = (weights_again * (grad_weights - delta_rows)).astype(jnp.bfloat16)
    grad_query_turned = (
        jnp.einsum("hqk,khd->qhd", grad_scores, keys_all, preferred_element_type=jnp.float32)
        * score_scale
    )
    grad_keys_all = (
        jnp.einsum("hqk,qhd->khd", grad_scores, query_low, preferred_element_type=jnp.float32)
        * score_scale
    )
    grad_values_all = jnp.einsum(
        "hqk,qhd->khd", weights_again_low, grad_attended, preferred_element_type=jnp.float32
    )
    grad_key_turned, grad_values = (
        lax.psum_scatter(
            grad_keys_all.astype(jnp.bfloat16), "expert", scatter_dimension=0, tiled=True
        ).astype(jnp.float32),
        lax.psum_scatter(
            grad_values_all.astype(jnp.bfloat16), "expert", scatter_dimension=0, tiled=True
        ).astype(jnp.float32),
    )
    grad_projected = jnp.concatenate(
        [
            rotate_back(grad_query_turned, cosine, sine).reshape(row_count, model_width),
            rotate_back(grad_key_turned, cosine, sine).reshape(row_count, model_width),
            grad_values.reshape(row_count, model_width),
        ],
        axis=-1,
    ).astype(jnp.bfloat16)
    term_bias = jnp.sum(grad_projected.astype(jnp.float32), axis=0)
    term_qkv = jnp.einsum(
        "td,tf->df", normed_one, grad_projected, preferred_element_type=jnp.float32
    )
    grad_normed_one = jnp.einsum(
        "tf,df->td", grad_projected, weight_qkv, preferred_element_type=jnp.float32
    )
    grad_input_norm, term_norm_one = norm_back(inputs, scale_first, gain_one, grad_normed_one)
    input_grad = (grad_middle + grad_input_norm).astype(jnp.bfloat16)
    grad_norm1, grad_qkv, grad_bias, grad_out_weight = (
        lax.psum_scatter(term_norm_one, ("dp", "expert"), scatter_dimension=0, tiled=True),
        lax.psum_scatter(term_qkv, ("dp", "expert"), scatter_dimension=0, tiled=True),
        lax.psum_scatter(term_bias, ("dp", "expert"), scatter_dimension=0, tiled=True),
        lax.psum_scatter(term_out_weight, ("dp", "expert"), scatter_dimension=0, tiled=True),
    )
    return (
        output,
        input_grad,
        grad_norm1,
        grad_qkv,
        grad_bias,
        grad_out_weight,
        grad_norm2,
        grad_router,
        grad_shared_gate,
        grad_shared_in,
        grad_shared_out,
        grad_expert_in,
        grad_expert_out,
    )


def solution(mesh):
    return jax.shard_map(
        per_device,
        mesh=mesh,
        in_specs=(
            P(("dp", "expert"), None),
            P(("dp", "expert"), None),
            P("dp", None),
            P(("dp", "expert"), None),
            P(("dp", "expert")),
            P(("dp", "expert"), None),
            P(("dp", "expert")),
            P(("dp", "expert"), None),
            P(("dp", "expert")),
            P(("dp", "expert"), None),
            P(("dp", "expert")),
            P(("dp", "expert"), None),
            P(("dp", "expert"), None),
            P("expert", "dp", None),
            P("expert", "dp", None),
        ),
        out_specs=(
            P(("dp", "expert"), None),
            P(("dp", "expert"), None),
            P(("dp", "expert")),
            P(("dp", "expert"), None),
            P(("dp", "expert")),
            P(("dp", "expert"), None),
            P(("dp", "expert")),
            P(("dp", "expert"), None),
            P(("dp", "expert")),
            P(("dp", "expert"), None),
            P(("dp", "expert"), None),
            P("expert", "dp", None),
            P("expert", "dp", None),
        ),
        check_vma=False,
    )
```

profile of v0, /device:TPU:0, one launch (start us, length us, event | category | flops | bytes accessed | tf_op | source)
XLA Modules:
  0.0 3790.5 jit_solution(11076804080346269259)
XLA Ops:
  12.2 43.4 %all-reduce.9 = (bf16[6144]{0:T(1024)(128)(2,1)S(1)}, bf16[2048]{0:T(1024)(128)(2,1)S(1)}, bf16[2048]{0:T(1024)(128)(2,1)S(1)}, bf16[2048]{0:T(1024)(128)(2,1)S(1)}) all-reduce(bf16[6144]{0:T(1024)(128)(2,1)S(1)} %dynamic-update-slice.1, bf16[2048]{0:T(1024)(128)(2,1)S(1)} %dynamic-update-slice, ...), channel_id=1, replica_groups=mesh['dp'=4,'expert'=8] {'dp','expert'}, use_global_device_ids=true, to_apply=%add.1 | all-reduce | flops 12288 | bytes 49152
  58.9 111.0 %all-gather.10.cloned.1.call-done = bf16[2048,6144]{1,0:T(8,128)(2,1)} async-done(((bf16[64,6144]{1,0:T(8,128)(2,1)}), bf16[2048,6144]{1,0:T(8,128)(2,1)}) %all-gather.10.cloned.1.call-update) | async-done | bytes 25165840 | tf_op jit(solution)/shard_map/all_gather | solution.py:105
  169.9 10.2 convolution_add_fusion
  192.1 36.6 all-gather.14.cloned.1.call-done
  235.7 41.6 %all-gather.12.cloned.1.call-done = bf16[1024,16,128]{0,2,1:T(8,128)(2,1)} async-done(((bf16[128,16,128]{0,2,1:T(8,128)(2,1)}), bf16[1024,16,128]{0,2,1:T(8,128)(2,1)}) %all-gather.12.cloned.1.call-update) | async-done | bytes 4194320 | tf_op jit(solution)/shard_map/all_gather | solution.py:157
  277.2 7.4 convolution_convert_fusion.4
  284.7 71.1 %all-gather.16.cloned.1.call-done = bf16[2048,2048]{1,0:T(8,128)(2,1)} async-done(((bf16[64,2048]{1,0:T(8,128)(2,1)}), bf16[2048,2048]{1,0:T(8,128)(2,1)}) %all-gather.16.cloned.1.call-update) | async-done | bytes 8388624 | tf_op jit(solution)/shard_map/all_gather | solution.py:107
  355.8 4.7 multiply_reduce_fusion.4
  364.4 4.8 all-to-all-start
  369.2 100.6 %all-gather.18.cloned.1.call-done = bf16[1,2048,2816]{2,1,0:T(8,128)(2,1)} async-done(((bf16[1,512,2816]{2,1,0:T(8,128)(2,1)}), bf16[1,2048,2816]{2,1,0:T(8,128)(2,1)}) %all-gather.18.cloned.1.call-update) | async-done | bytes 11534352 | tf_op jit(solution)/shard_map/all_gather | solution.py:126
  469.9 17.2 fusion.6
  494.1 43.3 %all-gather.20.cloned.1.call-done = bf16[1,1408,2048]{2,1,0:T(8,128)(2,1)} async-done(((bf16[1,352,2048]{2,1,0:T(8,128)(2,1)}), bf16[1,1408,2048]{2,1,0:T(8,128)(2,1)}) %all-gather.20.cloned.1.call-update) | async-done | bytes 5767184 | tf_op jit(solution)/shard_map/all_gather | solution.py:127
  537.4 10.8 fusion.21
  553.0 206.0 %all-gather = bf16[32,64,8]{1,2,0:T(8,128)(2,1)S(1)} all-gather(bf16[1,64,8]{1,2,0:T(8,128)(2,1)S(1)} %bitcast.198), channel_id=1, replica_groups=mesh['dp'=4,'expert'=8] {'dp','expert'}, dimensions={0}, use_global_device_ids=true | all-gather | bytes 33792 | tf_op jit(solution)/shard_map/all_gather | solution.py:109
  759.5 6.4 fusion.61
  766.6 7.2 convolution_convert_fusion
  773.9 184.5 %all_to_all.20 = bf16[8,128,2048]{2,1,0:T(8,128)(2,1)S(1)} all-to-all(bf16[8,128,2048]{2,1,0:T(8,128)(2,1)S(1)} %bitcast.184), channel_id=1, replica_groups=mesh['dp'=4,'expert'=8] {'expert'}, dimensions={0} | all-to-all | bytes 8388608 | tf_op jit(solution)/shard_map/all_to_all | solution.py:288
  958.4 14.2 fusion.30
  972.6 18.5 fusion.24
  996.5 176.8 %all-to-all-done.3 = bf16[8,128,2048]{2,1,0:T(8,128)(2,1)} async-done(((bf16[8,128,2048]{2,1,0:T(8,128)(2,1)}), bf16[8,128,2048]{2,1,0:T(8,128)(2,1)}, u32[]{:S(2)}, u32[]{:S(2)}) %all-to-all-start.3) | async-done | bytes 4194336 | tf_op jit(solution)/shard_map/all_to_all | solution.py:308
  1173.3 5.0 fusion.100
  1178.3 20.7 fusion.99
  1199.0 14.7 multiply_convert_fusion.4
  1213.7 12.2 multiply_reduce_fusion.3
  1226.5 21.6 fusion.37
  1251.1 6.3 convolution_convert_fusion.3
  1257.7 8.0 multiply_reduce_fusion
  1274.0 8.1 convolution_convert_fusion.2
  1282.1 6.5 copy.196
  1290.2 10.5 fusion.5
  1300.7 18.3 fusion.4
  1320.1 8.1 fusion.64
  1329.2 5.2 broadcast_multiply_fusion
  1337.9 37.0 reduce-scatter.28.cloned.1.call-done
  1376.2 20.7 fusion.68
  1398.0 19.3 fusion.90
  1417.6 33.6 fusion.36
  1451.2 58.9 %reduce-scatter.30.cloned.1.call-done = f32[64,8]{1,0:T(8,128)} async-done(((f32[2048,8]{1,0:T(8,128)}), f32[64,8]{1,0:T(8,128)}) %reduce-scatter.30.cloned.1.call-update) | async-done | bytes 2064
  1511.7 5.4 fusion.35
  1517.2 58.9 %reduce-scatter.26.cloned.1.call-done = bf16[1,352,2048]{2,1,0:T(8,128)(2,1)} async-done(((bf16[1,1408,2048]{2,1,0:T(8,128)(2,1)}), bf16[1,352,2048]{2,1,0:T(8,128)(2,1)}) %reduce-scatter.26.cloned.1.call-update) | async-done | bytes 1441808 | tf_op jit(solution)/shard_map/reduce_scatter | solution.py:315
  1579.8 20.6 fusion.55
  1600.5 40.4 %all-reduce.8 = (f32[2048]{0:T(1024)S(1)}, f32[6144]{0:T(1024)S(1)}, f32[2048]{0:T(1024)S(1)}, f32[2048]{0:T(1024)S(1)}) all-reduce(f32[2048]{0:T(1024)S(1)} %get-tuple-element.15, f32[6144]{0:T(1024)S(1)} %convert_reduce_fusion, f32[2048]{0:T(1024)S(1)} %copy-done.37, ...), channel_id=4, replica_groups=mesh['dp'=4,'expert'=8] {'dp','expert'}, use_global_device_ids=true, to_apply=%region_25.26.clone | all-reduce | flops 12288 | bytes 98304
  1645.6 47.3 %reduce-scatter.24.cloned.1.call-done = bf16[1,512,2816]{2,1,0:T(8,128)(2,1)} async-done(((bf16[1,2048,2816]{2,1,0:T(8,128)(2,1)}), bf16[1,512,2816]{2,1,0:T(8,128)(2,1)}) %reduce-scatter.24.cloned.1.call-update) | async-done | bytes 2883600 | tf_op jit(solution)/shard_map/reduce_scatter | solution.py:312
  1693.0 4.8 convert_element_type.212
  1697.7 184.7 %reduce-scatter.18.cloned.1.call-done = f32[64,2048]{1,0:T(8,128)} async-done(((f32[2048,2048]{1,0:T(8,128)}), f32[64,2048]{1,0:T(8,128)}) %reduce-scatter.18.cloned.1.call-update) | async-done | bytes 524304 | tf_op jit(solution)/shard_map/reduce_scatter | solution.py:397
  1882.5 437.3 %reduce-scatter.16.cloned.1.call-done = f32[64,6144]{1,0:T(8,128)} async-done(((f32[2048,6144]{1,0:T(8,128)}), f32[64,6144]{1,0:T(8,128)}) %reduce-scatter.16.cloned.1.call-update) | async-done | bytes 1572880 | tf_op jit(solution)/shard_map/reduce_scatter | solution.py:395
  2319.8 493.8 %reduce-scatter.22.cloned.1.call-done = f32[176,2048]{1,0:T(8,128)} async-done(((f32[5632,2048]{1,0:T(8,128)}), f32[176,2048]{1,0:T(8,128)}) %reduce-scatter.22.cloned.1.call-update) | async-done | bytes 1441808 | tf_op jit(solution)/shard_map/reduce_scatter | solution.py:339
  2813.5 970.3 %reduce-scatter.20.cloned.1.call-done = f32[64,11264]{1,0:T(8,128)} async-done(((f32[2048,11264]{1,0:T(8,128)}), f32[64,11264]{1,0:T(8,128)}) %reduce-scatter.20.cloned.1.call-update) | async-done | bytes 2883600 | tf_op jit(solution)/shard_map/reduce_scatter | solution.py:338
  (236 shorter events, 80.6 us)
Async XLA Ops:
  7.2 162.7 %all-gather.10.cloned.1.call-start = ((), (), s32[]{:S(2)}) async-start(), calls=%async_computation.13 | async-start | bytes 25952256 | tf_op jit(solution)/shard_map/all_gather | solution.py:105
  7.9 220.8 %all-gather.14.cloned.1.call-start = ((), (), s32[]{:S(2)}) async-start(), calls=%async_computation.15 | async-start | bytes 4718592 | tf_op jit(solution)/shard_map/all_gather | solution.py:156
  55.6 124.6 %copy-start.29 = (f32[2048]{0:T(1024)}, f32[2048]{0:T(1024)S(1)}, u32[]{:S(2)}) copy-start(f32[2048]{0:T(1024)S(1)} %convert_element_type.170) | copy-start | bytes 24580
  57.6 123.8 %copy-start.25 = (f32[128,128]{1,0:T(8,128)}, f32[128,128]{1,0:T(8,128)S(1)}, u32[]{:S(2)}) copy-start(f32[128,128]{1,0:T(8,128)S(1)} %get-tuple-element.51) | copy-start | bytes 196612
  57.6 123.8 %copy-start.27 = (f32[128,128]{1,0:T(8,128)}, f32[128,128]{1,0:T(8,128)S(1)}, u32[]{:S(2)}) copy-start(f32[128,128]{1,0:T(8,128)S(1)} %get-tuple-element.50) | copy-start | bytes 196612
  58.9 121.3 %copy-start.38 = (f32[128]{0:T(128)}, f32[128]{0:T(128)S(1)}, u32[]{:S(2)}) copy-start(f32[128]{0:T(128)S(1)} %add_rsqrt_fusion.1) | copy-start | bytes 1540
  183.0 94.2 %all-gather.12.cloned.1.call-start = ((), (), s32[]{:S(2)}) async-start(), calls=%async_computation.14 | async-start | bytes 4718592 | tf_op jit(solution)/shard_map/all_gather | solution.py:157
  186.0 42.7 %copy-start.19 = (bf16[128,16,128]{2,0,1:T(8,128)(2,1)S(1)}, bf16[128,16,128]{2,0,1:T(8,128)(2,1)}, u32[]{:S(2)}) copy-start(bf16[128,16,128]{2,0,1:T(8,128)(2,1)} %get-tuple-element.47) | copy-start | bytes 1572868
  186.0 169.7 %all-gather.16.cloned.1.call-start = ((), (), s32[]{:S(2)}) async-start(), calls=%async_computation.16 | async-start | bytes 8650752 | tf_op jit(solution)/shard_map/all_gather | solution.py:107
  186.6 283.2 %all-gather.18.cloned.1.call-start = ((), (), s32[]{:S(2)}) async-start(), calls=%async_computation.17 | async-start | bytes 14417920 | tf_op jit(solution)/shard_map/all_gather | solution.py:126
  187.2 350.2 %all-gather.20.cloned.1.call-start = ((), (), s32[]{:S(2)}) async-start(), calls=%async_computation.18 | async-start | bytes 7208960 | tf_op jit(solution)/shard_map/all_gather | solution.py:127
  187.8 990.5 %all-gather.22.cloned.1.call-start = ((), (), s32[]{:S(2)}) async-start(), calls=%async_computation.19 | async-start | bytes 47579136 | tf_op jit(solution)/shard_map/all_gather | solution.py:111
  188.5 1010.4 %all-gather.24.cloned.1.call-start = ((), (), s32[]{:S(2)}) async-start(), calls=%async_computation.20 | async-start | bytes 23789568 | tf_op jit(solution)/shard_map/all_gather | solution.py:112
  189.7 170.8 %copy-start.33 = (f32[2048]{0:T(1024)}, f32[2048]{0:T(1024)S(1)}, u32[]{:S(2)}) copy-start(f32[2048]{0:T(1024)S(1)} %convert_element_type.183) | copy-start | bytes 24580
  192.1 85.2 %copy-start.12 = (pred[128,1024]{0,1:T(8,128)(4,1)}, pred[128,1024]{0,1:T(8,128)(4,1)S(1)}, u32[]{:S(2)}) copy-start(pred[128,1024]{0,1:T(8,128)(4,1)S(1)} %compare_and_fusion) | copy-start | bytes 393220
  235.7 49.0 %copy-start.35 = (f32[16,128]{1,0:T(8,128)}, f32[16,128]{1,0:T(8,128)S(1)}, u32[]{:S(2)}) copy-start(f32[16,128]{1,0:T(8,128)S(1)} %log_add_fusion) | copy-start | bytes 24580
  235.7 120.1 %copy-start.5 = (bf16[128,2048]{1,0:T(8,128)(2,1)S(1)}, bf16[128,2048]{1,0:T(8,128)(2,1)}, u32[]{:S(2)}) copy-start(bf16[128,2048]{1,0:T(8,128)(2,1)} %param.15) | copy-start | bytes 1572868
  284.7 75.8 %copy-start.21 = (bf16[16,128,128]{2,1,0:T(8,128)(2,1)}, bf16[16,128,128]{2,1,0:T(8,128)(2,1)S(1)}, u32[]{:S(2)}) copy-start(bf16[16,128,128]{2,1,0:T(8,128)(2,1)S(1)} %convolution_convert_fusion.4) | copy-start | bytes 1572868
  364.4 105.5 %all-to-all-start = ((bf16[8,128,2048]{2,1,0:T(8,128)(2,1)}), bf16[8,128,2048]{2,1,0:T(8,128)(2,1)}, u32[]{:S(2)}, u32[]{:S(2)}) async-start(bf16[8,128,2048]{2,1,0:T(8,128)(2,1)} %bitcast.183), calls=%async_computation | async-start | bytes 8388608 | tf_op jit(solution)/shard_map/all_to_all | solution.py:212
  548.2 211.2 %copy-start.7 = (bf16[128,2048]{1,0:T(8,128)(2,1)S(1)}, bf16[128,2048]{1,0:T(8,128)(2,1)}, u32[]{:S(2)}) copy-start(bf16[128,2048]{1,0:T(8,128)(2,1)} %param.16) | copy-start | bytes 1572868
  548.2 211.2 %all-to-all-start.1 = ((bf16[8,128,2048]{2,1,0:T(8,128)(2,1)}), bf16[8,128,2048]{2,1,0:T(8,128)(2,1)}, u32[]{:S(2)}, u32[]{:S(2)}) async-start(bf16[8,128,2048]{2,1,0:T(8,128)(2,1)} %fusion.21), calls=%async_computation.1 | async-start | bytes 8388608 | tf_op jit(solution)/shard_map/all_to_all | solution.py:224
  766.6 191.8 %copy-start.11 = (f32[128,1024]{1,0:T(8,128)}, f32[128,1024]{1,0:T(8,128)S(1)}, u32[]{:S(2)}) copy-start(f32[128,1024]{1,0:T(8,128)S(1)} %select_reduce_fusion.1) | copy-start | bytes 1572868
  766.6 191.8 %slice-start.2 = ((s8[5767168]{0:T(1024)(128)(4,1)}), s8[4194304]{0:T(1024)(128)(4,1)S(1)}, s32[]{:S(2)}) async-start(s8[5767168]{0:T(1024)(128)(4,1)} %bitcast.199), calls=%async_computation.32 | async-start | bytes 8388608
  773.9 184.6 %slice-start.3 = ((s8[5767168]{0:T(1024)(128)(4,1)}), s8[1572864]{0:T(1024)(128)(4,1)S(1)}, s32[]{:S(2)}) async-start(s8[5767168]{0:T(1024)(128)(4,1)} %bitcast.199), calls=%async_computation.33 | async-start | bytes 3145728
  991.1 182.3 %all-to-all-start.3 = ((bf16[8,128,2048]{2,1,0:T(8,128)(2,1)}), bf16[8,128,2048]{2,1,0:T(8,128)(2,1)}, u32[]{:S(2)}, u32[]{:S(2)}) async-start(bf16[8,128,2048]{2,1,0:T(8,128)(2,1)} %fusion.24), calls=%async_computation.3 | async-start | bytes 8388608 | tf_op jit(solution)/shard_map/all_to_all | solution.py:308
  995.6 339.9 %reduce-scatter.14.cloned.1.call-start = ((), (), s32[]{:S(2)}) async-start(), calls=%async_computation.21 | async-start | bytes 4718592 | tf_op jit(solution)/shard_map/reduce_scatter | solution.py:369
  1226.5 21.7 copy-start.3
  1226.5 21.7 copy-start.34
  1226.5 21.7 copy-start.42
  1273.7 101.2 %reduce-scatter.28.cloned.1.call-start = ((), (), s32[]{:S(2)}) async-start(), calls=%async_computation.28 | async-start | bytes 4718592
  1288.7 221.4 %reduce-scatter.30.cloned.1.call-start = ((), (), s32[]{:S(2)}) async-start(), calls=%async_computation.29 | async-start | bytes 1081344
  1290.1 285.9 %reduce-scatter.26.cloned.1.call-start = ((), (), s32[]{:S(2)}) async-start(), calls=%async_computation.27 | async-start | bytes 7208960 | tf_op jit(solution)/shard_map/reduce_scatter | solution.py:315
  1300.7 392.3 %reduce-scatter.24.cloned.1.call-start = ((), (), s32[]{:S(2)}) async-start(), calls=%async_computation.26 | async-start | bytes 14417920 | tf_op jit(solution)/shard_map/reduce_scatter | solution.py:312
  1319.1 563.4 %reduce-scatter.18.cloned.1.call-start = ((), (), s32[]{:S(2)}) async-start(), calls=%async_computation.23 | async-start | bytes 17301504 | tf_op jit(solution)/shard_map/reduce_scatter | solution.py:397
  1328.2 991.6 %reduce-scatter.16.cloned.1.call-start = ((), (), s32[]{:S(2)}) async-start(), calls=%async_computation.22 | async-start | bytes 51904512 | tf_op jit(solution)/shard_map/reduce_scatter | solution.py:395
  1336.7 39.5 %copy-start.6 = (bf16[128,2048]{1,0:T(8,128)(2,1)S(1)}, bf16[128,2048]{1,0:T(8,128)(2,1)}, u32[]{:S(2)}) copy-start(bf16[128,2048]{1,0:T(8,128)(2,1)} %param.15) | copy-start | bytes 1572868
  1336.7 39.5 %copy-start.30 = (f32[2048]{0:T(1024)S(1)}, f32[2048]{0:T(1024)}, u32[]{:S(2)}) copy-start(f32[2048]{0:T(1024)} %copy-done.29) | copy-start | bytes 24580
  1336.8 39.5 %copy-start.39 = (f32[128]{0:T(128)S(1)}, f32[128]{0:T(128)}, u32[]{:S(2)}) copy-start(f32[128]{0:T(128)} %copy-done.38) | copy-start | bytes 1540
  1337.8 59.1 %copy-start.14 = (bf16[128,16,128]{0,2,1:T(8,128)(2,1)}, bf16[128,16,128]{0,2,1:T(8,128)(2,1)S(1)}, u32[]{:S(2)}) copy-start(bf16[128,16,128]{0,2,1:T(8,128)(2,1)S(1)} %copy.174) | copy-start | bytes 1572868
  1376.2 20.8 copy-start.16
  1397.0 1416.5 %reduce-scatter.22.cloned.1.call-start = ((), (), s32[]{:S(2)}) async-start(), calls=%async_computation.25 | async-start | bytes 47579136 | tf_op jit(solution)/shard_map/reduce_scatter | solution.py:339
  1417.3 2366.4 %reduce-scatter.20.cloned.1.call-start = ((), (), s32[]{:S(2)}) async-start(), calls=%async_computation.24 | async-start | bytes 95158272 | tf_op jit(solution)/shard_map/reduce_scatter | solution.py:338
  1451.2 60.4 %copy-start.45 = (f32[128]{0:T(128)S(1)}, f32[128]{0:T(128)}, u32[]{:S(2)}) copy-start(f32[128]{0:T(128)} %copy-done.44) | copy-start | bytes 1540
  1451.2 60.5 %copy-start.4 = (f32[128,2048]{1,0:T(8,128)S(1)}, f32[128,2048]{1,0:T(8,128)}, u32[]{:S(2)}) copy-start(f32[128,2048]{1,0:T(8,128)} %copy-done.2) | copy-start | bytes 3145732
  1511.7 67.6 %copy-start.15 = (bf16[128,16,128]{0,2,1:T(8,128)(2,1)S(1)}, bf16[128,16,128]{0,2,1:T(8,128)(2,1)}, u32[]{:S(2)}) copy-start(bf16[128,16,128]{0,2,1:T(8,128)(2,1)} %copy-done.14) | copy-start | bytes 1572868
  1517.2 62.2 %copy-start.17 = (bf16[128,2048]{0,1:T(8,128)(2,1)S(1)}, bf16[128,2048]{0,1:T(8,128)(2,1)}, u32[]{:S(2)}) copy-start(bf16[128,2048]{0,1:T(8,128)(2,1)} %copy-done.16) | copy-start | bytes 1572868
  1517.2 62.2 %copy-start.18 = (bf16[128,16,128]{0,2,1:T(8,128)(2,1)S(1)}, bf16[128,16,128]{0,2,1:T(8,128)(2,1)}, u32[]{:S(2)}) copy-start(bf16[128,16,128]{0,2,1:T(8,128)(2,1)} %fusion.60) | copy-start | bytes 1572868
  1579.8 20.7 copy-start.37
  (22 other events, 97.6 us)
Sparse Core Ops, SparseCore 0:
  11.0 158.8 all-gather.9
  183.2 45.4 all-gather.13
  230.9 46.3 all-gather.11
  280.1 75.6 all-gather.15
  357.4 112.3 all-gather.17
  471.6 65.7 all-gather.19
  540.2 422.8 all-gather.21
  966.0 219.3 all-gather.23
  1273.9 50.6 reduce-scatter.13
  1326.7 48.1 reduce-scatter.27
  1377.1 132.9 reduce-scatter.29
  1513.8 62.1 reduce-scatter.25
  1579.4 113.4 reduce-scatter.23
  1695.8 186.6 reduce-scatter.17
  1890.5 429.2 reduce-scatter.15
  2322.6 490.8 reduce-scatter.21
  2816.4 967.3 reduce-scatter.19
where the time goes:
time: 3800 us; the launch traced here: 3790 us
  waiting for transfers between devices  2870 us (76%)
  blocking collectives  474 us (12%)
  matrix products  350 us (9%)
    reduce_scatter x1, waiting for transfers between devices, per_device(): lax.psum_scatter(term_shared_in, ('dp', 'expert'), scatter_dimension=0, t...  970 us
    reduce_scatter x1, waiting for transfers between devices, per_device(): lax.psum_scatter(term_shared_out, ('dp', 'expert'), scatter_dimension=0,...  494 us
    reduce_scatter x1, waiting for transfers between devices, per_device(): lax.psum_scatter(term_qkv, ('dp', 'expert'), scatter_dimension=0, tiled=T...  437 us
    all_gather x1, blocking collectives, per_device(): lax.all_gather(router_weight, ('dp', 'expert'), axis=0, tiled=True)  206 us
    reduce_scatter x1, waiting for transfers between devices, per_device(): lax.psum_scatter(term_out_weight, ('dp', 'expert'), scatter_dimension=0,...  185 us
    all_to_all x1, blocking collectives, per_device(): lax.all_to_all(grad_result, 'expert', split_axis=0, concat_axis=0, tiled=...  185 us
    all_to_all x1, waiting for transfers between devices, per_device(): lax.all_to_all(grad_sent.astype(jnp.bfloat16), 'expert', split_axis=0, co...  177 us
    all_gather x1, waiting for transfers between devices, per_device(): lax.all_gather(qkv_weight, ('dp', 'expert'), axis=0, tiled=True)  111 us
  transfers between devices with their start and end apart: 20, of which 15 were waited for; matrix products, arithmetic and copies ran while one was open for 8% of the time, Pallas kernels for 0%

commit v1 on v0

--- a/solution.py
+++ b/solution.py
@@ -413,9 +413,374 @@
     )
 
 
+def bf16(values):
+    return values.astype(jnp.bfloat16)
+
+
+def two_parts(values):
+    high = lax.reduce_precision(values, exponent_bits=8, mantissa_bits=7)
+    return (bf16(high), bf16(values - high))
+
+
+def mm(left, right):
+    return jnp.dot(left, right, preferred_element_type=jnp.float32)
+
+
+def mm_nt(left, right):
+    return lax.dot_general(
+        left, right, (((1,), (1,)), ((), ())), preferred_element_type=jnp.float32
+    )
+
+
+def mm_tn(left, right):
+    return lax.dot_general(
+        left, right, (((0,), (0,)), ((), ())), preferred_element_type=jnp.float32
+    )
+
+
+def group_device(
+    hidden_in,
+    out_grad,
+    lengths,
+    routes,
+    norm1_gain,
+    qkv_weight,
+    qkv_bias,
+    out_weight,
+    norm2_gain,
+    router_weight,
+    shared_gate,
+    shared_in,
+    shared_out,
+    expert_in,
+    expert_out,
+):
+    size = lax.axis_size("expert")
+    parts = lax.axis_size("dp")
+    me = lax.axis_index("expert")
+    core = me % 2
+    rows, width = hidden_in.shape
+    group = rows * size
+    heads = width // HD
+    own_heads = heads // size
+    half = parts // 2
+    places = size // 2
+    block = width // (parts * size)
+    top = routes.shape[1]
+    experts = router_weight.shape[1]
+    score_scale = HD ** (-0.5)
+    bias_cols = 3 * width // (parts * size) // block
+    extra = 128
+    shared_block = shared_out.shape[0]
+    own_shared = parts * shared_block
+    own_qkv = 3 * own_heads * HD
+
+    def by_head(columns):
+        count = columns.shape[0]
+        cut = columns.reshape(count, 3, 2, half, places, HD)
+        return cut.transpose(4, 2, 0, 1, 3, 5).reshape(size, count, own_qkv)
+
+    def from_head(pieces):
+        count = pieces.shape[1]
+        cut = pieces.reshape(places, 2, count, 3, half, HD)
+        return cut.transpose(2, 3, 1, 4, 0, 5).reshape(count, 3 * width)
+
+    side = jnp.pad(bf16(routes), ((0, 0), (0, extra - top)))
+    gathered = lax.all_gather(
+        jnp.concatenate([hidden_in, side], axis=1), "expert", axis=0, tiled=True
+    )
+    hidden_all = gathered[:, :width].astype(jnp.float32)
+    routes_all = gathered[:, width : width + top].astype(jnp.int32)
+
+    small = jnp.concatenate(
+        [
+            norm1_gain[:, None],
+            norm2_gain[:, None],
+            shared_gate[:, None],
+            router_weight,
+            qkv_bias.reshape(block, bias_cols),
+        ],
+        axis=1,
+    )
+    small = jnp.pad(small, ((0, 0), (0, extra - small.shape[1])))
+    sent = jnp.concatenate(
+        [by_head(qkv_weight), jnp.broadcast_to(small[None], (size, block, extra))], axis=2
+    )
+    sent = lax.all_to_all(sent, "expert", split_axis=0, concat_axis=0, tiled=True)
+    qkv_full = lax.all_gather(
+        sent.reshape(size * block, own_qkv + extra), "dp", axis=0, tiled=True
+    )
+    weight_qkv = qkv_full[:, :own_qkv]
+    small = qkv_full[:, own_qkv:]
+    gain_one = small[:, 0].astype(jnp.float32)
+    gain_two = small[:, 1].astype(jnp.float32)
+    weight_router = small[:, 2 : 3 + experts]
+    bias_all = by_head(small[:, 3 + experts : 3 + experts + bias_cols].reshape(1, 3 * width))
+    bias_own = lax.dynamic_index_in_dim(bias_all, me, 0, keepdims=False).astype(jnp.float32)
+
+    swap = [(i, i ^ 1) for i in range(size)]
+
+    def own_half(values):
+        return lax.dynamic_slice_in_dim(values, core * half, half, 0)
+
+    def other_half(values):
+        return lax.dynamic_slice_in_dim(values, (1 - core) * half, half, 0)
+
+    out_blocks = lax.all_gather(out_weight[None], "dp", axis=0, tiled=True)
+    kept = own_half(out_blocks)
+    came = lax.ppermute(other_half(out_blocks), "expert", swap)
+    weight_out = jnp.stack(
+        [jnp.where(core == 0, kept, came), jnp.where(core == 0, came, kept)], axis=1
+    ).reshape(own_heads * HD, width)
+
+    cut = shared_in.reshape(block, 2, parts, size, shared_block)
+    cut = cut.transpose(3, 0, 1, 2, 4).reshape(size, block, 2 * own_shared)
+    cut = lax.all_to_all(cut, "expert", split_axis=0, concat_axis=0, tiled=True)
+
+    segment, position = segment_table(lengths[0], group)
+    valid_all = (segment < lengths.shape[1] - 1).astype(jnp.float32)[:, None]
+    cosine, sine = rotary_tables(position, HD)
+    allowed = (
+        (segment[:, None] == segment[None, :]) & (position[:, None] >= position[None, :])
+    )[None]
+    scale_first_all = rms_scale(hidden_all)
+    normed_one = bf16(hidden_all * scale_first_all * gain_one)
+    projected = mm(normed_one, weight_qkv) + bias_own
+    split = projected.reshape(group, 3, own_heads, HD)
+    query_low = bf16(rotate(split[:, 0], cosine, sine))
+    key_low = bf16(rotate(split[:, 1], cosine, sine))
+    value_low = bf16(split[:, 2])
+
+    def score_rows():
+        raw = (
+            jnp.einsum("qhd,khd->hqk", query_low, key_low, preferred_element_type=jnp.float32)
+            * score_scale
+        )
+        return jnp.where(allowed, raw, NEG_FILL)
+
+    scores = score_rows()
+    peak = jnp.max(scores, axis=-1, keepdims=True)
+    log_total = peak + jnp.log(jnp.sum(jnp.exp(scores - peak), axis=-1, keepdims=True))
+    weights_low = bf16(jnp.exp(scores - log_total))
+    attended = bf16(
+        jnp.einsum(
+            "hqk,khd->qhd", weights_low, value_low, preferred_element_type=jnp.float32
+        ).reshape(group, own_heads * HD)
+    )
+    branch = lax.psum_scatter(
+        bf16(mm(attended, weight_out)), "expert", scatter_dimension=0, tiled=True
+    )
+    inputs = hidden_in.astype(jnp.float32)
+    middle = inputs + branch.astype(jnp.float32)
+    scale_second = rms_scale(middle)
+    normed_two = bf16(middle * scale_second * gain_two)
+    normed_all = lax.all_gather(normed_two, "expert", axis=0, tiled=True)
+
+    weight_expert_in = lax.all_gather(expert_in, "dp", axis=1, tiled=True)[0]
+    weight_expert_out = lax.all_gather(expert_out, "dp", axis=1, tiled=True)[0]
+    weight_shared_in = lax.all_gather(
+        cut.reshape(size * block, 2 * own_shared), "dp", axis=0, tiled=True
+    )
+    weight_shared_out = lax.all_gather(shared_out, "dp", axis=0, tiled=True)
+    grad_all = lax.all_gather(out_grad, "expert", axis=0, tiled=True)
+
+    gate_logits = mm(normed_all, weight_router)
+    logits = gate_logits[:, 1:]
+    opener_all = jax.nn.sigmoid(gate_logits[:, :1])
+    peak_logit = jnp.max(logits, axis=-1, keepdims=True)
+    router_total = peak_logit + jnp.log(
+        jnp.sum(jnp.exp(logits - peak_logit), axis=-1, keepdims=True)
+    )
+    probs_all = jnp.exp(logits - router_total)
+    expert_ids = jnp.arange(experts, dtype=jnp.int32)
+    named = jnp.sum((routes_all == me).astype(jnp.float32), axis=1, keepdims=True)
+    own_prob = jnp.sum(
+        jnp.where(expert_ids[None, :] == me, probs_all, 0.0), axis=1, keepdims=True
+    )
+    gate_own = named * own_prob
+
+    expert_up = mm(normed_all, weight_expert_in)
+    expert_hidden = bf16(swiglu(expert_up))
+    expert_result = bf16(mm(expert_hidden, weight_expert_out)).astype(jnp.float32)
+    shared_up = mm(normed_all, weight_shared_in)
+    shared_hidden = bf16(swiglu(shared_up))
+    shared_rows = mm(shared_hidden, weight_shared_out)
+    grad_rows = grad_all.astype(jnp.float32) * valid_all
+    dot_expert = named * jnp.sum(grad_rows * expert_result, axis=1, keepdims=True)
+    dot_shared = jnp.sum(grad_rows * shared_rows, axis=1, keepdims=True)
+    mine = expert_ids[None, :] == me
+    expert_high, expert_low = two_parts(dot_expert)
+    shared_high, shared_low = two_parts(dot_shared)
+    zero = jnp.zeros((), jnp.bfloat16)
+    riders = jnp.concatenate(
+        [
+            jnp.where(mine, column, zero)
+            for column in (expert_high, expert_low, shared_high, shared_low)
+        ],
+        axis=1,
+    )
+    riders = jnp.pad(riders, ((0, 0), (0, extra - riders.shape[1])))
+    combined = jnp.concatenate(
+        [bf16(gate_own * expert_result + opener_all * shared_rows), riders], axis=1
+    )
+    summed = lax.psum_scatter(combined, "expert", scatter_dimension=0, tiled=True)
+
+    def rows_of(values):
+        return lax.dynamic_slice_in_dim(values, me * rows, rows, 0)
+
+    valid_rows = rows_of(valid_all)
+    output = bf16(valid_rows * (middle + summed[:, :width].astype(jnp.float32)))
+    tail = summed[:, width : width + 4 * experts].astype(jnp.float32)
+    grad_probs = tail[:, :experts] + tail[:, experts : 2 * experts]
+    dot_gate = jnp.sum(tail[:, 2 * experts :], axis=1, keepdims=True)
+
+    grad_shared_rows = bf16(grad_rows * opener_all)
+    grad_shared_up = bf16(swiglu_back(shared_up, mm_nt(grad_shared_rows, weight_shared_out)))
+    term_shared_out = mm_tn(shared_hidden, grad_shared_rows)
+    term_shared_in = mm_tn(normed_all, grad_shared_up)
+    grad_result = bf16(gate_own * grad_rows)
+    grad_expert_up = bf16(swiglu_back(expert_up, mm_nt(grad_result, weight_expert_out)))
+    term_expert_out = mm_tn(expert_hidden, grad_result)
+    term_expert_in = mm_tn(normed_all, grad_expert_up)
+    grad_normed_part = bf16(
+        mm_nt(grad_shared_up, weight_shared_in) + mm_nt(grad_expert_up, weight_expert_in)
+    )
+    grad_normed_two = lax.psum_scatter(
+        grad_normed_part, "expert", scatter_dimension=0, tiled=True
+    ).astype(jnp.float32)
+    grad_expert_in = lax.psum_scatter(
+        bf16(term_expert_in)[None], "dp", scatter_dimension=1, tiled=True
+    ).astype(jnp.float32)
+    grad_expert_out = lax.psum_scatter(
+        bf16(term_expert_out)[None], "dp", scatter_dimension=1, tiled=True
+    ).astype(jnp.float32)
+    grad_shared_out = lax.psum_scatter(
+        bf16(term_shared_out), "dp", scatter_dimension=0, tiled=True
+    ).astype(jnp.float32)
+    cut = lax.psum_scatter(bf16(term_shared_in), "dp", scatter_dimension=0, tiled=True)
+    cut = lax.all_to_all(
+        cut.reshape(size, block, 2 * own_shared), "expert", split_axis=0, concat_axis=0, tiled=True
+    )
+    grad_shared_in = (
+        cut.reshape(size, block, 2, parts, shared_block)
+        .transpose(1, 2, 3, 0, 4)
+        .reshape(block, 2 * parts * size * shared_block)
+        .astype(jnp.float32)
+    )
+
+    opener = rows_of(opener_all)
+    probs = rows_of(probs_all)
+    grad_gate_logit = dot_gate * opener * (1.0 - opener)
+    grad_logits = probs * (grad_probs - jnp.sum(probs * grad_probs, axis=-1, keepdims=True))
+    grad_heads = bf16(jnp.concatenate([grad_gate_logit, grad_logits], axis=1))
+    term_router = mm_tn(normed_two, grad_heads)
+    grad_normed_two = grad_normed_two + mm_nt(grad_heads, weight_router)
+    grad_middle_norm, term_norm_two = norm_back(middle, scale_second, gain_two, grad_normed_two)
+    grad_middle = rows_of(grad_rows) + grad_middle_norm
+    grad_branch = lax.all_gather(bf16(grad_middle), "expert", axis=0, tiled=True)
+
+    term_out = bf16(mm_tn(attended, grad_branch)).reshape(half, 2, block, width)
+    grad_attended = bf16(mm_nt(grad_branch, weight_out)).reshape(group, own_heads, HD)
+    weights_again = jnp.exp(score_rows() - log_total)
+    grad_weights = jnp.einsum(
+        "qhd,khd->hqk", grad_attended, value_low, preferred_element_type=jnp.float32
+    )
+    delta_rows = jnp.sum(weights_again * grad_weights, axis=-1, keepdims=True)
+    grad_scores = bf16(weights_again * (grad_weights - delta_rows))
+    grad_query_turned = (
+        jnp.einsum("hqk,khd->qhd", grad_scores, key_low, preferred_element_type=jnp.float32)
+        * score_scale
+    )
+    grad_key_turned = (
+        jnp.einsum("hqk,qhd->khd", grad_scores, query_low, preferred_element_type=jnp.float32)
+        * score_scale
+    )
+    grad_values = jnp.einsum(
+        "hqk,qhd->khd", bf16(weights_again), grad_attended, preferred_element_type=jnp.float32
+    )
+    grad_projected = bf16(
+        jnp.stack(
+            [
+                rotate_back(grad_query_turned, cosine, sine),
+                rotate_back(grad_key_turned, cosine, sine),
+                grad_values,
+            ],
+            axis=1,
+        ).reshape(group, own_qkv)
+    )
+    grad_normed_part = bf16(mm_nt(grad_projected, weight_qkv))
+    grad_normed_one = lax.psum_scatter(
+        grad_normed_part, "expert", scatter_dimension=0, tiled=True
+    ).astype(jnp.float32)
+    scale_first = rms_scale(inputs)
+    grad_input_norm, term_norm_one = norm_back(inputs, scale_first, gain_one, grad_normed_one)
+    input_grad = bf16(grad_middle + grad_input_norm)
+
+    kept = jnp.where(core == 0, term_out[:, 0], term_out[:, 1])
+    given = jnp.where(core == 0, term_out[:, 1], term_out[:, 0])
+    came = lax.ppermute(given, "expert", swap)
+    out_blocks = jnp.concatenate(
+        [jnp.where(core == 0, kept, came), jnp.where(core == 0, came, kept)], axis=0
+    )
+    grad_out_weight = lax.psum_scatter(
+        out_blocks, "dp", scatter_dimension=0, tiled=True
+    ).astype(jnp.float32)[0]
+
+    term_qkv = mm_tn(normed_one, grad_projected)
+    term_bias = jnp.sum(grad_projected.astype(jnp.float32), axis=0)
+    bias_slots = jnp.where(jnp.arange(size)[:, None] == me, term_bias[None, :], 0.0)
+    bias_rows = from_head(bias_slots[:, None, :]).reshape(width, bias_cols)
+    small_terms = jnp.concatenate(
+        [term_norm_one[:, None], term_norm_two[:, None], term_router, bias_rows], axis=1
+    )
+    count = small_terms.shape[1]
+    small_high, small_low = two_parts(small_terms)
+    small_terms = jnp.concatenate([small_high, small_low], axis=1)
+    small_terms = jnp.pad(small_terms, ((0, 0), (0, extra - 2 * count)))
+    back = lax.psum_scatter(
+        jnp.concatenate([bf16(term_qkv), small_terms], axis=1), "dp", scatter_dimension=0, tiled=True
+    )
+    back = lax.all_to_all(
+        back.reshape(size, block, own_qkv + extra), "expert", split_axis=0, concat_axis=0, tiled=True
+    ).astype(jnp.float32)
+    grad_qkv = from_head(back[:, :, :own_qkv])
+    small_sum = jnp.sum(back[:, :, own_qkv:], axis=0)
+    small_sum = small_sum[:, :count] + small_sum[:, count : 2 * count]
+    grad_norm1 = small_sum[:, 0]
+    grad_norm2 = small_sum[:, 1]
+    grad_shared_gate = small_sum[:, 2]
+    grad_router = small_sum[:, 3 : 3 + experts]
+    grad_bias = small_sum[:, 3 + experts :].reshape(block * bias_cols)
+    return (
+        output,
+        input_grad,
+        grad_norm1,
+        grad_qkv,
+        grad_bias,
+        grad_out_weight,
+        grad_norm2,
+        grad_router,
+        grad_shared_gate,
+        grad_shared_in,
+        grad_shared_out,
+        grad_expert_in,
+        grad_expert_out,
+    )
+
+
 def solution(mesh):
+    size, parts = mesh.shape["expert"], mesh.shape["dp"]
+
+    def device(*arrays):
+        block = arrays[5].shape[0]
+        whole_heads = 2 * block == HD and parts % 2 == 0 and size % 2 == 0
+        one_expert = arrays[13].shape[0] == 1
+        if whole_heads and one_expert and arrays[5].shape[1] % (3 * size * HD) == 0:
+            return group_device(*arrays)
+        return per_device(*arrays)
+
     return jax.shard_map(
-        per_device,
+        device,
         mesh=mesh,
         in_specs=(
             P(("dp", "expert"), None),

time: 3800 us -> 1310 us (0.34)
  waiting for transfers between devices: 2870 us -> 889 us
  blocking collectives: 474 us -> 63.9 us
  matrix products: 350 us -> 208 us
    reduce_scatter x7 -> x9, waiting for transfers between devices: 2190 us -> 426 us  [the longest x1 114 us: group_device(): lax.psum_scatter(bf16(term_expert_in)[None], 'dp', scatter_dimension=1, t...]
    all_gather x1 -> x0, blocking collectives: 206 us -> none  [per_device(): lax.all_gather(router_weight, ('dp', 'expert'), axis=0, tiled=True)]
    all_to_all x3, waiting for transfers between devices: 177 us -> 23 us  [the longest x1 23 us: group_device(): lax.all_to_all(sent, 'expert', split_axis=0, concat_axis=0, tiled=True)]
    dot_general x33 -> x27, matrix products: 349 us -> 208 us  [the longest x7 70 us: mm_nt(): lax.dot_general(left, right, (((1,), (1,)), ((), ())), preferred_element_...]
    all_to_all x1, blocking collectives: 185 us -> 63.9 us  [group_device(): cut = lax.all_to_all(cut, 'expert', split_axis=0, concat_axis=0, tiled=True)]
    unnamed x19 -> x21, waiting for transfers between devices: 99.2 us -> 11.9 us
    unnamed x2 -> x0, blocking collectives: 83.8 us -> none
    all_gather x8 -> x10, waiting for transfers between devices: 404 us -> 426 us  [the longest x1 99 us: group_device(): weight_expert_in = lax.all_gather(expert_in, 'dp', axis=1, tiled=True)[0]]
  transfers between devices with their start and end apart: 20 -> 25, of which waited for: 15 -> 21; matrix products, arithmetic and copies ran while one was open for 8% -> 16% of each run, Pallas kernels for 0% -> 0%
where the time goes in v1:
time: 1310 us
  waiting for transfers between devices  889 us (68%)
  matrix products  208 us (16%)
  blocking collectives  63.9 us (5%)
  local copies, waits for them, and re-layouts  62.8 us (5%)
  other arithmetic  51.2 us (4%)
  starting transfers between devices  17 us (1%)
  between operations  15.6 us (1%)
    reduce_scatter x1, waiting for transfers between devices, group_device(): lax.psum_scatter(bf16(term_expert_in)[None], 'dp', scatter_dimension=1, t...  114 us
    all_gather x1, waiting for transfers between devices, group_device(): weight_expert_in = lax.all_gather(expert_in, 'dp', axis=1, tiled=True)[0]  99 us
    reduce_scatter x2, waiting for transfers between devices, group_device(): lax.psum_scatter(grad_normed_part, 'expert', scatter_dimension=0, tiled=T...  76.6 us
    dot_general x7, matrix products, mm_nt(): lax.dot_general(left, right, (((1,), (1,)), ((), ())), preferred_element_...  70 us
    reduce_scatter x1, waiting for transfers between devices, group_device(): lax.psum_scatter(bf16(term_expert_out)[None], 'dp', scatter_dimension=1,...  66.3 us
    all_to_all x1, blocking collectives, group_device(): cut = lax.all_to_all(cut, 'expert', split_axis=0, concat_axis=0, tiled=True)  63.9 us
    dot_general x7, matrix products, mm(): return jnp.dot(left, right, preferred_element_type=jnp.float32)  63.1 us
    dot_general x7, matrix products, mm_tn(): lax.dot_general(left, right, (((0,), (0,)), ((), ())), preferred_element_...  59.6 us
  transfers between devices with their start and end apart: 25, of which 21 were waited for; matrix products, arithmetic and copies ran while one was open for 16% of the time, Pallas kernels for 0%

profile of v1, /device:TPU:0, one launch (start us, length us, event | category | flops | bytes accessed | tf_op | source)
XLA Modules:
  0.0 1307.3 jit_solution(3670700716677559977)
XLA Ops:
  12.2 6.5 all-to-all-start
  19.4 23.0 %all-to-all-done = bf16[8,64,896]{2,1,0:T(8,128)(2,1)S(1)} async-done(((bf16[8,64,896]{2,1,0:T(8,128)(2,1)}), bf16[8,64,896]{2,1,0:T(8,128)(2,1)S(1)}, u32[]{:S(2)}, u32[]{:S(2)}) %all-to-all-start) | async-done | bytes 917536 | tf_op jit(solution)/shard_map/all_to_all | solution.py:509
  45.6 3.8 all-gather.30.cloned.1.call-done
  57.2 42.9 %all-gather.14.cloned.1.call-done = bf16[2048,896]{0,1:T(8,128)(2,1)} async-done(((bf16[512,896]{0,1:T(8,128)(2,1)}), bf16[2048,896]{0,1:T(8,128)(2,1)}) %all-gather.14.cloned.1.call-update) | async-done | bytes 3670032 | tf_op jit(solution)/shard_map/all_gather | solution.py:510
  104.6 47.6 %all-gather.12.cloned.1.call-done = bf16[1024,2176]{0,1:T(8,128)(2,1)} async-done(((bf16[128,2176]{0,1:T(8,128)(2,1)}), bf16[1024,2176]{0,1:T(8,128)(2,1)}) %all-gather.12.cloned.1.call-update) | async-done | bytes 4456464 | tf_op jit(solution)/shard_map/all_gather | solution.py:489
  155.6 5.7 fusion.28
  175.7 48.3 %reduce-scatter.31.cloned.1.call-done = bf16[128,2048]{1,0:T(8,128)(2,1)} async-done(((bf16[1024,2048]{1,0:T(8,128)(2,1)}), bf16[128,2048]{1,0:T(8,128)(2,1)}) %reduce-scatter.31.cloned.1.call-update) | async-done | bytes 524304 | tf_op jit(solution)/shard_map/reduce_scatter | solution.py:570
  227.5 5.0 reshape.387
  238.2 63.9 %all_to_all.20 = bf16[8,64,1408]{2,1,0:T(8,128)(2,1)} all-to-all(bf16[8,64,1408]{2,1,0:T(8,128)(2,1)} %reshape.388), channel_id=1, replica_groups=mesh['dp'=4,'expert'=8] {'expert'}, dimensions={0} | all-to-all | bytes 2883584 | tf_op jit(solution)/shard_map/all_to_all | solution.py:538
  309.5 57.5 %all-gather.22.cloned.1.call-done = bf16[2048,1408]{1,0:T(8,128)(2,1)} async-done(((bf16[512,1408]{1,0:T(8,128)(2,1)}), bf16[2048,1408]{1,0:T(8,128)(2,1)}) %all-gather.22.cloned.1.call-update) | async-done | bytes 5767184 | tf_op jit(solution)/shard_map/all_gather | solution.py:581
  367.1 11.9 fusion.87
  379.0 31.8 %all-gather.24.cloned.1.call-done = bf16[704,2048]{1,0:T(8,128)(2,1)} async-done(((bf16[176,2048]{1,0:T(8,128)(2,1)}), bf16[704,2048]{1,0:T(8,128)(2,1)}) %all-gather.24.cloned.1.call-update) | async-done | bytes 2883600 | tf_op jit(solution)/shard_map/all_gather | solution.py:584
  410.8 48.8 %all-gather.26.cloned.1.call-done = bf16[1024,2048]{1,0:T(8,128)(2,1)} async-done(((bf16[128,2048]{1,0:T(8,128)(2,1)}), bf16[1024,2048]{1,0:T(8,128)(2,1)}) %all-gather.26.cloned.1.call-update) | async-done | bytes 4194320 | tf_op jit(solution)/shard_map/all_gather | solution.py:585
  459.6 9.8 multiply_convert_fusion.7
  469.4 5.6 fusion.88
  475.0 99.0 %all-gather.18.cloned.1.call-done = bf16[1,2048,2816]{2,1,0:T(8,128)(2,1)} async-done(((bf16[1,512,2816]{2,1,0:T(8,128)(2,1)}), bf16[1,2048,2816]{2,1,0:T(8,128)(2,1)}) %all-gather.18.cloned.1.call-update) | async-done | bytes 11534352 | tf_op jit(solution)/shard_map/all_gather | solution.py:579
  573.9 18.8 %fusion.2 = f32[1024,2816]{1,0:T(8,128)} fusion(bf16[1024,2048]{1,0:T(8,128)(2,1)} %all-gather.16.cloned.1.call-done, bf16[1,2048,2816]{2,1,0:T(8,128)(2,1)} %all-gather.18.cloned.1.call-done), kind=kOutput, calls=%fused_computation.2 | convolution fusion | flops 11811160064 | bytes 27262976 | tf_op jit(solution)/shard_map/dot_general | solution.py:426
  592.7 48.8 %all-gather.20.cloned.1.call-done = bf16[1,1408,2048]{2,1,0:T(8,128)(2,1)} async-done(((bf16[1,352,2048]{2,1,0:T(8,128)(2,1)}), bf16[1,1408,2048]{2,1,0:T(8,128)(2,1)}) %all-gather.20.cloned.1.call-update) | async-done | bytes 5767184 | tf_op jit(solution)/shard_map/all_gather | solution.py:580
  641.5 18.9 %multiply_convert_fusion.4 = (bf16[1024,1408]{1,0:T(8,128)(2,1)}, bf16[1024,1408]{1,0:T(8,128)(2,1)}, bf16[1024,1408]{1,0:T(8,128)(2,1)}) fusion(f32[1024,2816]{1,0:T(8,128)} %fusion.2, bf16[1,1408,2048]{2,1,0:T(8,128)(2,1)} %all-gather.20.cloned.1.call-done, bf16[1024,2048]{1,0:T(8,128)(2,1)} %all-gather.26.cloned.1.call-done, ...), kind=kOutput, calls=%fused_computation.37 | convolution fusion | flops 5937037312 | bytes 30154752 | tf_op jit(solution)/shard_map/dot_general | solution.py:430
  660.3 14.3 %fusion.10 = (f32[1024]{0:T(1024)S(1)}, f32[1024]{0:T(1024)S(1)}, bf16[1024,2048]{1,0:T(8,128)(2,1)}, f32[1024,2048]{1,0:T(8,128)}) fusion(bf16[1024,2048]{1,0:T(8,128)(2,1)} %all-gather.26.cloned.1.call-done, f32[1024]{0:T(1024)S(1)} %compare_convert_fusion, f32[1024,2048]{1,0:T(8,128)} %fusion.88, f32[1024]{0:T(1024)S(1)} %bitcast.207, ...), kind=kOutput, calls=%fused_computation.16 | convolution fusion | flops 5930743808 | bytes 33837056 | tf_op jit(solution)/shard_map/dot_general | solution.py:426
  674.9 3.9 fusion.17
  680.2 11.4 fusion.27
  691.6 19.4 %add_convert_fusion = bf16[1024,2048]{1,0:T(8,128)(2,1)} fusion(f32[1024,2048]{1,0:T(8,128)} %fusion.27, bf16[1,2048,2816]{2,1,0:T(8,128)(2,1)} %all-gather.18.cloned.1.call-done, bf16[1024,1408]{1,0:T(8,128)(2,1)} %get-tuple-element.95, bf16[1024,1408]{1,0:T(8,128)(2,1)} %get-tuple-element.94), kind=kOutput, calls=%fused_computation.19 | convolution fusion | flops 11826888704 | bytes 29884416 | tf_op jit(solution)/shard_map/dot_general | solution.py:430
  711.1 20.3 %reduce-scatter.33.cloned.1.call-done = bf16[128,2176]{1,0:T(8,128)(2,1)} async-done(((bf16[1024,2176]{1,0:T(8,128)(2,1)}), bf16[128,2176]{1,0:T(8,128)(2,1)}) %reduce-scatter.33.cloned.1.call-update) | async-done | bytes 557072 | tf_op jit(solution)/shard_map/reduce_scatter | solution.py:626
  732.4 49.4 %reduce-scatter.35.cloned.1.call-done = bf16[128,2048]{1,0:T(8,128)(2,1)} async-done(((bf16[1024,2048]{1,0:T(8,128)(2,1)}), bf16[128,2048]{1,0:T(8,128)(2,1)}) %reduce-scatter.35.cloned.1.call-update) | async-done | bytes 524304 | tf_op jit(solution)/shard_map/reduce_scatter | solution.py:648
  786.9 45.4 %all-gather.28.cloned.1.call-done = bf16[1024,2048]{1,0:T(8,128)(2,1)} async-done(((bf16[128,2048]{1,0:T(8,128)(2,1)}), bf16[1024,2048]{1,0:T(8,128)(2,1)}) %all-gather.28.cloned.1.call-update) | async-done | bytes 4194320 | tf_op jit(solution)/shard_map/all_gather | solution.py:680
  832.3 3.6 convolution_convert_fusion.8
  835.9 5.8 multiply_reduce_fusion
  852.8 5.1 convolution_convert_fusion.3
  858.0 11.6 convolution_convert_fusion.1
  872.2 7.5 convolution_convert_fusion.4
  879.6 27.2 %reduce-scatter.37.cloned.1.call-done = bf16[128,2048]{1,0:T(8,128)(2,1)} async-done(((bf16[1024,2048]{1,0:T(8,128)(2,1)}), bf16[128,2048]{1,0:T(8,128)(2,1)}) %reduce-scatter.37.cloned.1.call-update) | async-done | bytes 524304 | tf_op jit(solution)/shard_map/reduce_scatter | solution.py:712
  908.3 4.4 pad_maximum_fusion.3
  912.8 7.4 convolution_convert_fusion.5
  920.2 11.1 fusion.11
  939.1 18.4 %convert_bitcast_fusion = bf16[1,2048,2816]{2,1,0:T(8,128)(2,1)} fusion(bf16[1024,2048]{1,0:T(8,128)(2,1)} %all-gather.16.cloned.1.call-done, bf16[1024,1408]{1,0:T(8,128)(2,1)} %get-tuple-element.95, bf16[1024,1408]{1,0:T(8,128)(2,1)} %get-tuple-element.94), kind=kOutput, calls=%fused_computation.4 | convolution fusion | flops 11828461568 | bytes 21495808 | tf_op jit(solution)/shard_map/dot_general | solution.py:436
  957.5 16.7 %reduce-scatter.23.cloned.1.call-done = bf16[512,1408]{1,0:T(8,128)(2,1)} async-done(((bf16[2048,1408]{1,0:T(8,128)(2,1)}), bf16[512,1408]{1,0:T(8,128)(2,1)}) %reduce-scatter.23.cloned.1.call-update) | async-done | bytes 1441808 | tf_op jit(solution)/shard_map/reduce_scatter | solution.py:660
  974.2 4.6 all-to-all-start.3
  978.8 46.6 %reduce-scatter.21.cloned.1.call-done = bf16[512,896]{0,1:T(8,128)(2,1)} async-done(((bf16[2048,896]{0,1:T(8,128)(2,1)}), bf16[512,896]{0,1:T(8,128)(2,1)}) %reduce-scatter.21.cloned.1.call-update) | async-done | bytes 917520 | tf_op jit(solution)/shard_map/reduce_scatter | solution.py:740
  1027.6 4.8 all-to-all-start.2
  1032.5 37.6 %reduce-scatter.25.cloned.1.call-done = bf16[176,2048]{1,0:T(8,128)(2,1)} async-done(((bf16[704,2048]{1,0:T(8,128)(2,1)}), bf16[176,2048]{1,0:T(8,128)(2,1)}) %reduce-scatter.25.cloned.1.call-update) | async-done | bytes 720912 | tf_op jit(solution)/shard_map/reduce_scatter | solution.py:657
  1072.5 66.3 %reduce-scatter.29.cloned.1.call-done = bf16[1,352,2048]{2,1,0:T(8,128)(2,1)} async-done(((bf16[1,1408,2048]{2,1,0:T(8,128)(2,1)}), bf16[1,352,2048]{2,1,0:T(8,128)(2,1)}) %reduce-scatter.29.cloned.1.call-update) | async-done | bytes 1441808 | tf_op jit(solution)/shard_map/reduce_scatter | solution.py:654
  1142.1 7.5 reshape.402
  1149.6 6.6 copy.268
  1156.1 5.5 reshape.401
  1161.6 8.4 reduce-scatter.39.cloned.1.call-done
  1171.8 113.6 %reduce-scatter.27.cloned.1.call-done = bf16[1,512,2816]{2,1,0:T(8,128)(2,1)} async-done(((bf16[1,2048,2816]{2,1,0:T(8,128)(2,1)}), bf16[1,512,2816]{2,1,0:T(8,128)(2,1)}) %reduce-scatter.27.cloned.1.call-update) | async-done | bytes 2883600 | tf_op jit(solution)/shard_map/reduce_scatter | solution.py:651
  1285.4 4.8 convert_element_type.324
  (260 shorter events, 105.1 us)
Async XLA Ops:
  10.2 33.6 %copy-start.3 = (bf16[128,2048]{1,0:T(8,128)(2,1)S(1)}, bf16[128,2048]{1,0:T(8,128)(2,1)}, u32[]{:S(2)}) copy-start(bf16[128,2048]{1,0:T(8,128)(2,1)} %param.15) | copy-start | bytes 1572868
  10.6 33.5 %copy-start.34 = (s32[128,4]{0,1:T(4,128)S(1)}, s32[128,4]{0,1:T(4,128)}, u32[]{:S(2)}) copy-start(s32[128,4]{0,1:T(4,128)} %param.18) | copy-start | bytes 6148
  12.2 33.0 %copy-start.43 = (s32[1,5]{1,0:T(1,128)S(1)}, s32[1,5]{1,0:T(1,128)}, u32[]{:S(2)}) copy-start(s32[1,5]{1,0:T(1,128)} %param.17) | copy-start | bytes 64
  12.2 30.2 %all-to-all-start = ((bf16[8,64,896]{2,1,0:T(8,128)(2,1)}), bf16[8,64,896]{2,1,0:T(8,128)(2,1)S(1)}, u32[]{:S(2)}, u32[]{:S(2)}) async-start(bf16[8,64,896]{2,1,0:T(8,128)(2,1)} %pad_maximum_fusion.9), calls=%async_computation | async-start | bytes 1835008 | tf_op jit(solution)/shard_map/all_to_all | solution.py:509
  18.7 30.8 %all-gather.30.cloned.1.call-start = ((), (), s32[]{:S(2)}) async-start(), calls=%async_computation.28 | async-start | bytes 1310720 | tf_op jit(solution)/shard_map/all_gather | solution.py:529
  19.4 80.7 %all-gather.14.cloned.1.call-start = ((), (), s32[]{:S(2)}) async-start(), calls=%async_computation.15 | async-start | bytes 4587520 | tf_op jit(solution)/shard_map/all_gather | solution.py:510
  43.7 108.5 %all-gather.12.cloned.1.call-start = ((), (), s32[]{:S(2)}) async-start(), calls=%async_computation.14 | async-start | bytes 5013504 | tf_op jit(solution)/shard_map/all_gather | solution.py:489
  45.0 179.0 %reduce-scatter.31.cloned.1.call-start = ((), (), s32[]{:S(2)}) async-start(), calls=%async_computation.29 | async-start | bytes 4718592 | tf_op jit(solution)/shard_map/reduce_scatter | solution.py:570
  49.5 6.1 copy-start.22
  51.4 4.1 collective-permute-start
  55.5 112.2 %copy-start.1 = (pred[1024,1024]{0,1:T(8,128)(4,1)}, pred[1024,1024]{0,1:T(8,128)(4,1)S(1)}, u32[]{:S(2)}) copy-start(pred[1024,1024]{0,1:T(8,128)(4,1)S(1)} %compare_and_fusion) | copy-start | bytes 3145732
  57.2 114.3 %copy-start.10 = (bf16[2,2,64,2048]{3,2,1,0:T(8,128)(2,1)}, bf16[2,2,64,2048]{3,2,1,0:T(8,128)(2,1)S(1)}, u32[]{:S(2)}) copy-start(bf16[2,2,64,2048]{3,2,1,0:T(8,128)(2,1)S(1)} %pad_maximum_fusion.7) | copy-start | bytes 3145732
  104.6 56.7 %copy-start.25 = (f32[2048,1]{0,1:T(1,128)}, f32[2048,1]{0,1:T(1,128)S(1)}, u32[]{:S(2)}) copy-start(f32[2048,1]{0,1:T(1,128)S(1)} %get-tuple-element.105) | copy-start | bytes 24580
  104.6 120.7 %copy-start.27 = (f32[2048,1]{0,1:T(1,128)}, f32[2048,1]{0,1:T(1,128)S(1)}, u32[]{:S(2)}) copy-start(f32[2048,1]{0,1:T(1,128)S(1)} %get-tuple-element.104) | copy-start | bytes 24580
  161.3 6.4 copy-start.5
  175.6 51.8 %copy-start.19 = (bf16[64,11264]{1,0:T(8,128)(2,1)S(1)}, bf16[64,11264]{1,0:T(8,128)(2,1)}, u32[]{:S(2)}) copy-start(bf16[64,11264]{1,0:T(8,128)(2,1)} %param.26) | copy-start | bytes 4325380
  175.6 130.2 %all-gather.16.cloned.1.call-start = ((), (), s32[]{:S(2)}) async-start(), calls=%async_computation.16 | async-start | bytes 4718592 | tf_op jit(solution)/shard_map/all_gather | solution.py:577
  225.3 9.7 copy-start.35
  227.4 139.7 %all-gather.22.cloned.1.call-start = ((), (), s32[]{:S(2)}) async-start(), calls=%async_computation.19 | async-start | bytes 7208960 | tf_op jit(solution)/shard_map/all_gather | solution.py:581
  302.1 108.6 %all-gather.24.cloned.1.call-start = ((), (), s32[]{:S(2)}) async-start(), calls=%async_computation.20 | async-start | bytes 3604480 | tf_op jit(solution)/shard_map/all_gather | solution.py:584
  302.9 156.7 %all-gather.26.cloned.1.call-start = ((), (), s32[]{:S(2)}) async-start(), calls=%async_computation.21 | async-start | bytes 4718592 | tf_op jit(solution)/shard_map/all_gather | solution.py:585
  303.6 270.3 %all-gather.18.cloned.1.call-start = ((), (), s32[]{:S(2)}) async-start(), calls=%async_computation.17 | async-start | bytes 14417920 | tf_op jit(solution)/shard_map/all_gather | solution.py:579
  304.4 337.1 %all-gather.20.cloned.1.call-start = ((), (), s32[]{:S(2)}) async-start(), calls=%async_computation.18 | async-start | bytes 7208960 | tf_op jit(solution)/shard_map/all_gather | solution.py:580
  305.0 426.4 %reduce-scatter.33.cloned.1.call-start = ((), (), s32[]{:S(2)}) async-start(), calls=%async_computation.30 | async-start | bytes 5013504 | tf_op jit(solution)/shard_map/reduce_scatter | solution.py:626
  459.6 9.8 copy-start.42
  641.5 18.9 %copy-start.41 = (bf16[1,1408,2048]{2,1,0:T(8,128)(2,1)S(1)}, bf16[1,1408,2048]{2,1,0:T(8,128)(2,1)}, u32[]{:S(2)}) copy-start(bf16[1,1408,2048]{2,1,0:T(8,128)(2,1)} %all-gather.20.cloned.1.call-done) | copy-start | bytes 17301508
  678.8 103.0 %reduce-scatter.35.cloned.1.call-start = ((), (), s32[]{:S(2)}) async-start(), calls=%async_computation.31 | async-start | bytes 4718592 | tf_op jit(solution)/shard_map/reduce_scatter | solution.py:648
  710.9 70.9 %copy-start.4 = (bf16[128,2048]{1,0:T(8,128)(2,1)S(1)}, bf16[128,2048]{1,0:T(8,128)(2,1)}, u32[]{:S(2)}) copy-start(bf16[128,2048]{1,0:T(8,128)(2,1)} %param.15) | copy-start | bytes 1572868
  710.9 70.9 %copy-start.8 = (bf16[128,2048]{1,0:T(8,128)(2,1)S(1)}, bf16[128,2048]{1,0:T(8,128)(2,1)}, u32[]{:S(2)}) copy-start(bf16[128,2048]{1,0:T(8,128)(2,1)} %reduce-scatter.31.cloned.1.call-done) | copy-start | bytes 1572868
  710.9 70.9 %copy-start.28 = (f32[2048,1]{0,1:T(1,128)S(1)}, f32[2048,1]{0,1:T(1,128)}, u32[]{:S(2)}) copy-start(f32[2048,1]{0,1:T(1,128)} %copy-done.27) | copy-start | bytes 24580
  710.9 70.8 %copy-start.36 = (f32[128]{0:T(128)S(1)}, f32[128]{0:T(128)}, u32[]{:S(2)}) copy-start(f32[128]{0:T(128)} %copy-done.35) | copy-start | bytes 1540
  711.0 121.3 %all-gather.28.cloned.1.call-start = ((), (), s32[]{:S(2)}) async-start(), calls=%async_computation.22 | async-start | bytes 4718592 | tf_op jit(solution)/shard_map/all_gather | solution.py:680
  732.3 99.9 %copy-start.11 = (bf16[2,2,64,2048]{3,2,1,0:T(8,128)(2,1)S(1)}, bf16[2,2,64,2048]{3,2,1,0:T(8,128)(2,1)}, u32[]{:S(2)}) copy-start(bf16[2,2,64,2048]{3,2,1,0:T(8,128)(2,1)} %copy-done.10) | copy-start | bytes 3145732
  786.8 49.1 %copy-start.2 = (pred[1024,1024]{0,1:T(8,128)(4,1)S(1)}, pred[1024,1024]{0,1:T(8,128)(4,1)}, u32[]{:S(2)}) copy-start(pred[1024,1024]{0,1:T(8,128)(4,1)} %copy-done.1) | copy-start | bytes 3145732
  786.8 49.1 %copy-start.24 = (f32[2,1024]{1,0:T(2,128)S(1)}, f32[2,1024]{1,0:T(2,128)}, u32[]{:S(2)}) copy-start(f32[2,1024]{1,0:T(2,128)} %copy-done.23) | copy-start | bytes 24580
  786.8 120.0 %reduce-scatter.37.cloned.1.call-start = ((), (), s32[]{:S(2)}) async-start(), calls=%async_computation.32 | async-start | bytes 4718592 | tf_op jit(solution)/shard_map/reduce_scatter | solution.py:712
  832.3 9.5 slice-start
  857.9 116.3 %reduce-scatter.23.cloned.1.call-start = ((), (), s32[]{:S(2)}) async-start(), calls=%async_computation.24 | async-start | bytes 7208960 | tf_op jit(solution)/shard_map/reduce_scatter | solution.py:660
  869.7 155.8 %reduce-scatter.21.cloned.1.call-start = ((), (), s32[]{:S(2)}) async-start(), calls=%async_computation.23 | async-start | bytes 4587520 | tf_op jit(solution)/shard_map/reduce_scatter | solution.py:740
  912.7 157.4 %reduce-scatter.25.cloned.1.call-start = ((), (), s32[]{:S(2)}) async-start(), calls=%async_computation.25 | async-start | bytes 3604480 | tf_op jit(solution)/shard_map/reduce_scatter | solution.py:657
  920.2 218.6 %reduce-scatter.29.cloned.1.call-start = ((), (), s32[]{:S(2)}) async-start(), calls=%async_computation.27 | async-start | bytes 7208960 | tf_op jit(solution)/shard_map/reduce_scatter | solution.py:654
  931.3 238.7 %reduce-scatter.39.cloned.1.call-start = ((), (), s32[]{:S(2)}) async-start(), calls=%async_computation.33 | async-start | bytes 1310720
  935.9 2.0 collective-permute-start.1
  939.1 346.3 %reduce-scatter.27.cloned.1.call-start = ((), (), s32[]{:S(2)}) async-start(), calls=%async_computation.26 | async-start | bytes 14417920 | tf_op jit(solution)/shard_map/reduce_scatter | solution.py:651
  974.2 53.4 %all-to-all-start.3 = ((bf16[8,64,1408]{2,1,0:T(8,128)(2,1)}), bf16[8,64,1408]{2,1,0:T(8,128)(2,1)S(1)}, u32[]{:S(2)}, u32[]{:S(2)}) async-start(bf16[8,64,1408]{2,1,0:T(8,128)(2,1)} %bitcast.189), calls=%async_computation.5 | async-start | bytes 2883584 | tf_op jit(solution)/shard_map/all_to_all | solution.py:661
  1027.6 263.7 %all-to-all-start.2 = ((bf16[8,64,896]{2,1,0:T(8,128)(2,1)}), bf16[8,64,896]{2,1,0:T(8,128)(2,1)S(1)}, u32[]{:S(2)}, u32[]{:S(2)}) async-start(bf16[8,64,896]{2,1,0:T(8,128)(2,1)} %bitcast.184), calls=%async_computation.3 | async-start | bytes 1835008 | tf_op jit(solution)/shard_map/all_to_all | solution.py:743
  1171.8 118.4 %copy-start.9 = (f32[128,2048]{1,0:T(8,128)S(1)}, f32[128,2048]{1,0:T(8,128)}, u32[]{:S(2)}) copy-start(f32[128,2048]{1,0:T(8,128)} %get-tuple-element.91) | copy-start | bytes 3145732
  1171.8 118.4 %copy-start.14 = (bf16[128,2048]{1,0:T(8,128)(2,1)S(1)}, bf16[128,2048]{1,0:T(8,128)(2,1)}, u32[]{:S(2)}) copy-start(bf16[128,2048]{1,0:T(8,128)(2,1)} %reduce-scatter.37.cloned.1.call-done) | copy-start | bytes 1572868
  (26 other events, 72.8 us)
Sparse Core Ops, SparseCore 0:
  21.3 28.0 all-gather.29
  51.8 48.1 all-gather.13
  102.2 49.9 all-gather.11
  175.8 48.2 reduce-scatter.30
  227.5 72.8 all-gather.15
  302.3 64.7 all-gather.21
  368.9 41.7 all-gather.23
  412.4 47.1 all-gather.25
  461.4 112.4 all-gather.17
  575.6 65.7 all-gather.19
  678.9 52.4 reduce-scatter.32
  733.6 48.1 reduce-scatter.34
  786.9 45.2 all-gather.27
  858.0 48.7 reduce-scatter.36
  910.2 63.9 reduce-scatter.22
  977.1 48.3 reduce-scatter.20
  1028.3 41.7 reduce-scatter.24
  1072.9 65.8 reduce-scatter.28
  1142.2 27.6 reduce-scatter.38
  1173.2 112.1 reduce-scatter.26

commit v2 on v1

--- a/solution.py
+++ b/solution.py
@@ -1,6 +1,10 @@
+import functools
+
 import jax
 import jax.numpy as jnp
 from jax import lax
+from jax.experimental import pallas as pl
+from jax.experimental.pallas import tpu as pltpu
 from jax.sharding import PartitionSpec as P
 
 HD = 128
@@ -413,6 +417,357 @@
     )
 
 
+MESH_IDS = pl.DeviceIdType.MESH
+STRIP = 16
+
+
+class Line:
+    def __init__(self, chips):
+        me = lax.axis_index("expert")
+        self.chips = chips
+        self.z = me // 2
+        self.core = lax.rem(me, 2)
+        self.below = self.z > 0
+        self.above = self.z < chips - 1
+
+    def at(self, z, core):
+        return {"expert": 2 * z + core}
+
+    def meet(self):
+        barrier = pltpu.get_barrier_semaphore()
+
+        def hello(z, core):
+            pl.semaphore_signal(
+                barrier, inc=1, device_id=self.at(z, core), device_id_type=MESH_IDS
+            )
+
+        hello(self.z, 1 - self.core)
+        pl.when(self.above)(lambda: hello(self.z + 1, self.core))
+        pl.when(self.below)(lambda: hello(self.z - 1, self.core))
+        peers = 1 + jnp.minimum(self.z, 1) + jnp.minimum(self.chips - 1 - self.z, 1)
+        pl.semaphore_wait(barrier, peers)
+
+
+def gather_scratch(chips):
+    return [
+        pltpu.SemaphoreType.DMA((2, chips - 1)),
+        pltpu.SemaphoreType.DMA((2, chips - 1)),
+        pltpu.SemaphoreType.DMA((2 * chips - 1,)),
+        pltpu.SemaphoreType.DMA((2 * chips - 1,)),
+        pltpu.SemaphoreType.DMA,
+    ]
+
+
+def gather_line(line, own, out, send, recv, pair_send, pair_recv, local):
+    chips, z, core = line.chips, line.z, line.core
+    rows = own.shape[0]
+
+    def block(chip, which):
+        return out.at[pl.ds((2 * chip + which) * rows, rows)]
+
+    def hop(step, up):
+        origin = z - step if up else z + step
+        return pltpu.make_async_remote_copy(
+            src_ref=own if step == 0 else block(origin, core),
+            dst_ref=block(origin, core),
+            send_sem=send.at[0 if up else 1, step],
+            recv_sem=recv.at[0 if up else 1, step],
+            device_id=line.at(z + 1 if up else z - 1, core),
+            device_id_type=MESH_IDS,
+        )
+
+    def arrival(step, up):
+        origin = z - 1 - step if up else z + 1 + step
+        return pltpu.make_async_remote_copy(
+            src_ref=own,
+            dst_ref=block(origin, core),
+            send_sem=send.at[0 if up else 1, step],
+            recv_sem=recv.at[0 if up else 1, step],
+            device_id=line.at(z - 1 if up else z + 1, core),
+            device_id_type=MESH_IDS,
+        )
+
+    def across(index, origin, source, which):
+        return pltpu.make_async_remote_copy(
+            src_ref=source,
+            dst_ref=block(origin, which),
+            send_sem=pair_send.at[index],
+            recv_sem=pair_recv.at[index],
+            device_id=line.at(z, 1 - core),
+            device_id_type=MESH_IDS,
+        )
+
+    def sends(step, up):
+        return (z >= step) & line.above if up else (z + step <= chips - 1) & line.below
+
+    def comes(step, up):
+        return z - 1 - step >= 0 if up else z + 1 + step <= chips - 1
+
+    def pair_of(step, up):
+        return 1 + step + (0 if up else chips - 1)
+
+    keep = pltpu.make_async_copy(own, block(z, core), local)
+    keep.start()
+    for step in range(chips - 1):
+        for up in (True, False):
+            pl.when(sends(step, up))(lambda step=step, up=up: hop(step, up).start())
+        if step == 0:
+            across(0, z, own, core).start()
+        for up in (True, False):
+
+            def take(step=step, up=up):
+                arrival(step, up).wait_recv()
+                origin = z - 1 - step if up else z + 1 + step
+                across(pair_of(step, up), origin, block(origin, core), core).start()
+
+            pl.when(comes(step, up))(take)
+    across(0, z, own, core).wait_send()
+    across(0, z, own, 1 - core).wait_recv()
+    for step in range(chips - 1):
+        for up in (True, False):
+            pl.when(sends(step, up))(lambda step=step, up=up: hop(step, up).wait_send())
+
+            def settle(step=step, up=up):
+                origin = z - 1 - step if up else z + 1 + step
+                across(pair_of(step, up), origin, block(origin, core), core).wait_send()
+                across(pair_of(step, up), origin, block(origin, core), 1 - core).wait_recv()
+
+            pl.when(comes(step, up))(settle)
+    keep.wait()
+
+
+def scatter_scratch(chips, rows, width):
+    return [
+        pltpu.VMEM((chips, rows, width), jnp.bfloat16),
+        pltpu.VMEM((2, chips, rows, width), jnp.bfloat16),
+        pltpu.SemaphoreType.DMA((chips,)),
+        pltpu.SemaphoreType.DMA((chips,)),
+        pltpu.SemaphoreType.DMA((2, chips)),
+        pltpu.SemaphoreType.DMA((2, chips)),
+    ]
+
+
+def strips(rows, body):
+    @pl.loop(0, rows // STRIP)
+    def _(index):
+        body(pl.ds(pl.multiple_of(index * STRIP, STRIP), STRIP))
+
+
+def scatter_line(line, part, total, held, come, pair_send, pair_recv, send, recv):
+    chips, z, core = line.chips, line.z, line.core
+    rows = total.shape[0]
+
+    def start_of(chip, which):
+        return (2 * chip + which) * rows
+
+    def across(chip):
+        return pltpu.make_async_remote_copy(
+            src_ref=part.at[pl.ds(start_of(chip, 1 - core), rows)],
+            dst_ref=held.at[chip],
+            send_sem=pair_send.at[chip],
+            recv_sem=pair_recv.at[chip],
+            device_id=line.at(z, 1 - core),
+            device_id_type=MESH_IDS,
+        )
+
+    def hop(chip, up, target):
+        way = 0 if up else 1
+        return pltpu.make_async_remote_copy(
+            src_ref=held.at[chip],
+            dst_ref=come.at[way, chip],
+            send_sem=send.at[way, chip],
+            recv_sem=recv.at[way, chip],
+            device_id=line.at(target, core),
+            device_id_type=MESH_IDS,
+        )
+
+    def value(chip, strip, ways):
+        first = start_of(chip, core)
+        mine = part[pl.ds(pl.multiple_of(first + strip.start, STRIP), STRIP), :]
+        summed = mine.astype(jnp.float32) + held[chip, strip, :].astype(jnp.float32)
+        for way in ways:
+            summed = summed + come[way, chip, strip, :].astype(jnp.float32)
+        return summed
+
+    def add(chip, ways):
+        def body(strip):
+            held[chip, strip, :] = value(chip, strip, ways).astype(jnp.bfloat16)
+
+        strips(rows, body)
+
+    order = []
+    for near in range((chips + 1) // 2):
+        for chip in (chips - 1 - near, near):
+            if chip not in order:
+                order.append(chip)
+    for chip in order:
+        across(chip).start()
+
+    def forward(chip, up):
+        across(chip).wait_recv()
+        way = 0 if up else 1
+
+        def with_arrival():
+            hop(chip, up, z).wait_recv()
+            add(chip, (way,))
+
+        more = line.below if up else line.above
+        pl.when(more)(with_arrival)
+        pl.when(jnp.logical_not(more))(lambda: add(chip, ()))
+        hop(chip, up, z + 1 if up else z - 1).start()
+
+    def up_chip(step):
+        return chips - 1 - step + z
+
+    def down_chip(step):
+        return step - (chips - 1 - z)
+
+    def up_sends(step):
+        return (z <= step) & line.above
+
+    def down_sends(step):
+        return (step >= chips - 1 - z) & line.below
+
+    for step in range(chips - 1):
+        pl.when(up_sends(step))(lambda step=step: forward(up_chip(step), True))
+        pl.when(down_sends(step))(lambda step=step: forward(down_chip(step), False))
+
+    across(z).wait_recv()
+    pl.when(line.below)(lambda: hop(z, True, z).wait_recv())
+    pl.when(line.above)(lambda: hop(z, False, z).wait_recv())
+
+    def last(ways):
+        def body(strip):
+            total[strip, :] = value(z, strip, ways)
+
+        strips(rows, body)
+
+    inner = line.below & line.above
+    pl.when(inner)(lambda: last((0, 1)))
+    pl.when(jnp.logical_not(line.below))(lambda: last((1,)))
+    pl.when(jnp.logical_not(line.above))(lambda: last((0,)))
+    for chip in order:
+        across(chip).wait_send()
+    for step in range(chips - 1):
+        pl.when(up_sends(step))(
+            lambda step=step: hop(up_chip(step), True, z + 1).wait_send()
+        )
+        pl.when(down_sends(step))(
+            lambda step=step: hop(down_chip(step), False, z - 1).wait_send()
+        )
+
+
+def gather_kernel(chips, own, out, *scratch):
+    line = Line(chips)
+    line.meet()
+    gather_line(line, own, out, *scratch)
+
+
+def middle_kernel(chips, part, hidden, gain, middle, normed_all, total, normed, *scratch):
+    line = Line(chips)
+    line.meet()
+    scatter_line(line, part, total, *scratch[:6])
+
+    def body(strip):
+        rows = hidden[strip, :].astype(jnp.float32) + total[strip, :]
+        middle[strip, :] = rows
+        normed[strip, :] = (rows * rms_scale(rows) * gain[...]).astype(jnp.bfloat16)
+
+    strips(hidden.shape[0], body)
+    gather_line(line, normed, normed_all, *scratch[6:])
+
+
+def branch_kernel(
+    chips, part, middle, gain, out_grad, probs, collect, router,
+    grad_middle, grad_all, heads, term, total, turned, *scratch
+):
+    line = Line(chips)
+    line.meet()
+    scatter_line(line, part, total, *scratch[:6])
+    width = middle.shape[1]
+    term[...] = jnp.zeros_like(term)
+
+    def body(strip):
+        tail = jnp.dot(
+            total[strip, width:].astype(jnp.bfloat16), collect[...],
+            preferred_element_type=jnp.float32,
+        )
+        prob = probs[strip, :]
+        lane = lax.broadcasted_iota(jnp.int32, prob.shape, 1)
+        inner = jnp.sum(jnp.where(lane > 0, prob * tail, 0.0), axis=1, keepdims=True)
+        head = jnp.where(lane > 0, prob * (tail - inner), tail * prob * (1.0 - prob))
+        head = head.astype(jnp.bfloat16)
+        heads[strip, :] = head
+        grad = total[strip, :width] + jnp.dot(
+            head, router[...], preferred_element_type=jnp.float32
+        )
+        rows = middle[strip, :]
+        scale = rms_scale(rows)
+        weighted = grad * gain[...]
+        mean = jnp.mean(weighted * rows, axis=-1, keepdims=True)
+        term[...] += jnp.sum(grad * rows * scale, axis=0, keepdims=True)
+        result = (
+            out_grad[strip, :].astype(jnp.float32)
+            + scale * weighted
+            - rows * scale * scale * scale * mean
+        )
+        grad_middle[strip, :] = result
+        turned[strip, :] = result.astype(jnp.bfloat16)
+
+    strips(middle.shape[0], body)
+    gather_line(line, turned, grad_all, *scratch[6:])
+
+
+def input_kernel(chips, part, hidden, gain, grad_middle, input_grad, term, total, *scratch):
+    line = Line(chips)
+    line.meet()
+    scatter_line(line, part, total, *scratch)
+    term[...] = jnp.zeros_like(term)
+
+    def body(strip):
+        grad = total[strip, :]
+        rows = hidden[strip, :].astype(jnp.float32)
+        scale = rms_scale(rows)
+        weighted = grad * gain[...]
+        mean = jnp.mean(weighted * rows, axis=-1, keepdims=True)
+        term[...] += jnp.sum(grad * rows * scale, axis=0, keepdims=True)
+        result = (
+            grad_middle[strip, :] + scale * weighted - rows * scale * scale * scale * mean
+        )
+        input_grad[strip, :] = result.astype(jnp.bfloat16)
+
+    strips(hidden.shape[0], body)
+
+
+def output_kernel(chips, part, middle, valid, output, total, *scratch):
+    line = Line(chips)
+    line.meet()
+    scatter_line(line, part, total, *scratch)
+
+    def body(strip):
+        rows = valid[strip, :] * (middle[strip, :] + total[strip, :])
+        output[strip, :] = rows.astype(jnp.bfloat16)
+
+    strips(middle.shape[0], body)
+
+
+def remote_call(kernel, chips, inputs, outputs, scratch, number, micros):
+    moved = sum(a.size * a.dtype.itemsize for a in inputs)
+    return pl.pallas_call(
+        functools.partial(kernel, chips),
+        out_shape=[jax.ShapeDtypeStruct(shape, kind) for shape, kind, _ in outputs],
+        in_specs=[pl.BlockSpec(memory_space=pltpu.VMEM)] * len(inputs),
+        out_specs=[
+            pl.BlockSpec(memory_space=pl.ANY if far else pltpu.VMEM) for _, _, far in outputs
+        ],
+        scratch_shapes=scratch,
+        compiler_params=pltpu.CompilerParams(collective_id=number, has_side_effects=True),
+        cost_estimate=pl.CostEstimate(
+            flops=int(micros * 1e9), bytes_accessed=moved, transcendentals=0
+        ),
+    )(*inputs)
+
+
 def bf16(values):
     return values.astype(jnp.bfloat16)
 
@@ -472,7 +827,12 @@
     bias_cols = 3 * width // (parts * size) // block
     extra = 128
     shared_block = shared_out.shape[0]
+    expert_block = expert_out.shape[1]
+    pair_block = expert_block + shared_block
+    hidden_units = parts * pair_block
+    padded = -(-hidden_units // 128) * 128
     own_shared = parts * shared_block
+    chips = places
     own_qkv = 3 * own_heads * HD
 
     def by_head(columns):
@@ -486,11 +846,21 @@
         return cut.transpose(2, 3, 1, 4, 0, 5).reshape(count, 3 * width)
 
     side = jnp.pad(bf16(routes), ((0, 0), (0, extra - top)))
-    gathered = lax.all_gather(
-        jnp.concatenate([hidden_in, side], axis=1), "expert", axis=0, tiled=True
+    (gathered,) = remote_call(
+        gather_kernel,
+        chips,
+        [jnp.concatenate([hidden_in, out_grad, side], axis=1)],
+        [((group, 2 * width + extra), jnp.bfloat16, True)],
+        gather_scratch(chips),
+        0,
+        70,
     )
     hidden_all = gathered[:, :width].astype(jnp.float32)
-    routes_all = gathered[:, width : width + top].astype(jnp.int32)
+    routes_all = gathered[:, 2 * width : 2 * width + top].astype(jnp.int32)
+
+    weight_down = lax.all_gather(
+        jnp.concatenate([expert_out[0], shared_out], axis=0), "dp", axis=0, tiled=True
+    )
 
     small = jnp.concatenate(
         [
@@ -503,21 +873,35 @@
         axis=1,
     )
     small = jnp.pad(small, ((0, 0), (0, extra - small.shape[1])))
+    cut = shared_in.reshape(block, 2, parts, size, shared_block)
+    cut = cut.transpose(3, 0, 1, 2, 4).reshape(size, block, 2 * own_shared)
     sent = jnp.concatenate(
-        [by_head(qkv_weight), jnp.broadcast_to(small[None], (size, block, extra))], axis=2
+        [by_head(qkv_weight), jnp.broadcast_to(small[None], (size, block, extra)), cut], axis=2
     )
     sent = lax.all_to_all(sent, "expert", split_axis=0, concat_axis=0, tiled=True)
-    qkv_full = lax.all_gather(
-        sent.reshape(size * block, own_qkv + extra), "dp", axis=0, tiled=True
-    )
+    sent = sent.reshape(size * block, own_qkv + extra + 2 * own_shared)
+    out_cols = width * block // (size * block)
+    first = jnp.concatenate(
+        [sent[:, : own_qkv + extra], out_weight.reshape(size * block, out_cols)], axis=1
+    )
+    first, weight_down = lax.optimization_barrier((first, weight_down))
+    qkv_full = lax.all_gather(first, "dp", axis=0, tiled=True)
     weight_qkv = qkv_full[:, :own_qkv]
-    small = qkv_full[:, own_qkv:]
+    small = qkv_full[:, own_qkv : own_qkv + extra]
     gain_one = small[:, 0].astype(jnp.float32)
     gain_two = small[:, 1].astype(jnp.float32)
-    weight_router = small[:, 2 : 3 + experts]
+    router_rows = jnp.pad(small[:, 2 : 3 + experts].T, ((0, 127 - experts), (0, 0)))
     bias_all = by_head(small[:, 3 + experts : 3 + experts + bias_cols].reshape(1, 3 * width))
     bias_own = lax.dynamic_index_in_dim(bias_all, me, 0, keepdims=False).astype(jnp.float32)
 
+    cut = sent[:, own_qkv + extra :].reshape(size * block, 2, parts, shared_block)
+    up = expert_in[0].reshape(size * block, 2, parts, expert_block)
+    up = jnp.concatenate([up, cut], axis=3).reshape(size * block, 2, hidden_units)
+    up = jnp.pad(up, ((0, 0), (0, 0), (0, padded - hidden_units)))
+    up = up.reshape(size * block, 2 * padded)
+    up, qkv_full = lax.optimization_barrier((up, qkv_full))
+    weight_up = lax.all_gather(up, "dp", axis=0, tiled=True)
+
     swap = [(i, i ^ 1) for i in range(size)]
 
     def own_half(values):
@@ -526,16 +910,12 @@
     def other_half(values):
         return lax.dynamic_slice_in_dim(values, (1 - core) * half, half, 0)
 
-    out_blocks = lax.all_gather(out_weight[None], "dp", axis=0, tiled=True)
+    out_blocks = qkv_full[:, own_qkv + extra :].reshape(parts, block, width)
     kept = own_half(out_blocks)
     came = lax.ppermute(other_half(out_blocks), "expert", swap)
     weight_out = jnp.stack(
         [jnp.where(core == 0, kept, came), jnp.where(core == 0, came, kept)], axis=1
     ).reshape(own_heads * HD, width)
-
-    cut = shared_in.reshape(block, 2, parts, size, shared_block)
-    cut = cut.transpose(3, 0, 1, 2, 4).reshape(size, block, 2 * own_shared)
-    cut = lax.all_to_all(cut, "expert", split_axis=0, concat_axis=0, tiled=True)
 
     segment, position = segment_table(lengths[0], group)
     valid_all = (segment < lengths.shape[1] - 1).astype(jnp.float32)[:, None]
@@ -543,8 +923,7 @@
     allowed = (
         (segment[:, None] == segment[None, :]) & (position[:, None] >= position[None, :])
     )[None]
-    scale_first_all = rms_scale(hidden_all)
-    normed_one = bf16(hidden_all * scale_first_all * gain_one)
+    normed_one = bf16(hidden_all * rms_scale(hidden_all) * gain_one)
     projected = mm(normed_one, weight_qkv) + bias_own
     split = projected.reshape(group, 3, own_heads, HD)
     query_low = bf16(rotate(split[:, 0], cosine, sine))
@@ -567,25 +946,20 @@
             "hqk,khd->qhd", weights_low, value_low, preferred_element_type=jnp.float32
         ).reshape(group, own_heads * HD)
     )
-    branch = lax.psum_scatter(
-        bf16(mm(attended, weight_out)), "expert", scatter_dimension=0, tiled=True
-    )
-    inputs = hidden_in.astype(jnp.float32)
-    middle = inputs + branch.astype(jnp.float32)
-    scale_second = rms_scale(middle)
-    normed_two = bf16(middle * scale_second * gain_two)
-    normed_all = lax.all_gather(normed_two, "expert", axis=0, tiled=True)
-
-    weight_expert_in = lax.all_gather(expert_in, "dp", axis=1, tiled=True)[0]
-    weight_expert_out = lax.all_gather(expert_out, "dp", axis=1, tiled=True)[0]
-    weight_shared_in = lax.all_gather(
-        cut.reshape(size * block, 2 * own_shared), "dp", axis=0, tiled=True
-    )
-    weight_shared_out = lax.all_gather(shared_out, "dp", axis=0, tiled=True)
-    grad_all = lax.all_gather(out_grad, "expert", axis=0, tiled=True)
-
-    gate_logits = mm(normed_all, weight_router)
-    logits = gate_logits[:, 1:]
+    middle, normed_all = remote_call(
+        middle_kernel,
+        chips,
+        [bf16(mm(attended, weight_out)), hidden_in, gain_two[None, :]],
+        [((rows, width), jnp.float32, False), ((group, width), jnp.bfloat16, True)],
+        [pltpu.VMEM((rows, width), jnp.float32), pltpu.VMEM((rows, width), jnp.bfloat16)]
+        + scatter_scratch(chips, rows, width)
+        + gather_scratch(chips),
+        1,
+        70,
+    )
+
+    gate_logits = mm_nt(normed_all, router_rows)
+    logits = gate_logits[:, 1 : 1 + experts]
     opener_all = jax.nn.sigmoid(gate_logits[:, :1])
     peak_logit = jnp.max(logits, axis=-1, keepdims=True)
     router_total = peak_logit + jnp.log(
@@ -593,73 +967,56 @@
     )
     probs_all = jnp.exp(logits - router_total)
     expert_ids = jnp.arange(experts, dtype=jnp.int32)
+    mine = expert_ids[None, :] == me
     named = jnp.sum((routes_all == me).astype(jnp.float32), axis=1, keepdims=True)
-    own_prob = jnp.sum(
-        jnp.where(expert_ids[None, :] == me, probs_all, 0.0), axis=1, keepdims=True
-    )
-    gate_own = named * own_prob
-
-    expert_up = mm(normed_all, weight_expert_in)
-    expert_hidden = bf16(swiglu(expert_up))
-    expert_result = bf16(mm(expert_hidden, weight_expert_out)).astype(jnp.float32)
-    shared_up = mm(normed_all, weight_shared_in)
-    shared_hidden = bf16(swiglu(shared_up))
-    shared_rows = mm(shared_hidden, weight_shared_out)
-    grad_rows = grad_all.astype(jnp.float32) * valid_all
-    dot_expert = named * jnp.sum(grad_rows * expert_result, axis=1, keepdims=True)
-    dot_shared = jnp.sum(grad_rows * shared_rows, axis=1, keepdims=True)
-    mine = expert_ids[None, :] == me
-    expert_high, expert_low = two_parts(dot_expert)
-    shared_high, shared_low = two_parts(dot_shared)
-    zero = jnp.zeros((), jnp.bfloat16)
-    riders = jnp.concatenate(
-        [
-            jnp.where(mine, column, zero)
-            for column in (expert_high, expert_low, shared_high, shared_low)
-        ],
-        axis=1,
-    )
-    riders = jnp.pad(riders, ((0, 0), (0, extra - riders.shape[1])))
-    combined = jnp.concatenate(
-        [bf16(gate_own * expert_result + opener_all * shared_rows), riders], axis=1
-    )
-    summed = lax.psum_scatter(combined, "expert", scatter_dimension=0, tiled=True)
-
-    def rows_of(values):
-        return lax.dynamic_slice_in_dim(values, me * rows, rows, 0)
-
-    valid_rows = rows_of(valid_all)
-    output = bf16(valid_rows * (middle + summed[:, :width].astype(jnp.float32)))
-    tail = summed[:, width : width + 4 * experts].astype(jnp.float32)
-    grad_probs = tail[:, :experts] + tail[:, experts : 2 * experts]
-    dot_gate = jnp.sum(tail[:, 2 * experts :], axis=1, keepdims=True)
-
-    grad_shared_rows = bf16(grad_rows * opener_all)
-    grad_shared_up = bf16(swiglu_back(shared_up, mm_nt(grad_shared_rows, weight_shared_out)))
-    term_shared_out = mm_tn(shared_hidden, grad_shared_rows)
-    term_shared_in = mm_tn(normed_all, grad_shared_up)
-    grad_result = bf16(gate_own * grad_rows)
-    grad_expert_up = bf16(swiglu_back(expert_up, mm_nt(grad_result, weight_expert_out)))
-    term_expert_out = mm_tn(expert_hidden, grad_result)
-    term_expert_in = mm_tn(normed_all, grad_expert_up)
-    grad_normed_part = bf16(
-        mm_nt(grad_shared_up, weight_shared_in) + mm_nt(grad_expert_up, weight_expert_in)
-    )
-    grad_normed_two = lax.psum_scatter(
-        grad_normed_part, "expert", scatter_dimension=0, tiled=True
-    ).astype(jnp.float32)
-    grad_expert_in = lax.psum_scatter(
-        bf16(term_expert_in)[None], "dp", scatter_dimension=1, tiled=True
-    ).astype(jnp.float32)
-    grad_expert_out = lax.psum_scatter(
-        bf16(term_expert_out)[None], "dp", scatter_dimension=1, tiled=True
-    ).astype(jnp.float32)
-    grad_shared_out = lax.psum_scatter(
-        bf16(term_shared_out), "dp", scatter_dimension=0, tiled=True
-    ).astype(jnp.float32)
-    cut = lax.psum_scatter(bf16(term_shared_in), "dp", scatter_dimension=0, tiled=True)
+    gate_own = named * jnp.sum(jnp.where(mine, probs_all, 0.0), axis=1, keepdims=True)
+
+    routed_unit = (jnp.arange(hidden_units, dtype=jnp.int32) % pair_block < expert_block)[None, :]
+    unit_scale = jnp.where(routed_unit, gate_own, opener_all)
+    grad_rows = bf16(
+        gathered[:, width : 2 * width].astype(jnp.float32) * valid_all
+    )
+    both_up = mm(normed_all, weight_up)
+
+    gate_part = both_up[:, :hidden_units]
+    up_part = both_up[:, padded : padded + hidden_units]
+    hidden = bf16(jax.nn.silu(gate_part) * up_part)
+    scaled_hidden = bf16(unit_scale * hidden.astype(jnp.float32))
+    term_down = bf16(mm_tn(scaled_hidden, grad_rows))
+    grad_down = lax.psum_scatter(term_down, "dp", scatter_dimension=0, tiled=True).astype(
+        jnp.float32
+    )
+    grad_shared_out = grad_down[expert_block:]
+    grad_expert_out = grad_down[None, :expert_block]
+    combined = bf16(mm(scaled_hidden, weight_down))
+
+    grad_hidden = mm_nt(grad_rows, weight_down)
+    product = hidden.astype(jnp.float32) * grad_hidden
+    dot_expert = named * jnp.sum(jnp.where(routed_unit, product, 0.0), axis=1, keepdims=True)
+    dot_shared = jnp.sum(jnp.where(routed_unit, 0.0, product), axis=1, keepdims=True)
+    grad_hidden = grad_hidden * unit_scale
+    sigmoid_gate = jax.nn.sigmoid(gate_part)
+    grad_gate = grad_hidden * up_part * sigmoid_gate * (1.0 + gate_part * (1.0 - sigmoid_gate))
+    grad_up = grad_hidden * gate_part * sigmoid_gate
+    wide = ((0, 0), (0, padded - hidden_units))
+    grad_both_up = jnp.concatenate(
+        [jnp.pad(bf16(grad_gate), wide), jnp.pad(bf16(grad_up), wide)], axis=1
+    )
+    term_up = bf16(mm_tn(normed_all, grad_both_up))
+    up = lax.psum_scatter(term_up, "dp", scatter_dimension=0, tiled=True)
+    up = up.reshape(size * block, 2, padded)[:, :, :hidden_units]
+    up = up.reshape(size * block, 2, parts, pair_block)
+    grad_expert_in = (
+        up[:, :, :, :expert_block]
+        .reshape(1, size * block, 2 * parts * expert_block)
+        .astype(jnp.float32)
+    )
     cut = lax.all_to_all(
-        cut.reshape(size, block, 2 * own_shared), "expert", split_axis=0, concat_axis=0, tiled=True
+        up[:, :, :, expert_block:].reshape(size, block, 2 * own_shared),
+        "expert",
+        split_axis=0,
+        concat_axis=0,
+        tiled=True,
     )
     grad_shared_in = (
         cut.reshape(size, block, 2, parts, shared_block)
@@ -668,18 +1025,50 @@
         .astype(jnp.float32)
     )
 
-    opener = rows_of(opener_all)
-    probs = rows_of(probs_all)
-    grad_gate_logit = dot_gate * opener * (1.0 - opener)
-    grad_logits = probs * (grad_probs - jnp.sum(probs * grad_probs, axis=-1, keepdims=True))
-    grad_heads = bf16(jnp.concatenate([grad_gate_logit, grad_logits], axis=1))
-    term_router = mm_tn(normed_two, grad_heads)
-    grad_normed_two = grad_normed_two + mm_nt(grad_heads, weight_router)
-    grad_middle_norm, term_norm_two = norm_back(middle, scale_second, gain_two, grad_normed_two)
-    grad_middle = rows_of(grad_rows) + grad_middle_norm
-    grad_branch = lax.all_gather(bf16(grad_middle), "expert", axis=0, tiled=True)
-
-    term_out = bf16(mm_tn(attended, grad_branch)).reshape(half, 2, block, width)
+    zero = jnp.zeros((), jnp.bfloat16)
+    riders = jnp.concatenate(
+        [
+            jnp.where(mine, column, zero)
+            for column in two_parts(dot_shared) + two_parts(dot_expert)
+        ],
+        axis=1,
+    )
+    riders = jnp.pad(riders, ((0, 0), (0, extra - riders.shape[1])))
+    part = jnp.concatenate([bf16(mm_nt(grad_both_up, weight_up)), riders], axis=1)
+
+    def rows_of(values):
+        return lax.dynamic_slice_in_dim(values, me * rows, rows, 0)
+
+    rider = jnp.arange(extra, dtype=jnp.int32)[:, None]
+    lane = jnp.arange(128, dtype=jnp.int32)[None, :]
+    collect = bf16(
+        ((rider < 2 * experts) & (lane == 0))
+        | ((rider >= 2 * experts) & (rider < 4 * experts) & (lane == 1 + rider % experts))
+    )
+    probs = jnp.pad(
+        rows_of(jnp.concatenate([opener_all, probs_all], axis=1)), ((0, 0), (0, 127 - experts))
+    )
+    grad_middle, grad_branch, grad_heads, term_norm_two = remote_call(
+        branch_kernel,
+        chips,
+        [part, middle, gain_two[None, :], rows_of(grad_rows), probs, collect, router_rows],
+        [
+            ((rows, width), jnp.float32, False),
+            ((group, width), jnp.bfloat16, True),
+            ((rows, 128), jnp.bfloat16, False),
+            ((1, width), jnp.float32, False),
+        ],
+        [
+            pltpu.VMEM((rows, width + extra), jnp.float32),
+            pltpu.VMEM((rows, width), jnp.bfloat16),
+        ]
+        + scatter_scratch(chips, rows, width + extra)
+        + gather_scratch(chips),
+        2,
+        75,
+    )
+    term_router = mm_tn(rows_of(normed_all), grad_heads)[:, : 1 + experts]
+
     grad_attended = bf16(mm_nt(grad_branch, weight_out)).reshape(group, own_heads, HD)
     weights_again = jnp.exp(score_rows() - log_total)
     grad_weights = jnp.einsum(
@@ -708,44 +1097,63 @@
             axis=1,
         ).reshape(group, own_qkv)
     )
-    grad_normed_part = bf16(mm_nt(grad_projected, weight_qkv))
-    grad_normed_one = lax.psum_scatter(
-        grad_normed_part, "expert", scatter_dimension=0, tiled=True
-    ).astype(jnp.float32)
-    scale_first = rms_scale(inputs)
-    grad_input_norm, term_norm_one = norm_back(inputs, scale_first, gain_one, grad_normed_one)
-    input_grad = bf16(grad_middle + grad_input_norm)
-
+    input_grad, term_norm_one = remote_call(
+        input_kernel,
+        chips,
+        [
+            bf16(mm_nt(grad_projected, weight_qkv)),
+            hidden_in,
+            gain_one[None, :],
+            grad_middle,
+        ],
+        [((rows, width), jnp.bfloat16, False), ((1, width), jnp.float32, False)],
+        [pltpu.VMEM((rows, width), jnp.float32)] + scatter_scratch(chips, rows, width),
+        3,
+        40,
+    )
+
+    term_out = bf16(mm_tn(attended, grad_branch)).reshape(half, 2, block, width)
     kept = jnp.where(core == 0, term_out[:, 0], term_out[:, 1])
     given = jnp.where(core == 0, term_out[:, 1], term_out[:, 0])
     came = lax.ppermute(given, "expert", swap)
     out_blocks = jnp.concatenate(
         [jnp.where(core == 0, kept, came), jnp.where(core == 0, came, kept)], axis=0
     )
-    grad_out_weight = lax.psum_scatter(
-        out_blocks, "dp", scatter_dimension=0, tiled=True
-    ).astype(jnp.float32)[0]
-
     term_qkv = mm_tn(normed_one, grad_projected)
     term_bias = jnp.sum(grad_projected.astype(jnp.float32), axis=0)
     bias_slots = jnp.where(jnp.arange(size)[:, None] == me, term_bias[None, :], 0.0)
     bias_rows = from_head(bias_slots[:, None, :]).reshape(width, bias_cols)
     small_terms = jnp.concatenate(
-        [term_norm_one[:, None], term_norm_two[:, None], term_router, bias_rows], axis=1
+        [term_norm_one[0][:, None], term_norm_two[0][:, None], term_router, bias_rows], axis=1
     )
     count = small_terms.shape[1]
     small_high, small_low = two_parts(small_terms)
     small_terms = jnp.concatenate([small_high, small_low], axis=1)
     small_terms = jnp.pad(small_terms, ((0, 0), (0, extra - 2 * count)))
     back = lax.psum_scatter(
-        jnp.concatenate([bf16(term_qkv), small_terms], axis=1), "dp", scatter_dimension=0, tiled=True
-    )
+        jnp.concatenate(
+            [bf16(term_qkv), small_terms, out_blocks.reshape(width, out_cols)], axis=1
+        ),
+        "dp",
+        scatter_dimension=0,
+        tiled=True,
+    )
+    grad_out_weight = back[:, own_qkv + extra :].reshape(block, width).astype(jnp.float32)
     back = lax.all_to_all(
-        back.reshape(size, block, own_qkv + extra), "expert", split_axis=0, concat_axis=0, tiled=True
+        back[:, : own_qkv + extra].reshape(size, block, own_qkv + extra), "expert", split_axis=0, concat_axis=0, tiled=True
     ).astype(jnp.float32)
     grad_qkv = from_head(back[:, :, :own_qkv])
     small_sum = jnp.sum(back[:, :, own_qkv:], axis=0)
     small_sum = small_sum[:, :count] + small_sum[:, count : 2 * count]
+    (output,) = remote_call(
+        output_kernel,
+        chips,
+        [combined, middle, rows_of(valid_all)],
+        [((rows, width), jnp.bfloat16, False)],
+        [pltpu.VMEM((rows, width), jnp.float32)] + scatter_scratch(chips, rows, width),
+        4,
+        40,
+    )
     grad_norm1 = small_sum[:, 0]
     grad_norm2 = small_sum[:, 1]
     grad_shared_gate = small_sum[:, 2]

time: 1310 us -> 1000 us (0.76)
  waiting for transfers between devices: 889 us -> 265 us
  Pallas kernels: 0 us -> 361 us
  blocking collectives: 63.9 us -> 0 us
  local copies, waits for them, and re-layouts: 62.8 us -> 104 us
  matrix products: 208 us -> 187 us
    all_gather x10 -> x3, waiting for transfers between devices: 426 us -> 57.9 us  [the longest x1 46.1 us: group_device(): qkv_full = lax.all_gather(first, 'dp', axis=0, tiled=True)]
    pallas_call x0 -> x5, Pallas kernels: none -> 361 us  [remote_call(): pl.pallas_call(functools.partial(kernel, chips), out_shape=[jax.ShapeDtyp...]
    reduce_scatter x9 -> x3, waiting for transfers between devices: 426 us -> 153 us  [the longest x1 142 us: group_device(): up = lax.psum_scatter(term_up, 'dp', scatter_dimension=0, tiled=True)]
    all_to_all x1 -> x0, blocking collectives: 63.9 us -> none  [group_device(): cut = lax.all_to_all(cut, 'expert', split_axis=0, concat_axis=0, tiled=True)]
    all_to_all x1, waiting for transfers between devices: 23 us -> 54.4 us  [group_device(): lax.all_to_all(sent, 'expert', split_axis=0, concat_axis=0, tiled=True)]
    slice x1 -> x13, local copies, waits for them, and re-layouts: 0.76 us -> 19 us  [the longest x2 5.1 us: group_device(): sent[:, own_qkv + extra:].reshape(size * block, 2, parts, shared_block)]
    dot_general x7 -> x4, matrix products: 63.1 us -> 52.6 us  [mm(): return jnp.dot(left, right, preferred_element_type=jnp.float32)]
    dot_general x7 -> x5, matrix products: 59.6 us -> 53.1 us  [mm_tn(): lax.dot_general(left, right, (((0,), (0,)), ((), ())), preferred_element_...]
  transfers between devices with their start and end apart: 25 -> 11, of which waited for: 21 -> 5; matrix products, arithmetic and copies ran while one was open for 16% -> 20% of each run, Pallas kernels for 0% -> 28%
where the time goes in v2:
time: 1000 us; the launch traced here: 993 us
  Pallas kernels  361 us (36%)
  waiting for transfers between devices  265 us (26%)
  matrix products  187 us (19%)
  local copies, waits for them, and re-layouts  104 us (10%)
  other arithmetic  43.8 us (4%)
  starting transfers between devices  16.7 us (2%)
  between operations  15.6 us (2%)
    pallas_call x5, Pallas kernels, remote_call(): pl.pallas_call(functools.partial(kernel, chips), out_shape=[jax.ShapeDtyp...  361 us
    reduce_scatter x1, waiting for transfers between devices, group_device(): up = lax.psum_scatter(term_up, 'dp', scatter_dimension=0, tiled=True)  142 us
    dot_general x5, matrix products, mm_nt(): lax.dot_general(left, right, (((1,), (1,)), ((), ())), preferred_element_...  63.5 us
    all_to_all x1, waiting for transfers between devices, group_device(): lax.all_to_all(sent, 'expert', split_axis=0, concat_axis=0, tiled=True)  54.4 us
    dot_general x5, matrix products, mm_tn(): lax.dot_general(left, right, (((0,), (0,)), ((), ())), preferred_element_...  53.1 us
    dot_general x4, matrix products, mm(): return jnp.dot(left, right, preferred_element_type=jnp.float32)  52.6 us
    all_gather x1, waiting for transfers between devices, group_device(): qkv_full = lax.all_gather(first, 'dp', axis=0, tiled=True)  46.1 us
    convert_element_type x3, local copies, waits for them, and re-layouts, group_device(): grad_shared_in = cut.reshape(size, block, 2, parts, shared_block).transpo...  20.6 us
  transfers between devices with their start and end apart: 11, of which 5 were waited for; matrix products, arithmetic and copies ran while one was open for 20% of the time, Pallas kernels for 28%

profile of v2, /device:TPU:0, one launch (start us, length us, event | category | flops | bytes accessed | tf_op | source)
XLA Modules:
  0.0 992.8 jit_solution(3567444815789010282)
XLA Ops:
  7.2 3.3 pad_maximum_fusion.3
  10.5 5.0 reshape.455
  15.6 2.5 copy.294
  26.6 6.4 all-to-all-start
  33.4 54.4 %all-to-all-done = bf16[8,64,2304]{2,1,0:T(8,128)(2,1)S(1)} async-done(((bf16[8,64,2304]{2,1,0:T(8,128)(2,1)}), bf16[8,64,2304]{2,1,0:T(8,128)(2,1)S(1)}, u32[]{:S(2)}, u32[]{:S(2)}) %all-to-all-start) | async-done | bytes 2359328 | tf_op jit(solution)/shard_map/all_to_all | solution.py:881
  91.4 11.8 %all-gather.4.cloned.1.call-done = bf16[2112,2048]{1,0:T(8,128)(2,1)} async-done(((bf16[528,2048]{1,0:T(8,128)(2,1)}), bf16[2112,2048]{1,0:T(8,128)(2,1)}) %all-gather.4.cloned.1.call-update) | async-done | bytes 8650768 | tf_op jit(solution)/shard_map/all_gather | solution.py:861
  103.3 3.1 copy.251
  106.4 2.6 slice.205
  109.0 2.5 copy.252
  115.9 46.1 %all-gather.6.cloned.1.call-done = bf16[2048,1152]{0,1:T(8,128)(2,1)} async-done(((bf16[512,1152]{0,1:T(8,128)(2,1)}), bf16[2048,1152]{0,1:T(8,128)(2,1)}) %all-gather.6.cloned.1.call-update) | async-done | bytes 4718608 | tf_op jit(solution)/shard_map/all_gather | solution.py:888
  165.3 80.2 %shard_map.246 = bf16[1024,4224]{1,0:T(8,128)(2,1)} custom-call(bf16[128,4224]{1,0:T(8,128)(2,1)} %fusion.20.own), custom_call_target="tpu_custom_call" | custom-call | flops 70000001024 | bytes 1081344 | tf_op jit(solution)/shard_map/pallas_call | solution.py:756
  247.0 2.9 broadcast_multiply_fusion.3
  249.9 4.9 fusion.5
  264.1 6.9 fusion.15
  278.9 2.7 convolution_convert_fusion.8
  282.8 3.2 convolution_convert_fusion.4.part
  286.0 81.5 %shard_map.247 = (f32[128,2048]{1,0:T(8,128)}, bf16[1024,2048]{1,0:T(8,128)(2,1)}) custom-call(bf16[1024,2048]{1,0:T(8,128)(2,1)} %convolution_convert_fusion.4.part, bf16[128,2048]{1,0:T(8,128)(2,1)} %hidden.3, f32[1,2048]{1,0:T(1,128)} %get-tuple-element.133.gain), custom_call_target="tpu_custom_call" | custom-call | flops 70000001024 | bytes 4726784 | tf_op jit(solution)/shard_map/pallas_call | solution.py:756
  367.6 3.7 fusion.40
  372.3 26.6 %fusion.76 = f32[1024,4352]{1,0:T(8,128)} fusion(bf16[1024,2048]{1,0:T(8,128)(2,1)} %get-tuple-element.27, bf16[2048,4352]{0,1:T(8,128)(2,1)} %all-gather.8.cloned.1.call-done), kind=kOutput, calls=%fused_computation.193 | convolution fusion | flops 18253611008 | bytes 39845888 | tf_op jit(solution)/shard_map/dot_general | solution.py:781
  399.0 22.3 %multiply_convert_fusion.1 = (bf16[1024,2112]{1,0:T(8,128)(2,1)}, bf16[1024,2112]{1,0:T(8,128)(2,1)}, f32[1024]{0:T(1024)S(1)}, f32[1024]{0:T(1024)S(1)}, bf16[1024,2112]{1,0:T(8,128)(2,1)}) fusion(f32[1024,4352]{1,0:T(8,128)} %fusion.76, f32[1024]{0:T(1024)S(1)} %bitcast.179, f32[1024]{0:T(1024)S(1)} %mul.213, pred[2112]{0:T(1024)(128)(4,1)S(1)} %copy-done.39, ...), kind=kOutput, calls=%fused_computation.17 | convolution fusion | flops 8910272512 | bytes 43141184 | tf_op jit(solution)/shard_map/dot_general | solution.py:785
  421.6 26.1 %convolution_convert_fusion.2 = bf16[1024,2048]{1,0:T(8,128)(2,1)S(1)} fusion(bf16[2048,4352]{0,1:T(8,128)(2,1)} %all-gather.8.cloned.1.call-done, bf16[1024,2112]{1,0:T(8,128)(2,1)} %get-tuple-element.126, bf16[1024,2112]{1,0:T(8,128)(2,1)} %get-tuple-element.125), kind=kOutput, calls=%fused_computation.36 | convolution fusion | flops 18291359744 | bytes 30670848 | tf_op jit(solution)/shard_map/dot_general | solution.py:785
  450.0 87.8 %shard_map.249 = (f32[128,2048]{1,0:T(8,128)}, bf16[1024,2048]{1,0:T(8,128)(2,1)}, bf16[128,128]{1,0:T(8,128)(2,1)}, f32[1,2048]{1,0:T(1,128)}) custom-call(bf16[1024,2176]{1,0:T(8,128)(2,1)} %fusion.9.part, f32[128,2048]{1,0:T(8,128)} %get-tuple-element.30.middle, f32[1,2048]{1,0:T(1,128)} %get-tuple-element.133.gain, ...), custom_call_target="tpu_custom_call" | custom-call | flops 74999996416 | bytes 6660096 | tf_op jit(solution)/shard_map/pallas_call | solution.py:756
  537.8 3.6 convolution_convert_fusion.9
  541.5 6.1 convolution_bitcast_fusion
  547.7 4.4 multiply_reduce_fusion
  553.4 2.9 multiply_convert_fusion.3
  564.7 7.9 convolution_convert_fusion.5.part
  572.6 45.8 %shard_map.250 = (bf16[128,2048]{1,0:T(8,128)(2,1)}, f32[1,2048]{1,0:T(1,128)}) custom-call(bf16[1024,2048]{1,0:T(8,128)(2,1)} %convolution_convert_fusion.5.part, bf16[128,2048]{1,0:T(8,128)(2,1)} %hidden.3, f32[1,2048]{1,0:T(1,128)} %get-tuple-element.132.gain, f32[128,2048]{1,0:T(8,128)} %get-tuple-element.32.grad_middle), custom_call_target="tpu_custom_call" | custom-call | flops 40000000000 | bytes 5775360 | tf_op jit(solution)/shard_map/pallas_call | solution.py:756
  619.2 7.9 convolution_convert_fusion.6
  628.5 3.9 pad_maximum_fusion
  632.4 27.1 %convolution_convert_fusion = bf16[2048,4352]{1,0:T(8,128)(2,1)} fusion(bf16[1024,2048]{1,0:T(8,128)(2,1)} %get-tuple-element.27, bf16[1024,2112]{1,0:T(8,128)(2,1)} %get-tuple-element.126, bf16[1024,2112]{1,0:T(8,128)(2,1)} %get-tuple-element.125), kind=kOutput, calls=%fused_computation | convolution fusion | flops 18298175488 | bytes 30670848 | tf_op jit(solution)/shard_map/dot_general | solution.py:791
  660.3 15.6 %convolution_convert_fusion.1 = bf16[2112,2048]{1,0:T(8,128)(2,1)} fusion(bf16[1024,2048]{1,0:T(8,128)(2,1)} %copy-done.6, bf16[1024,2112]{1,0:T(8,128)(2,1)} %get-tuple-element.129, f32[1024]{0:T(1024)S(1)} %bitcast.180, f32[1024]{0:T(1024)S(1)} %copy-done.36, pred[2112]{0:T(1024)(128)(4,1)S(1)} %copy-done.40), kind=kOutput, calls=%fused_computation.7 | convolution fusion | flops 8871346176 | bytes 17180736 | tf_op jit(solution)/shard_map/dot_general | solution.py:791
  677.4 10.4 %reduce-scatter.4.cloned.1.call-done = bf16[512,1152]{0,1:T(8,128)(2,1)} async-done(((bf16[2048,1152]{0,1:T(8,128)(2,1)}), bf16[512,1152]{0,1:T(8,128)(2,1)}) %reduce-scatter.4.cloned.1.call-update) | async-done | bytes 1179664 | tf_op jit(solution)/shard_map/reduce_scatter | solution.py:1133
  690.3 4.6 all-to-all-start.1
  694.9 15.9 %convolution_convert_fusion.3.part = bf16[1024,2048]{1,0:T(8,128)(2,1)} fusion(bf16[2112,2048]{1,0:T(8,128)(2,1)} %all-gather.4.cloned.1.call-done, bf16[1024,2112]{1,0:T(8,128)(2,1)} %get-tuple-element.129, f32[1024]{0:T(1024)S(1)} %bitcast.181, f32[1024]{0:T(1024)S(1)} %copy-done.36, pred[2112]{0:T(1024)(128)(4,1)S(1)} %copy-done.40), kind=kOutput, calls=%fused_computation.37 | convolution fusion | flops 8869117952 | bytes 17180736 | tf_op jit(solution)/shard_map/dot_general | solution.py:781
  710.8 142.4 %reduce-scatter.6.cloned.1.call-done = bf16[512,4352]{1,0:T(8,128)(2,1)} async-done(((bf16[2048,4352]{1,0:T(8,128)(2,1)}), bf16[512,4352]{1,0:T(8,128)(2,1)}) %reduce-scatter.6.cloned.1.call-update) | async-done | bytes 4456464 | tf_op jit(solution)/shard_map/reduce_scatter | solution.py:1006
  853.2 6.5 copy.286
  859.7 2.5 slice.229
  865.5 3.3 copy.273
  868.8 3.2 reshape.477
  872.0 4.7 all-to-all-start.2
  876.6 65.6 %shard_map.248 = bf16[128,2048]{1,0:T(8,128)(2,1)} custom-call(bf16[1024,2048]{1,0:T(8,128)(2,1)} %convolution_convert_fusion.3.part, f32[128,2048]{1,0:T(8,128)} %get-tuple-element.30.middle, f32[128,1]{1,0:T(8,128)} %copy.255.valid), custom_call_target="tpu_custom_call" | custom-call | flops 40000000000 | bytes 5243392 | tf_op jit(solution)/shard_map/pallas_call | solution.py:756
  946.8 2.4 copy.270
  953.2 2.5 slice.231
  960.0 3.6 copy.276
  963.6 8.4 reshape.485
  972.0 6.6 copy.274
  978.6 5.5 reshape.483
  (256 shorter events, 77.4 us)
Async XLA Ops:
  7.2 96.0 %all-gather.4.cloned.1.call-start = ((), (), s32[]{:S(2)}) async-start(), calls=%async_computation.6 | async-start | bytes 10813440 | tf_op jit(solution)/shard_map/all_gather | solution.py:861
  15.6 4.8 copy-start.45
  15.6 5.0 copy-start.42
  15.6 5.0 copy-start.46
  15.6 5.1 copy-start.47
  26.6 6.5 copy-start.25
  26.6 61.1 %all-to-all-start = ((bf16[8,64,2304]{2,1,0:T(8,128)(2,1)}), bf16[8,64,2304]{2,1,0:T(8,128)(2,1)S(1)}, u32[]{:S(2)}, u32[]{:S(2)}) async-start(bf16[8,64,2304]{2,1,0:T(8,128)(2,1)} %pad_maximum_fusion.2), calls=%async_computation | async-start | bytes 4718592 | tf_op jit(solution)/shard_map/all_to_all | solution.py:881
  33.0 128.9 %all-gather.6.cloned.1.call-start = ((), (), s32[]{:S(2)}) async-start(), calls=%async_computation.7 | async-start | bytes 5898240 | tf_op jit(solution)/shard_map/all_gather | solution.py:888
  87.7 15.5 %copy-start.4 = (bf16[8,64,2304]{2,1,0:T(8,128)(2,1)}, bf16[8,64,2304]{2,1,0:T(8,128)(2,1)S(1)}, u32[]{:S(2)}) copy-start(bf16[8,64,2304]{2,1,0:T(8,128)(2,1)S(1)} %all-to-all-done) | copy-start | bytes 7077892
  103.2 269.1 %all-gather.8.cloned.1.call-start = ((), (), s32[]{:S(2)}) async-start(), calls=%async_computation.8 | async-start | bytes 22282240 | tf_op jit(solution)/shard_map/all_gather | solution.py:903
  113.5 48.6 %copy-start.43 = (s32[128,4]{0,1:T(4,128)S(1)}, s32[128,4]{0,1:T(4,128)}, u32[]{:S(2)}) copy-start(s32[128,4]{0,1:T(4,128)} %param.18) | copy-start | bytes 6148
  115.9 46.3 %copy-start.48 = (s32[1,5]{1,0:T(1,128)S(1)}, s32[1,5]{1,0:T(1,128)}, u32[]{:S(2)}) copy-start(s32[1,5]{1,0:T(1,128)} %param.17) | copy-start | bytes 64
  115.9 48.4 %copy-start.23 = (bf16[128,2048]{1,0:T(8,128)(2,1)S(1)}, bf16[128,2048]{1,0:T(8,128)(2,1)}, u32[]{:S(2)}) copy-start(bf16[128,2048]{1,0:T(8,128)(2,1)} %param.16) | copy-start | bytes 1572868
  115.9 48.4 %copy-start.24 = (bf16[128,2048]{1,0:T(8,128)(2,1)S(1)}, bf16[128,2048]{1,0:T(8,128)(2,1)}, u32[]{:S(2)}) copy-start(bf16[128,2048]{1,0:T(8,128)(2,1)} %hidden.3) | copy-start | bytes 1572868
  162.0 525.8 %reduce-scatter.4.cloned.1.call-start = ((), (), s32[]{:S(2)}) async-start(), calls=%async_computation.9 | async-start | bytes 5898240 | tf_op jit(solution)/shard_map/reduce_scatter | solution.py:1133
  245.5 12.6 %slice-start.4 = ((s8[4718592]{0:T(1024)(128)(4,1)}), s8[4194304]{0:T(1024)(128)(4,1)S(1)}, s32[]{:S(2)}) async-start(s8[4718592]{0:T(1024)(128)(4,1)} %bitcast.166), calls=%async_computation.16 | async-start | bytes 8388608
  249.9 4.9 copy-start.29
  249.9 8.2 slice-start.5
  254.8 4.5 slice-start.6
  254.8 9.2 copy-start.37
  258.1 20.0 %copy-start.1 = (pred[1024,1024]{0,1:T(8,128)(4,1)}, pred[1024,1024]{0,1:T(8,128)(4,1)S(1)}, u32[]{:S(2)}) copy-start(pred[1024,1024]{0,1:T(8,128)(4,1)S(1)} %compare_and_fusion) | copy-start | bytes 3145732
  260.4 21.2 %collective-permute-start = (bf16[2,64,2048]{2,1,0:T(8,128)(2,1)S(1)}, bf16[2,64,2048]{2,1,0:T(8,128)(2,1)S(1)}, u32[]{:S(2)}, u32[]{:S(2)}) collective-permute-start(bf16[2,64,2048]{2,1,0:T(8,128)(2,1)S(1)} %constant_dynamic-slice_fusion.1), channel_id=1, source_target_pairs={{0,1},{1,0},{2,3},{3,2},{4,5},{5,4},{6,7},{7,6},{8,9},{9,8},{10,11... | collective-permute-start | bytes 1572872 | tf_op jit(solution)/shard_map/ppermute | solution.py:915
  264.1 6.9 copy-start.32
  270.9 7.2 copy-start.5
  281.5 4.5 copy-start.19
  367.6 3.8 copy-start.41
  371.4 27.6 %copy-start.30 = (f32[1024,1]{0,1:T(1,128)}, f32[1024,1]{0,1:T(1,128)S(1)}, u32[]{:S(2)}) copy-start(f32[1024,1]{0,1:T(1,128)S(1)} %fusion.57) | copy-start | bytes 12292
  371.7 27.3 %copy-start.35 = (f32[1024]{0:T(1024)}, f32[1024]{0:T(1024)S(1)}, u32[]{:S(2)}) copy-start(f32[1024]{0:T(1024)S(1)} %mul.213) | copy-start | bytes 12292
  372.3 26.6 %copy-start.39 = (pred[2112]{0:T(1024)(128)(4,1)S(1)}, pred[2112]{0:T(1024)(128)(4,1)}, u32[]{:S(2)}) copy-start(pred[2112]{0:T(1024)(128)(4,1)} %fusion.47) | copy-start | bytes 6340
  372.3 26.6 %copy-start.7 = (bf16[1024,2048]{1,0:T(8,128)(2,1)S(1)}, bf16[1024,2048]{1,0:T(8,128)(2,1)}, u32[]{:S(2)}) copy-start(bf16[1024,2048]{1,0:T(8,128)(2,1)} %copy-done.6) | copy-start | bytes 12582916
  450.0 87.8 %copy-start.10 = (bf16[2,2,64,2048]{3,2,1,0:T(8,128)(2,1)S(1)}, bf16[2,2,64,2048]{3,2,1,0:T(8,128)(2,1)}, u32[]{:S(2)}) copy-start(bf16[2,2,64,2048]{3,2,1,0:T(8,128)(2,1)} %copy-done.9) | copy-start | bytes 3145732
  537.8 3.7 copy-start.2
  537.8 9.8 slice-start
  541.5 6.2 slice-start.1
  547.6 4.4 copy-start.20
  547.7 4.4 copy-start.49
  559.8 67.3 %collective-permute-start.1 = (bf16[2,64,2048]{2,1,0:T(8,128)(2,1)}, bf16[2,64,2048]{2,1,0:T(8,128)(2,1)S(1)}, u32[]{:S(2)}, u32[]{:S(2)}) collective-permute-start(bf16[2,64,2048]{2,1,0:T(8,128)(2,1)} %select_bitcast_fusion), channel_id=1, source_target_pairs={{0,1},{1,0},{2,3},{3,2},{4,5},{5,4},{6,7},{7,6},{8,9},{9,8},{10,11... | collective-permute-start | bytes 1572872 | tf_op jit(solution)/shard_map/ppermute | solution.py:1118
  572.6 45.8 %copy-start.34 = (f32[1,2048]{1,0:T(1,128)S(1)}, f32[1,2048]{1,0:T(1,128)}, u32[]{:S(2)}) copy-start(f32[1,2048]{1,0:T(1,128)} %get-tuple-element.35) | copy-start | bytes 24580
  572.6 46.7 %copy-start.33 = (f32[2048,1]{0,1:T(1,128)S(1)}, f32[2048,1]{0,1:T(1,128)}, u32[]{:S(2)}) copy-start(f32[2048,1]{0,1:T(1,128)} %copy-done.32) | copy-start | bytes 24580
  572.6 46.7 %copy-start.38 = (f32[1024]{0:T(1024)S(1)}, f32[1024]{0:T(1024)}, u32[]{:S(2)}) copy-start(f32[1024]{0:T(1024)} %copy-done.37) | copy-start | bytes 12292
  632.4 220.8 %reduce-scatter.6.cloned.1.call-start = ((), (), s32[]{:S(2)}) async-start(), calls=%async_computation.10 | async-start | bytes 22282240 | tf_op jit(solution)/shard_map/reduce_scatter | solution.py:1006
  659.6 293.6 %reduce-scatter.8.cloned.1.call-start = ((), (), s32[]{:S(2)}) async-start(), calls=%async_computation.11 | async-start | bytes 10813440 | tf_op jit(solution)/shard_map/reduce_scatter | solution.py:986
  690.3 181.6 %all-to-all-start.1 = ((bf16[8,64,896]{2,1,0:T(8,128)(2,1)}), bf16[8,64,896]{2,1,0:T(8,128)(2,1)S(1)}, u32[]{:S(2)}, u32[]{:S(2)}) async-start(bf16[8,64,896]{2,1,0:T(8,128)(2,1)} %bitcast.47), calls=%async_computation.2 | async-start | bytes 1835008 | tf_op jit(solution)/shard_map/all_to_all | solution.py:1142
  872.0 91.6 %all-to-all-start.2 = ((bf16[8,64,1408]{2,1,0:T(8,128)(2,1)}), bf16[8,64,1408]{2,1,0:T(8,128)(2,1)}, u32[]{:S(2)}, u32[]{:S(2)}) async-start(bf16[8,64,1408]{2,1,0:T(8,128)(2,1)} %reshape.477), calls=%async_computation.4 | async-start | bytes 2883584 | tf_op jit(solution)/shard_map/all_to_all | solution.py:1014
  953.2 6.5 slice-start.2
  955.7 4.0 slice-start.3
  978.6 5.6 copy-start.22
  978.6 6.3 copy-start.21
  (20 other events, 40.4 us)
Sparse Core Ops, SparseCore 0:
  10.7 92.4 all-gather.3
  105.0 56.9 all-gather.5
  164.4 167.1 all-gather.7
  632.5 55.2 reduce-scatter.3
  690.8 162.3 reduce-scatter.5
  856.5 88.5 reduce-scatter.7

commit v3 on v2

--- a/solution.py
+++ b/solution.py
@@ -422,129 +422,216 @@
 
 
 class Line:
-    def __init__(self, chips):
+    def __init__(self, chips, wide):
         me = lax.axis_index("expert")
+        group = lax.axis_index("dp")
         self.chips = chips
+        self.wide = wide
         self.z = me // 2
         self.core = lax.rem(me, 2)
+        self.x = lax.rem(group, 2)
+        self.group = group
         self.below = self.z > 0
         self.above = self.z < chips - 1
 
     def at(self, z, core):
         return {"expert": 2 * z + core}
 
+    def beside(self):
+        return {"dp": self.group + 1 - 2 * self.x, "expert": 2 * self.z + self.core}
+
     def meet(self):
         barrier = pltpu.get_barrier_semaphore()
 
-        def hello(z, core):
-            pl.semaphore_signal(
-                barrier, inc=1, device_id=self.at(z, core), device_id_type=MESH_IDS
-            )
-
-        hello(self.z, 1 - self.core)
-        pl.when(self.above)(lambda: hello(self.z + 1, self.core))
-        pl.when(self.below)(lambda: hello(self.z - 1, self.core))
+        def hello(target):
+            pl.semaphore_signal(barrier, inc=1, device_id=target, device_id_type=MESH_IDS)
+
+        hello(self.at(self.z, 1 - self.core))
+        pl.when(self.above)(lambda: hello(self.at(self.z + 1, self.core)))
+        pl.when(self.below)(lambda: hello(self.at(self.z - 1, self.core)))
+        if self.wide:
+            hello(self.beside())
         peers = 1 + jnp.minimum(self.z, 1) + jnp.minimum(self.chips - 1 - self.z, 1)
-        pl.semaphore_wait(barrier, peers)
-
-
-def gather_scratch(chips):
+        pl.semaphore_wait(barrier, peers + (1 if self.wide else 0))
+
+
+def gather_scratch(chips, wide):
+    items = 2 * chips - 1
+    pair = [pltpu.SemaphoreType.DMA((items,)) for _ in range(6 if wide else 2)]
     return [
         pltpu.SemaphoreType.DMA((2, chips - 1)),
         pltpu.SemaphoreType.DMA((2, chips - 1)),
-        pltpu.SemaphoreType.DMA((2 * chips - 1,)),
-        pltpu.SemaphoreType.DMA((2 * chips - 1,)),
         pltpu.SemaphoreType.DMA,
-    ]
-
-
-def gather_line(line, own, out, send, recv, pair_send, pair_recv, local):
-    chips, z, core = line.chips, line.z, line.core
-    rows = own.shape[0]
-
-    def block(chip, which):
-        return out.at[pl.ds((2 * chip + which) * rows, rows)]
-
-    def hop(step, up):
-        origin = z - step if up else z + step
+    ] + pair
+
+
+class Gather:
+    def __init__(self, line, own, out, scratch):
+        self.line, self.own, self.out = line, own, out
+        self.send, self.recv, self.local = scratch[:3]
+        self.pair = scratch[3:]
+        self.wide = len(self.pair) == 6
+        self.rows = own.shape[0]
+
+    def block(self, group, chip, which):
+        place = 2 * chip + which
+        if self.wide:
+            place = place + group * (2 * self.line.chips)
+        return self.out.at[pl.ds(place * self.rows, self.rows)]
+
+    def mine(self, chip, which):
+        return self.block(self.line.x, chip, which)
+
+    def theirs(self, chip, which):
+        return self.block(1 - self.line.x, chip, which)
+
+    def origin(self, step, up):
+        return self.line.z - step if up else self.line.z + step
+
+    def hop(self, step, up):
+        z, core = self.line.z, self.line.core
+        origin = self.origin(step, up)
         return pltpu.make_async_remote_copy(
-            src_ref=own if step == 0 else block(origin, core),
-            dst_ref=block(origin, core),
-            send_sem=send.at[0 if up else 1, step],
-            recv_sem=recv.at[0 if up else 1, step],
-            device_id=line.at(z + 1 if up else z - 1, core),
+            src_ref=self.own if step == 0 else self.mine(origin, core),
+            dst_ref=self.mine(origin, core),
+            send_sem=self.send.at[0 if up else 1, step],
+            recv_sem=self.recv.at[0 if up else 1, step],
+            device_id=self.line.at(z + 1 if up else z - 1, core),
             device_id_type=MESH_IDS,
         )
 
-    def arrival(step, up):
-        origin = z - 1 - step if up else z + 1 + step
+    def arrival(self, step, up):
+        z, core = self.line.z, self.line.core
         return pltpu.make_async_remote_copy(
-            src_ref=own,
-            dst_ref=block(origin, core),
-            send_sem=send.at[0 if up else 1, step],
-            recv_sem=recv.at[0 if up else 1, step],
-            device_id=line.at(z - 1 if up else z + 1, core),
+            src_ref=self.own,
+            dst_ref=self.mine(self.origin(step + 1, up), core),
+            send_sem=self.send.at[0 if up else 1, step],
+            recv_sem=self.recv.at[0 if up else 1, step],
+            device_id=self.line.at(z - 1 if up else z + 1, core),
             device_id_type=MESH_IDS,
         )
 
-    def across(index, origin, source, which):
+    def across(self, index, source, target, kind):
+        line = self.line
         return pltpu.make_async_remote_copy(
             src_ref=source,
-            dst_ref=block(origin, which),
-            send_sem=pair_send.at[index],
-            recv_sem=pair_recv.at[index],
-            device_id=line.at(z, 1 - core),
+            dst_ref=target,
+            send_sem=self.pair[2 * kind].at[index],
+            recv_sem=self.pair[2 * kind + 1].at[index],
+            device_id=line.beside() if kind == 1 else line.at(line.z, 1 - line.core),
             device_id_type=MESH_IDS,
         )
 
-    def sends(step, up):
-        return (z >= step) & line.above if up else (z + step <= chips - 1) & line.below
-
-    def comes(step, up):
-        return z - 1 - step >= 0 if up else z + 1 + step <= chips - 1
-
-    def pair_of(step, up):
-        return 1 + step + (0 if up else chips - 1)
-
-    keep = pltpu.make_async_copy(own, block(z, core), local)
-    keep.start()
+    def sends(self, step, up):
+        line = self.line
+        if up:
+            return (line.z >= step) & line.above
+        return (line.z + step <= line.chips - 1) & line.below
+
+    def items(self):
+        line = self.line
+        found = [(0, line.z, None)]
+        for step in range(line.chips - 1):
+            found.append((1 + step, line.z - 1 - step, line.z - 1 - step >= 0))
+            found.append(
+                (line.chips + step, line.z + 1 + step, line.z + 1 + step <= line.chips - 1)
+            )
+        return found
+
+    def spread(self, index, origin, source):
+        core = self.line.core
+        self.across(index, source, self.mine(origin, core), 0).start()
+        if self.wide:
+            self.across(index, source, self.mine(origin, core), 1).start()
+
+    def begin(self):
+        line = self.line
+        pltpu.make_async_copy(self.own, self.mine(line.z, line.core), self.local).start()
+
+    def push(self, step):
+        line = self.line
+        for up in (True, False):
+            pl.when(self.sends(step, up))(lambda up=up: self.hop(step, up).start())
+        if step == 0:
+            self.spread(0, line.z, self.own)
+
+    def pull(self, step):
+        for index, origin, comes in self.items():
+            if index not in (1 + step, self.line.chips + step):
+                continue
+
+            def take(index=index, origin=origin):
+                self.arrival(step, index < self.line.chips).wait_recv()
+                self.spread(index, origin, self.mine(origin, self.line.core))
+
+            pl.when(comes)(take)
+
+    def end(self):
+        line, core = self.line, self.line.core
+
+        def each(act):
+            for index, origin, comes in self.items():
+                if comes is None:
+                    act(index, origin)
+                else:
+                    pl.when(comes)(lambda index=index, origin=origin: act(index, origin))
+
+        def turn(index, origin):
+            landed = self.theirs(origin, core)
+            self.across(index, landed, landed, 1).wait_recv()
+            self.across(index, landed, landed, 2).start()
+
+        def settle(index, origin):
+            here = self.mine(origin, core)
+            self.across(index, here, here, 0).wait_send()
+            self.across(index, here, self.mine(origin, 1 - core), 0).wait_recv()
+            if self.wide:
+                there = self.theirs(origin, core)
+                self.across(index, here, here, 1).wait_send()
+                self.across(index, there, there, 2).wait_send()
+                self.across(index, there, self.theirs(origin, 1 - core), 2).wait_recv()
+
+        if self.wide:
+            each(turn)
+        each(settle)
+        for step in range(line.chips - 1):
+            for up in (True, False):
+                pl.when(self.sends(step, up))(
+                    lambda step=step, up=up: self.hop(step, up).wait_send()
+                )
+        pltpu.make_async_copy(self.own, self.mine(line.z, core), self.local).wait()
+
+
+def gather_lines(*gathers):
+    chips = gathers[0].line.chips
+    for one in gathers:
+        one.begin()
     for step in range(chips - 1):
-        for up in (True, False):
-            pl.when(sends(step, up))(lambda step=step, up=up: hop(step, up).start())
-        if step == 0:
-            across(0, z, own, core).start()
-        for up in (True, False):
-
-            def take(step=step, up=up):
-                arrival(step, up).wait_recv()
-                origin = z - 1 - step if up else z + 1 + step
-                across(pair_of(step, up), origin, block(origin, core), core).start()
-
-            pl.when(comes(step, up))(take)
-    across(0, z, own, core).wait_send()
-    across(0, z, own, 1 - core).wait_recv()
-    for step in range(chips - 1):
-        for up in (True, False):
-            pl.when(sends(step, up))(lambda step=step, up=up: hop(step, up).wait_send())
-
-            def settle(step=step, up=up):
-                origin = z - 1 - step if up else z + 1 + step
-                across(pair_of(step, up), origin, block(origin, core), core).wait_send()
-                across(pair_of(step, up), origin, block(origin, core), 1 - core).wait_recv()
-
-            pl.when(comes(step, up))(settle)
-    keep.wait()
-
-
-def scatter_scratch(chips, rows, width):
-    return [
-        pltpu.VMEM((chips, rows, width), jnp.bfloat16),
+        for one in gathers:
+            one.push(step)
+        for one in gathers:
+            one.pull(step)
+    for one in gathers:
+        one.end()
+
+
+def scatter_scratch(chips, rows, width, wide):
+    groups = 2 if wide else 1
+    found = [
+        pltpu.VMEM((groups, chips, rows, width), jnp.bfloat16),
         pltpu.VMEM((2, chips, rows, width), jnp.bfloat16),
-        pltpu.SemaphoreType.DMA((chips,)),
-        pltpu.SemaphoreType.DMA((chips,)),
+        pltpu.SemaphoreType.DMA((groups, chips)),
+        pltpu.SemaphoreType.DMA((groups, chips)),
         pltpu.SemaphoreType.DMA((2, chips)),
         pltpu.SemaphoreType.DMA((2, chips)),
     ]
+    if wide:
+        found += [
+            pltpu.VMEM((chips, rows, width), jnp.bfloat16),
+            pltpu.SemaphoreType.DMA((chips,)),
+            pltpu.SemaphoreType.DMA((chips,)),
+        ]
+    return found
 
 
 def strips(rows, body):
@@ -553,27 +640,44 @@
         body(pl.ds(pl.multiple_of(index * STRIP, STRIP), STRIP))
 
 
-def scatter_line(line, part, total, held, come, pair_send, pair_recv, send, recv):
+def scatter_line(line, part, total, scratch):
     chips, z, core = line.chips, line.z, line.core
     rows = total.shape[0]
-
-    def start_of(chip, which):
-        return (2 * chip + which) * rows
-
-    def across(chip):
+    held, come, pair_send, pair_recv, send, recv = scratch[:6]
+    wide = len(scratch) == 9
+    if wide:
+        aside, side_send, side_recv = scratch[6:]
+
+    def start_of(other, chip, which):
+        place = 2 * chip + which
+        if wide:
+            place = place + (1 - line.x if other else line.x) * (2 * chips)
+        return place * rows
+
+    def across(other, chip):
         return pltpu.make_async_remote_copy(
-            src_ref=part.at[pl.ds(start_of(chip, 1 - core), rows)],
-            dst_ref=held.at[chip],
-            send_sem=pair_send.at[chip],
-            recv_sem=pair_recv.at[chip],
+            src_ref=part.at[pl.ds(start_of(other, chip, 1 - core), rows)],
+            dst_ref=held.at[other, chip],
+            send_sem=pair_send.at[other, chip],
+            recv_sem=pair_recv.at[other, chip],
             device_id=line.at(z, 1 - core),
             device_id_type=MESH_IDS,
         )
 
+    def beside(chip):
+        return pltpu.make_async_remote_copy(
+            src_ref=held.at[1, chip],
+            dst_ref=aside.at[chip],
+            send_sem=side_send.at[chip],
+            recv_sem=side_recv.at[chip],
+            device_id=line.beside(),
+            device_id_type=MESH_IDS,
+        )
+
     def hop(chip, up, target):
         way = 0 if up else 1
         return pltpu.make_async_remote_copy(
-            src_ref=held.at[chip],
+            src_ref=held.at[0, chip],
             dst_ref=come.at[way, chip],
             send_sem=send.at[way, chip],
             recv_sem=recv.at[way, chip],
@@ -581,92 +685,113 @@
             device_id_type=MESH_IDS,
         )
 
-    def value(chip, strip, ways):
-        first = start_of(chip, core)
+    def value(other, chip, strip, ways):
+        first = start_of(other, chip, core)
         mine = part[pl.ds(pl.multiple_of(first + strip.start, STRIP), STRIP), :]
-        summed = mine.astype(jnp.float32) + held[chip, strip, :].astype(jnp.float32)
+        summed = mine.astype(jnp.float32) + held[other, chip, strip, :].astype(jnp.float32)
+        if wide and other == 0:
+            summed = summed + aside[chip, strip, :].astype(jnp.float32)
         for way in ways:
             summed = summed + come[way, chip, strip, :].astype(jnp.float32)
         return summed
 
-    def add(chip, ways):
+    def add(other, chip, ways):
         def body(strip):
-            held[chip, strip, :] = value(chip, strip, ways).astype(jnp.bfloat16)
+            held[other, chip, strip, :] = value(other, chip, strip, ways).astype(jnp.bfloat16)
 
         strips(rows, body)
 
-    order = []
-    for near in range((chips + 1) // 2):
-        for chip in (chips - 1 - near, near):
-            if chip not in order:
-                order.append(chip)
-    for chip in order:
-        across(chip).start()
+    def up_chip(step):
+        return chips - 1 - step + z
+
+    def down_chip(step):
+        return step - (chips - 1 - z)
+
+    def up_sends(step):
+        return (z <= step) & line.above
+
+    def down_sends(step):
+        return (step >= chips - 1 - z) & line.below
+
+    def each(act):
+        for step in range(chips - 1):
+            pl.when(up_sends(step))(lambda step=step: act(up_chip(step), True))
+            pl.when(down_sends(step))(lambda step=step: act(down_chip(step), False))
+
+    if wide:
+        each(lambda chip, up: across(1, chip).start())
+        across(1, z).start()
+    each(lambda chip, up: across(0, chip).start())
+    across(0, z).start()
+
+    def give(chip):
+        across(1, chip).wait_recv()
+        add(1, chip, ())
+        beside(chip).start()
+
+    if wide:
+        each(lambda chip, up: give(chip))
+        give(z)
+
+    def ready(chip):
+        across(0, chip).wait_recv()
+        if wide:
+            beside(chip).wait_recv()
 
     def forward(chip, up):
-        across(chip).wait_recv()
+        ready(chip)
         way = 0 if up else 1
 
         def with_arrival():
             hop(chip, up, z).wait_recv()
-            add(chip, (way,))
+            add(0, chip, (way,))
 
         more = line.below if up else line.above
         pl.when(more)(with_arrival)
-        pl.when(jnp.logical_not(more))(lambda: add(chip, ()))
+        pl.when(jnp.logical_not(more))(lambda: add(0, chip, ()))
         hop(chip, up, z + 1 if up else z - 1).start()
 
-    def up_chip(step):
-        return chips - 1 - step + z
-
-    def down_chip(step):
-        return step - (chips - 1 - z)
-
-    def up_sends(step):
-        return (z <= step) & line.above
-
-    def down_sends(step):
-        return (step >= chips - 1 - z) & line.below
-
-    for step in range(chips - 1):
-        pl.when(up_sends(step))(lambda step=step: forward(up_chip(step), True))
-        pl.when(down_sends(step))(lambda step=step: forward(down_chip(step), False))
-
-    across(z).wait_recv()
+    each(forward)
+    ready(z)
     pl.when(line.below)(lambda: hop(z, True, z).wait_recv())
     pl.when(line.above)(lambda: hop(z, False, z).wait_recv())
 
     def last(ways):
         def body(strip):
-            total[strip, :] = value(z, strip, ways)
+            total[strip, :] = value(0, z, strip, ways)
 
         strips(rows, body)
 
-    inner = line.below & line.above
-    pl.when(inner)(lambda: last((0, 1)))
+    pl.when(line.below & line.above)(lambda: last((0, 1)))
     pl.when(jnp.logical_not(line.below))(lambda: last((1,)))
     pl.when(jnp.logical_not(line.above))(lambda: last((0,)))
-    for chip in order:
-        across(chip).wait_send()
-    for step in range(chips - 1):
-        pl.when(up_sends(step))(
-            lambda step=step: hop(up_chip(step), True, z + 1).wait_send()
-        )
-        pl.when(down_sends(step))(
-            lambda step=step: hop(down_chip(step), False, z - 1).wait_send()
-        )
-
-
-def gather_kernel(chips, own, out, *scratch):
-    line = Line(chips)
+
+    def settle(chip):
+        across(0, chip).wait_send()
+        if wide:
+            across(1, chip).wait_send()
+            beside(chip).wait_send()
+
+    def settle_hop(chip, up):
+        settle(chip)
+        hop(chip, up, z + 1 if up else z - 1).wait_send()
+
+    each(settle_hop)
+    settle(z)
+
+
+def gather_kernel(chips, near, far, near_all, far_all, *scratch):
+    line = Line(chips, True)
     line.meet()
-    gather_line(line, own, out, *scratch)
+    gather_lines(
+        Gather(line, near, near_all, scratch[:5]), Gather(line, far, far_all, scratch[5:])
+    )
 
 
 def middle_kernel(chips, part, hidden, gain, middle, normed_all, total, normed, *scratch):
-    line = Line(chips)
+    line = Line(chips, True)
     line.meet()
-    scatter_line(line, part, total, *scratch[:6])
+    scatter_line(line, part, total, scratch[:6])
 
     def body(strip):
         rows = hidden[strip, :].astype(jnp.float32) + total[strip, :]
@@ -674,16 +799,16 @@
         normed[strip, :] = (rows * rms_scale(rows) * gain[...]).astype(jnp.bfloat16)
 
     strips(hidden.shape[0], body)
-    gather_line(line, normed, normed_all, *scratch[6:])
+    gather_lines(Gather(line, normed, normed_all, scratch[6:]))
 
 
 def branch_kernel(
     chips, part, middle, gain, out_grad, probs, collect, router,
     grad_middle, grad_all, heads, term, total, turned, *scratch
 ):
-    line = Line(chips)
+    line = Line(chips, True)
     line.meet()
-    scatter_line(line, part, total, *scratch[:6])
+    scatter_line(line, part, total, scratch[:9])
     width = middle.shape[1]
     term[...] = jnp.zeros_like(term)
 
@@ -715,13 +840,13 @@
         turned[strip, :] = result.astype(jnp.bfloat16)
 
     strips(middle.shape[0], body)
-    gather_line(line, turned, grad_all, *scratch[6:])
+    gather_lines(Gather(line, turned, grad_all, scratch[9:]))
 
 
 def input_kernel(chips, part, hidden, gain, grad_middle, input_grad, term, total, *scratch):
-    line = Line(chips)
+    line = Line(chips, False)
     line.meet()
-    scatter_line(line, part, total, *scratch)
+    scatter_line(line, part, total, scratch)
     term[...] = jnp.zeros_like(term)
 
     def body(strip):
@@ -740,9 +865,9 @@
 
 
 def output_kernel(chips, part, middle, valid, output, total, *scratch):
-    line = Line(chips)
+    line = Line(chips, True)
     line.meet()
-    scatter_line(line, part, total, *scratch)
+    scatter_line(line, part, total, scratch)
 
     def body(strip):
         rows = valid[strip, :] * (middle[strip, :] + total[strip, :])
@@ -766,7 +891,6 @@
             flops=int(micros * 1e9), bytes_accessed=moved, transcendentals=0
         ),
     )(*inputs)
-
 
 def bf16(values):
     return values.astype(jnp.bfloat16)
@@ -829,10 +953,16 @@
     shared_block = shared_out.shape[0]
     expert_block = expert_out.shape[1]
     pair_block = expert_block + shared_block
-    hidden_units = parts * pair_block
-    padded = -(-hidden_units // 128) * 128
+    hidden_units = half * pair_block
     own_shared = parts * shared_block
     chips = places
+    data = lax.axis_index("dp")
+    side_by = data % 2
+    above = data // 2
+    slots = 2 * size
+    slot = side_by * size + me
+    swap_side = [(g, g ^ 1) for g in range(parts)]
+    swap_above = [(g, g ^ 2) for g in range(parts)]
     own_qkv = 3 * own_heads * HD
 
     def by_head(columns):
@@ -845,22 +975,13 @@
         cut = pieces.reshape(places, 2, count, 3, half, HD)
         return cut.transpose(2, 3, 1, 4, 0, 5).reshape(count, 3 * width)
 
-    side = jnp.pad(bf16(routes), ((0, 0), (0, extra - top)))
-    (gathered,) = remote_call(
-        gather_kernel,
-        chips,
-        [jnp.concatenate([hidden_in, out_grad, side], axis=1)],
-        [((group, 2 * width + extra), jnp.bfloat16, True)],
-        gather_scratch(chips),
-        0,
-        70,
-    )
-    hidden_all = gathered[:, :width].astype(jnp.float32)
-    routes_all = gathered[:, 2 * width : 2 * width + top].astype(jnp.int32)
-
-    weight_down = lax.all_gather(
-        jnp.concatenate([expert_out[0], shared_out], axis=0), "dp", axis=0, tiled=True
-    )
+    def ordered(which, own, other, axis):
+        first = jnp.where(which == 0, own, other)
+        second = jnp.where(which == 0, other, own)
+        return jnp.concatenate([first, second], axis=axis)
+
+    def rows_of(values, first):
+        return lax.dynamic_slice_in_dim(values, first * rows, rows, 0)
 
     small = jnp.concatenate(
         [
@@ -873,19 +994,67 @@
         axis=1,
     )
     small = jnp.pad(small, ((0, 0), (0, extra - small.shape[1])))
+    first = jnp.concatenate(
+        [by_head(qkv_weight), jnp.broadcast_to(small[None], (size, block, extra))], axis=2
+    )
+    first = lax.all_to_all(first, "expert", split_axis=0, concat_axis=0, tiled=True)
+    first = first.reshape(size * block, own_qkv + extra)
+    out_cols = width * block // (size * block)
+    qkv_full = lax.all_gather(
+        jnp.concatenate([first, out_weight.reshape(size * block, out_cols)], axis=1),
+        "dp",
+        axis=0,
+        tiled=True,
+    )
+
+    down = jnp.concatenate([expert_out[0], shared_out], axis=0)
+    down_came = lax.ppermute(down, "dp", swap_above)
+
+    def units(values, count):
+        cut = values.reshape(size * block, 2, half, 2, count)
+        return cut.transpose(3, 1, 2, 4, 0).reshape(2, 2 * half * count, size * block)
+
+    def aside(values):
+        kept = lax.dynamic_index_in_dim(values, side_by, 0, keepdims=False)
+        given = lax.dynamic_index_in_dim(values, 1 - side_by, 0, keepdims=False)
+        return kept, lax.ppermute(given, "dp", swap_side)
+
+    routed_kept, routed_came = aside(units(expert_in[0], expert_block))
+
+    segment, position = segment_table(lengths[0], group)
+    valid_all = (segment < lengths.shape[1] - 1).astype(jnp.float32)[:, None]
+    valid_rows = rows_of(valid_all, me)
+    grad_own = bf16(out_grad.astype(jnp.float32) * valid_rows)
+    side = jnp.pad(bf16(routes), ((0, 0), (0, extra - top)))
+    far = jnp.concatenate([grad_own, side], axis=1)
+    far, first = lax.optimization_barrier((far, first))
+    hidden_all, far_all = remote_call(
+        gather_kernel,
+        chips,
+        [hidden_in, far],
+        [
+            ((group, width), jnp.bfloat16, True),
+            ((2 * group, width + extra), jnp.bfloat16, True),
+        ],
+        gather_scratch(chips, False) + gather_scratch(chips, True),
+        0,
+        75,
+    )
+    hidden_all, far_all, routed_came, down_came = lax.optimization_barrier(
+        (hidden_all, far_all, routed_came, down_came)
+    )
+    weight_down = ordered(above, down, down_came, 0)
+    routed_up = ordered(side_by, routed_kept, routed_came, 1)
+    routed_came = lax.ppermute(routed_up, "dp", swap_above)
+
     cut = shared_in.reshape(block, 2, parts, size, shared_block)
     cut = cut.transpose(3, 0, 1, 2, 4).reshape(size, block, 2 * own_shared)
-    sent = jnp.concatenate(
-        [by_head(qkv_weight), jnp.broadcast_to(small[None], (size, block, extra)), cut], axis=2
-    )
-    sent = lax.all_to_all(sent, "expert", split_axis=0, concat_axis=0, tiled=True)
-    sent = sent.reshape(size * block, own_qkv + extra + 2 * own_shared)
-    out_cols = width * block // (size * block)
-    first = jnp.concatenate(
-        [sent[:, : own_qkv + extra], out_weight.reshape(size * block, out_cols)], axis=1
-    )
-    first, weight_down = lax.optimization_barrier((first, weight_down))
-    qkv_full = lax.all_gather(first, "dp", axis=0, tiled=True)
+    cut, hidden_all = lax.optimization_barrier((cut, hidden_all))
+    cut = lax.all_to_all(cut, "expert", split_axis=0, concat_axis=0, tiled=True)
+    hidden_all = hidden_all.astype(jnp.float32)
+    grad_rows = far_all[:, :width]
+    routes_all = far_all[:, width : width + top].astype(jnp.int32)
+
     weight_qkv = qkv_full[:, :own_qkv]
     small = qkv_full[:, own_qkv : own_qkv + extra]
     gain_one = small[:, 0].astype(jnp.float32)
@@ -894,14 +1063,6 @@
     bias_all = by_head(small[:, 3 + experts : 3 + experts + bias_cols].reshape(1, 3 * width))
     bias_own = lax.dynamic_index_in_dim(bias_all, me, 0, keepdims=False).astype(jnp.float32)
 
-    cut = sent[:, own_qkv + extra :].reshape(size * block, 2, parts, shared_block)
-    up = expert_in[0].reshape(size * block, 2, parts, expert_block)
-    up = jnp.concatenate([up, cut], axis=3).reshape(size * block, 2, hidden_units)
-    up = jnp.pad(up, ((0, 0), (0, 0), (0, padded - hidden_units)))
-    up = up.reshape(size * block, 2 * padded)
-    up, qkv_full = lax.optimization_barrier((up, qkv_full))
-    weight_up = lax.all_gather(up, "dp", axis=0, tiled=True)
-
     swap = [(i, i ^ 1) for i in range(size)]
 
     def own_half(values):
@@ -917,8 +1078,6 @@
         [jnp.where(core == 0, kept, came), jnp.where(core == 0, came, kept)], axis=1
     ).reshape(own_heads * HD, width)
 
-    segment, position = segment_table(lengths[0], group)
-    valid_all = (segment < lengths.shape[1] - 1).astype(jnp.float32)[:, None]
     cosine, sine = rotary_tables(position, HD)
     allowed = (
         (segment[:, None] == segment[None, :]) & (position[:, None] >= position[None, :])
@@ -946,17 +1105,30 @@
             "hqk,khd->qhd", weights_low, value_low, preferred_element_type=jnp.float32
         ).reshape(group, own_heads * HD)
     )
+    part, routed_came = lax.optimization_barrier((bf16(mm(attended, weight_out)), routed_came))
+    shared_kept, shared_came = aside(units(cut.reshape(size * block, 2 * own_shared), shared_block))
+    shared_up = ordered(side_by, shared_kept, shared_came, 1)
+    shared_came = lax.ppermute(shared_up, "dp", swap_above)
     middle, normed_all = remote_call(
         middle_kernel,
         chips,
-        [bf16(mm(attended, weight_out)), hidden_in, gain_two[None, :]],
-        [((rows, width), jnp.float32, False), ((group, width), jnp.bfloat16, True)],
+        [part, hidden_in, gain_two[None, :]],
+        [((rows, width), jnp.float32, False), ((2 * group, width), jnp.bfloat16, True)],
         [pltpu.VMEM((rows, width), jnp.float32), pltpu.VMEM((rows, width), jnp.bfloat16)]
-        + scatter_scratch(chips, rows, width)
-        + gather_scratch(chips),
+        + scatter_scratch(chips, rows, width, False)
+        + gather_scratch(chips, True),
         1,
-        70,
-    )
+        85,
+    )
+
+    normed_all, shared_came = lax.optimization_barrier((normed_all, shared_came))
+    weight_up = jnp.concatenate(
+        [
+            ordered(above, routed_up, routed_came, 1).reshape(2, half, expert_block, width),
+            ordered(above, shared_up, shared_came, 1).reshape(2, half, shared_block, width),
+        ],
+        axis=2,
+    ).reshape(2 * hidden_units, width)
 
     gate_logits = mm_nt(normed_all, router_rows)
     logits = gate_logits[:, 1 : 1 + experts]
@@ -971,87 +1143,67 @@
     named = jnp.sum((routes_all == me).astype(jnp.float32), axis=1, keepdims=True)
     gate_own = named * jnp.sum(jnp.where(mine, probs_all, 0.0), axis=1, keepdims=True)
 
-    routed_unit = (jnp.arange(hidden_units, dtype=jnp.int32) % pair_block < expert_block)[None, :]
-    unit_scale = jnp.where(routed_unit, gate_own, opener_all)
-    grad_rows = bf16(
-        gathered[:, width : 2 * width].astype(jnp.float32) * valid_all
-    )
-    both_up = mm(normed_all, weight_up)
-
-    gate_part = both_up[:, :hidden_units]
-    up_part = both_up[:, padded : padded + hidden_units]
+    routed_unit = (jnp.arange(hidden_units, dtype=jnp.int32) % pair_block < expert_block)[:, None]
+    unit_scale = jnp.where(routed_unit, gate_own.T, opener_all.T)
+    both_up = mm_nt(weight_up, normed_all)
+    gate_part = both_up[:hidden_units]
+    up_part = both_up[hidden_units:]
     hidden = bf16(jax.nn.silu(gate_part) * up_part)
     scaled_hidden = bf16(unit_scale * hidden.astype(jnp.float32))
-    term_down = bf16(mm_tn(scaled_hidden, grad_rows))
-    grad_down = lax.psum_scatter(term_down, "dp", scatter_dimension=0, tiled=True).astype(
-        jnp.float32
-    )
-    grad_shared_out = grad_down[expert_block:]
-    grad_expert_out = grad_down[None, :expert_block]
-    combined = bf16(mm(scaled_hidden, weight_down))
-
-    grad_hidden = mm_nt(grad_rows, weight_down)
+
+    def half_rows(values, which):
+        return lax.dynamic_slice_in_dim(values, which * pair_block, pair_block, 0)
+
+    sent_down = bf16(mm(half_rows(scaled_hidden, 1 - above), grad_rows))
+    term_down = mm(half_rows(scaled_hidden, above), grad_rows)
+    came_down = lax.ppermute(sent_down, "dp", swap_above)
+    combined = bf16(mm_tn(scaled_hidden, weight_down))
+
+    grad_hidden = mm_nt(weight_down, grad_rows)
     product = hidden.astype(jnp.float32) * grad_hidden
-    dot_expert = named * jnp.sum(jnp.where(routed_unit, product, 0.0), axis=1, keepdims=True)
-    dot_shared = jnp.sum(jnp.where(routed_unit, 0.0, product), axis=1, keepdims=True)
+    dot_expert = named * jnp.sum(jnp.where(routed_unit, product, 0.0), axis=0)[:, None]
+    dot_shared = jnp.sum(jnp.where(routed_unit, 0.0, product), axis=0)[:, None]
     grad_hidden = grad_hidden * unit_scale
     sigmoid_gate = jax.nn.sigmoid(gate_part)
     grad_gate = grad_hidden * up_part * sigmoid_gate * (1.0 + gate_part * (1.0 - sigmoid_gate))
     grad_up = grad_hidden * gate_part * sigmoid_gate
-    wide = ((0, 0), (0, padded - hidden_units))
-    grad_both_up = jnp.concatenate(
-        [jnp.pad(bf16(grad_gate), wide), jnp.pad(bf16(grad_up), wide)], axis=1
-    )
-    term_up = bf16(mm_tn(normed_all, grad_both_up))
-    up = lax.psum_scatter(term_up, "dp", scatter_dimension=0, tiled=True)
-    up = up.reshape(size * block, 2, padded)[:, :, :hidden_units]
-    up = up.reshape(size * block, 2, parts, pair_block)
-    grad_expert_in = (
-        up[:, :, :, :expert_block]
-        .reshape(1, size * block, 2 * parts * expert_block)
-        .astype(jnp.float32)
-    )
-    cut = lax.all_to_all(
-        up[:, :, :, expert_block:].reshape(size, block, 2 * own_shared),
-        "expert",
-        split_axis=0,
-        concat_axis=0,
-        tiled=True,
-    )
-    grad_shared_in = (
-        cut.reshape(size, block, 2, parts, shared_block)
-        .transpose(1, 2, 3, 0, 4)
-        .reshape(block, 2 * parts * size * shared_block)
-        .astype(jnp.float32)
-    )
-
+    grad_both_up = jnp.concatenate([bf16(grad_gate), bf16(grad_up)], axis=0)
+    half_width = width // 2
+
+    def half_cols(values, which):
+        return lax.dynamic_slice_in_dim(values, which * half_width, half_width, 1)
+
+    sent_up = bf16(mm(grad_both_up, half_cols(normed_all, 1 - above)))
+    came_up = lax.ppermute(sent_up, "dp", swap_above)
+    term_up = mm(grad_both_up, half_cols(normed_all, above))
+
+    taken = jnp.arange(slots, dtype=jnp.int32)[None, :] == slot
     zero = jnp.zeros((), jnp.bfloat16)
     riders = jnp.concatenate(
         [
-            jnp.where(mine, column, zero)
+            jnp.where(taken, column, zero)
             for column in two_parts(dot_shared) + two_parts(dot_expert)
         ],
         axis=1,
     )
     riders = jnp.pad(riders, ((0, 0), (0, extra - riders.shape[1])))
-    part = jnp.concatenate([bf16(mm_nt(grad_both_up, weight_up)), riders], axis=1)
-
-    def rows_of(values):
-        return lax.dynamic_slice_in_dim(values, me * rows, rows, 0)
+    part = jnp.concatenate([bf16(mm_tn(grad_both_up, weight_up)), riders], axis=1)
+    part, sent_up, sent_down = lax.optimization_barrier((part, sent_up, sent_down))
 
     rider = jnp.arange(extra, dtype=jnp.int32)[:, None]
     lane = jnp.arange(128, dtype=jnp.int32)[None, :]
     collect = bf16(
-        ((rider < 2 * experts) & (lane == 0))
-        | ((rider >= 2 * experts) & (rider < 4 * experts) & (lane == 1 + rider % experts))
+        ((rider < 2 * slots) & (lane == 0))
+        | ((rider >= 2 * slots) & (rider < 4 * slots) & (lane == 1 + rider % size))
     )
     probs = jnp.pad(
-        rows_of(jnp.concatenate([opener_all, probs_all], axis=1)), ((0, 0), (0, 127 - experts))
+        rows_of(jnp.concatenate([opener_all, probs_all], axis=1), slot),
+        ((0, 0), (0, 127 - experts)),
     )
     grad_middle, grad_branch, grad_heads, term_norm_two = remote_call(
         branch_kernel,
         chips,
-        [part, middle, gain_two[None, :], rows_of(grad_rows), probs, collect, router_rows],
+        [part, middle, gain_two[None, :], grad_own, probs, collect, router_rows],
         [
             ((rows, width), jnp.float32, False),
             ((group, width), jnp.bfloat16, True),
@@ -1062,12 +1214,20 @@
             pltpu.VMEM((rows, width + extra), jnp.float32),
             pltpu.VMEM((rows, width), jnp.bfloat16),
         ]
-        + scatter_scratch(chips, rows, width + extra)
-        + gather_scratch(chips),
+        + scatter_scratch(chips, rows, width + extra, True)
+        + gather_scratch(chips, False),
         2,
-        75,
-    )
-    term_router = mm_tn(rows_of(normed_all), grad_heads)[:, : 1 + experts]
+        90,
+    )
+    grad_branch, came_up = lax.optimization_barrier((grad_branch, came_up))
+    term_router = mm_tn(rows_of(normed_all, slot), grad_heads)[:, : 1 + experts]
+
+    up = bf16(term_up + came_up.astype(jnp.float32))
+    quarter = half_width // 2
+    side_kept = lax.dynamic_slice_in_dim(up, side_by * quarter, quarter, 1)
+    side_came = lax.ppermute(
+        lax.dynamic_slice_in_dim(up, (1 - side_by) * quarter, quarter, 1), "dp", swap_side
+    )
 
     grad_attended = bf16(mm_nt(grad_branch, weight_out)).reshape(group, own_heads, HD)
     weights_again = jnp.exp(score_rows() - log_total)
@@ -1097,21 +1257,7 @@
             axis=1,
         ).reshape(group, own_qkv)
     )
-    input_grad, term_norm_one = remote_call(
-        input_kernel,
-        chips,
-        [
-            bf16(mm_nt(grad_projected, weight_qkv)),
-            hidden_in,
-            gain_one[None, :],
-            grad_middle,
-        ],
-        [((rows, width), jnp.bfloat16, False), ((1, width), jnp.float32, False)],
-        [pltpu.VMEM((rows, width), jnp.float32)] + scatter_scratch(chips, rows, width),
-        3,
-        40,
-    )
-
+    part = bf16(mm_nt(grad_projected, weight_qkv))
     term_out = bf16(mm_tn(attended, grad_branch)).reshape(half, 2, block, width)
     kept = jnp.where(core == 0, term_out[:, 0], term_out[:, 1])
     given = jnp.where(core == 0, term_out[:, 1], term_out[:, 0])
@@ -1119,7 +1265,54 @@
     out_blocks = jnp.concatenate(
         [jnp.where(core == 0, kept, came), jnp.where(core == 0, came, kept)], axis=0
     )
-    term_qkv = mm_tn(normed_one, grad_projected)
+    back = jnp.concatenate(
+        [bf16(mm_tn(normed_one, grad_projected)), out_blocks.reshape(width, out_cols)], axis=1
+    )
+    part, back, came_down, side_came = lax.optimization_barrier((part, back, came_down, side_came))
+    back = lax.psum_scatter(back, "dp", scatter_dimension=0, tiled=True)
+    grad_out_weight = back[:, own_qkv:].reshape(block, width).astype(jnp.float32)
+    input_grad, term_norm_one = remote_call(
+        input_kernel,
+        chips,
+        [part, hidden_in, gain_one[None, :], grad_middle],
+        [((rows, width), jnp.bfloat16, False), ((1, width), jnp.float32, False)],
+        [pltpu.VMEM((rows, width), jnp.float32)] + scatter_scratch(chips, rows, width, False),
+        3,
+        40,
+    )
+    grad_down = term_down + came_down.astype(jnp.float32)
+    grad_shared_out = grad_down[expert_block:]
+    grad_expert_out = grad_down[None, :expert_block]
+    up = ordered(side_by, side_kept[None], side_came[None], 0)
+    up = up.reshape(2, 2, half, pair_block, quarter)
+    grad_expert_in = (
+        up[:, :, :, :expert_block]
+        .transpose(4, 1, 2, 0, 3)
+        .reshape(1, quarter, 2 * parts * expert_block)
+        .astype(jnp.float32)
+    )
+    cut = lax.all_to_all(
+        up[:, :, :, expert_block:].transpose(4, 1, 2, 0, 3).reshape(size, block, 2 * own_shared),
+        "expert",
+        split_axis=0,
+        concat_axis=0,
+        tiled=True,
+    )
+    grad_shared_in = (
+        cut.reshape(size, block, 2, parts, shared_block)
+        .transpose(1, 2, 3, 0, 4)
+        .reshape(block, 2 * parts * size * shared_block)
+        .astype(jnp.float32)
+    )
+    back = lax.all_to_all(
+        back[:, :own_qkv].reshape(size, block, own_qkv),
+        "expert",
+        split_axis=0,
+        concat_axis=0,
+        tiled=True,
+    )
+    grad_qkv = from_head(back).astype(jnp.float32)
+
     term_bias = jnp.sum(grad_projected.astype(jnp.float32), axis=0)
     bias_slots = jnp.where(jnp.arange(size)[:, None] == me, term_bias[None, :], 0.0)
     bias_rows = from_head(bias_slots[:, None, :]).reshape(width, bias_cols)
@@ -1127,38 +1320,29 @@
         [term_norm_one[0][:, None], term_norm_two[0][:, None], term_router, bias_rows], axis=1
     )
     count = small_terms.shape[1]
-    small_high, small_low = two_parts(small_terms)
-    small_terms = jnp.concatenate([small_high, small_low], axis=1)
-    small_terms = jnp.pad(small_terms, ((0, 0), (0, extra - 2 * count)))
-    back = lax.psum_scatter(
-        jnp.concatenate(
-            [bf16(term_qkv), small_terms, out_blocks.reshape(width, out_cols)], axis=1
-        ),
-        "dp",
-        scatter_dimension=0,
+    small_terms = lax.all_to_all(
+        small_terms.T.reshape(count, parts * size, block).transpose(1, 0, 2),
+        ("dp", "expert"),
+        split_axis=0,
+        concat_axis=0,
         tiled=True,
     )
-    grad_out_weight = back[:, own_qkv + extra :].reshape(block, width).astype(jnp.float32)
-    back = lax.all_to_all(
-        back[:, : own_qkv + extra].reshape(size, block, own_qkv + extra), "expert", split_axis=0, concat_axis=0, tiled=True
-    ).astype(jnp.float32)
-    grad_qkv = from_head(back[:, :, :own_qkv])
-    small_sum = jnp.sum(back[:, :, own_qkv:], axis=0)
-    small_sum = small_sum[:, :count] + small_sum[:, count : 2 * count]
+    small_sum = jnp.sum(small_terms, axis=0)
+    combined, input_grad = lax.optimization_barrier((combined, input_grad))
     (output,) = remote_call(
         output_kernel,
         chips,
-        [combined, middle, rows_of(valid_all)],
+        [combined, middle, valid_rows],
         [((rows, width), jnp.bfloat16, False)],
-        [pltpu.VMEM((rows, width), jnp.float32)] + scatter_scratch(chips, rows, width),
+        [pltpu.VMEM((rows, width), jnp.float32)] + scatter_scratch(chips, rows, width, True),
         4,
-        40,
-    )
-    grad_norm1 = small_sum[:, 0]
-    grad_norm2 = small_sum[:, 1]
-    grad_shared_gate = small_sum[:, 2]
-    grad_router = small_sum[:, 3 : 3 + experts]
-    grad_bias = small_sum[:, 3 + experts :].reshape(block * bias_cols)
+        55,
+    )
+    grad_norm1 = small_sum[0]
+    grad_norm2 = small_sum[1]
+    grad_shared_gate = small_sum[2]
+    grad_router = small_sum[3 : 3 + experts].T
+    grad_bias = small_sum[3 + experts :].T.reshape(block * bias_cols)
     return (
         output,
         input_grad,
@@ -1181,7 +1365,7 @@
 
     def device(*arrays):
         block = arrays[5].shape[0]
-        whole_heads = 2 * block == HD and parts % 2 == 0 and size % 2 == 0
+        whole_heads = 2 * block == HD and parts == 4 and size % 2 == 0
         one_expert = arrays[13].shape[0] == 1
         if whole_heads and one_expert and arrays[5].shape[1] % (3 * size * HD) == 0:
             return group_device(*arrays)

time: 1000 us -> 930 us (0.930)
  waiting for transfers between devices: 265 us -> 55 us
  Pallas kernels: 361 us -> 410 us
  other arithmetic: 43.8 us -> 82.7 us
  local copies, waits for them, and re-layouts: 104 us -> 141 us
  starting transfers between devices: 16.7 us -> 33.2 us
    reduce_scatter x3 -> x1, waiting for transfers between devices: 153 us -> 0.01 us  [group_device(): back = lax.psum_scatter(back, 'dp', scatter_dimension=0, tiled=True)]
    all_gather x3 -> x1, waiting for transfers between devices: 57.9 us -> 0.01 us  [group_device(): lax.all_gather(jnp.concatenate([first, out_weight.reshape(size * block, o...]
    pallas_call x5, Pallas kernels: 361 us -> 410 us  [remote_call(): pl.pallas_call(functools.partial(kernel, chips), out_shape=[jax.ShapeDtyp...]
    ppermute x0 -> x8, waiting for transfers between devices: none -> 33.5 us  [the longest x1 23.9 us: group_device(): lax.ppermute(lax.dynamic_slice_in_dim(up, (1 - side_by) * quarter, quarte...]
    all_to_all x3 -> x5, waiting for transfers between devices: 54.4 us -> 21.4 us  [the longest x1 21.4 us: group_device(): cut = lax.all_to_all(cut, 'expert', split_axis=0, concat_axis=0, tiled=True)]
    select_n x1 -> x7, other arithmetic: 0.08 us -> 18.8 us  [the longest x6 16.9 us: ordered(): first = jnp.where(which == 0, own, other)]
    slice x13 -> x2, local copies, waits for them, and re-layouts: 17 us -> 2.33 us  [group_device(): back[:, :own_qkv].reshape(size, block, own_qkv)]
    concatenate x8 -> x11, other arithmetic: 13.6 us -> 26.5 us  [the longest x1 7.89 us: group_device(): jnp.concatenate([bf16(mm_tn(grad_both_up, weight_up)), riders], axis=1)]
  transfers between devices with their start and end apart: 11 -> 17, of which waited for: 5 -> 3; matrix products, arithmetic and copies ran while one was open for 20% -> 29% of each run, Pallas kernels for 28% -> 45%
where the time goes in v3:
time: 930 us; the launch traced here: 920 us
  Pallas kernels  410 us (44%)
  matrix products  183 us (20%)
  local copies, waits for them, and re-layouts  141 us (15%)
  other arithmetic  82.7 us (9%)
  waiting for transfers between devices  55 us (6%)
  starting transfers between devices  33.2 us (4%)
  between operations  15.6 us (2%)
    pallas_call x5, Pallas kernels, remote_call(): pl.pallas_call(functools.partial(kernel, chips), out_shape=[jax.ShapeDtyp...  410 us
    dot_general x5, matrix products, mm_nt(): lax.dot_general(left, right, (((1,), (1,)), ((), ())), preferred_element_...  63.5 us
    dot_general x6, matrix products, mm(): return jnp.dot(left, right, preferred_element_type=jnp.float32)  54.8 us
    dot_general x5, matrix products, mm_tn(): lax.dot_general(left, right, (((0,), (0,)), ((), ())), preferred_element_...  50.1 us
    unnamed x134, local copies, waits for them, and re-layouts  30.2 us
    ppermute x1, waiting for transfers between devices, group_device(): lax.ppermute(lax.dynamic_slice_in_dim(up, (1 - side_by) * quarter, quarte...  23.9 us
    all_to_all x1, waiting for transfers between devices, group_device(): cut = lax.all_to_all(cut, 'expert', split_axis=0, concat_axis=0, tiled=True)  21.4 us
    convert_element_type x3, local copies, waits for them, and re-layouts, group_device(): grad_shared_in = cut.reshape(size, block, 2, parts, shared_block).transpo...  20.5 us
  transfers between devices with their start and end apart: 17, of which 3 were waited for; matrix products, arithmetic and copies ran while one was open for 29% of the time, Pallas kernels for 45%

profile of v3, /device:TPU:0, one launch (start us, length us, event | category | flops | bytes accessed | tf_op | source)
XLA Modules:
  0.0 919.9 jit_solution(18056566424616424120)
XLA Ops:
  14.1 6.3 all-to-all-start
  20.5 4.5 copy.206
  29.9 3.2 pad_maximum_fusion.14
  35.9 5.8 reshape.473
  41.7 3.7 copy.257
  45.4 5.4 reshape.474
  57.6 95.7 %shard_map.246 = (bf16[1024,2048]{1,0:T(8,128)(2,1)}, bf16[2048,2176]{1,0:T(8,128)(2,1)}) custom-call(bf16[128,2048]{1,0:T(8,128)(2,1)} %hidden.3, bf16[128,2176]{1,0:T(8,128)(2,1)} %fusion.41.far), custom_call_target="tpu_custom_call" | custom-call | flops 74999996416 | bytes 1081344 | tf_op jit(solution)/shard_map/pallas_call | solution.py:881
  153.4 4.6 all-to-all-start.1
  171.7 21.4 %all-to-all-done.1 = bf16[8,64,1408]{2,1,0:T(8,128)(2,1)} async-done(((bf16[8,64,1408]{2,1,0:T(8,128)(2,1)}), bf16[8,64,1408]{2,1,0:T(8,128)(2,1)}, u32[]{:S(2)}, u32[]{:S(2)}) %all-to-all-start.1) | async-done | bytes 1441824 | tf_op jit(solution)/shard_map/all_to_all | solution.py:1053
  193.1 9.0 reshape_reshape.10
  202.2 6.0 copy.218
  211.9 5.5 broadcast_select_fusion.5
  217.4 9.6 %collective-permute-done.4 = bf16[704,512]{1,0:T(8,128)(2,1)S(1)} collective-permute-done((bf16[704,512]{1,0:T(8,128)(2,1)S(1)}, bf16[704,512]{1,0:T(8,128)(2,1)S(1)}, u32[]{:S(2)}, u32[]{:S(2)}) %collective-permute-start.4) | collective-permute-done | bytes 720928 | tf_op jit(solution)/shard_map/ppermute | solution.py:1020
  236.0 7.3 fusion.25
  268.1 3.3 convolution_convert_fusion.3.part
  271.4 94.6 %shard_map.247 = (f32[128,2048]{1,0:T(8,128)}, bf16[2048,2048]{1,0:T(8,128)(2,1)}) custom-call(bf16[1024,2048]{1,0:T(8,128)(2,1)} %convolution_convert_fusion.3.part, bf16[128,2048]{1,0:T(8,128)(2,1)} %hidden.3, f32[1,2048]{1,0:T(1,128)} %get-tuple-element.155.gain), custom_call_target="tpu_custom_call" | custom-call | flops 85000003584 | bytes 4726784 | tf_op jit(solution)/shard_map/pallas_call | solution.py:881
  366.0 6.3 fusion.53
  375.4 3.7 broadcast_select_fusion.1
  381.6 3.9 pad_maximum_fusion.1
  385.5 24.9 %fusion.91 = f32[2112,2048]{1,0:T(8,128)} fusion(bf16[2112,2048]{1,0:T(8,128)(2,1)} %bitcast.193, bf16[2048,2048]{1,0:T(8,128)(2,1)} %get-tuple-element.53), kind=kOutput, calls=%fused_computation.227 | convolution fusion | flops 17716740096 | bytes 34340864 | tf_op jit(solution)/shard_map/dot_general | solution.py:909
  412.4 23.2 %multiply_convert_fusion.1 = (bf16[1056,2048]{1,0:T(8,128)(2,1)}, bf16[1056,2048]{1,0:T(8,128)(2,1)}, f32[2048]{0:T(1024)S(1)}, f32[2048]{0:T(1024)S(1)}, bf16[1056,2048]{1,0:T(8,128)(2,1)}) fusion(f32[2112,2048]{1,0:T(8,128)} %fusion.91, f32[2048]{0:T(1024)S(1)} %bitcast.214, f32[2048]{0:T(1024)S(1)} %mul.239, pred[1056]{0:T(1024)(128)(4,1)S(1)} %copy-done.44, ...), kind=kOutput, calls=%fused_computation.13 | convolution fusion | flops 8918921216 | bytes 43025440 | tf_op jit(solution)/shard_map/dot_general | solution.py:909
  435.6 3.5 fusion
  441.0 25.5 %convolution_convert_fusion = bf16[2048,2048]{1,0:T(8,128)(2,1)} fusion(bf16[2112,2048]{1,0:T(8,128)(2,1)S(1)} %bitcast.194, bf16[1056,2048]{1,0:T(8,128)(2,1)} %get-tuple-element.146, bf16[1056,2048]{1,0:T(8,128)(2,1)} %get-tuple-element.145), kind=kOutput, calls=%fused_computation.24 | convolution fusion | flops 17738235904 | bytes 25690112 | tf_op jit(solution)/shard_map/dot_general | solution.py:915
  466.6 11.5 %convolution_convert_fusion.2 = bf16[2112,1024]{1,0:T(8,128)(2,1)} fusion(bf16[2048,2048]{1,0:T(8,128)(2,1)S(1)} %bitcast.218, s32[]{:T(128)S(6)} %select_n.282, bf16[1056,2048]{1,0:T(8,128)(2,1)} %get-tuple-element.146, bf16[1056,2048]{1,0:T(8,128)(2,1)S(1)} %bitcast.228), kind=kOutput, calls=%fused_computation.34 | convolution fusion | flops 8877834240 | bytes 17170436 | tf_op jit(solution)/shard_map/dot_general | solution.py:905
  478.6 9.2 fusion.14
  492.0 7.9 pad_maximum_fusion.part
  500.7 108.5 %shard_map.248 = (f32[128,2048]{1,0:T(8,128)}, bf16[1024,2048]{1,0:T(8,128)(2,1)}, bf16[128,128]{1,0:T(8,128)(2,1)}, f32[1,2048]{1,0:T(1,128)}) custom-call(bf16[2048,2176]{1,0:T(8,128)(2,1)} %pad_maximum_fusion.part, f32[128,2048]{1,0:T(8,128)} %get-tuple-element.58.middle, f32[1,2048]{1,0:T(1,128)} %get-tuple-element.155.gain, ...), custom_call_target="tpu_custom_call" | custom-call | flops 89999998976 | bytes 11116544 | tf_op jit(solution)/shard_map/pallas_call | solution.py:881
  611.3 15.8 %convolution_convert_fusion.1.part = bf16[2048,2048]{1,0:T(8,128)(2,1)} fusion(bf16[1056,2048]{1,0:T(8,128)(2,1)} %copy-done.16, bf16[528,2048]{1,0:T(8,128)(2,1)} %get-tuple-element.160, bf16[528,2048]{1,0:T(8,128)(2,1)S(1)} %copy-done.26), kind=kOutput, calls=%fused_computation.25 | convolution fusion | flops 8871215104 | bytes 17039360 | tf_op jit(solution)/shard_map/dot_general | solution.py:915
  631.2 4.4 multiply_reduce_fusion
  643.8 14.1 %add_convert_fusion = bf16[2112,1024]{1,0:T(8,128)(2,1)S(1)} fusion(bf16[2112,1024]{1,0:T(8,128)(2,1)} %collective-permute-done.6, bf16[2048,2048]{1,0:T(8,128)(2,1)} %get-tuple-element.53, s32[]{:T(128)S(6)} %select_n.293, bf16[1056,2048]{1,0:T(8,128)(2,1)} %get-tuple-element.146, bf16[1056,2048]{1,0:T(8,128)(2,1)} %get-tuple-element.145), kind=kOutput, calls=%fused_computation.9 | convolution fusion | flops 8882159616 | bytes 21495812 | tf_op jit(solution)/shard_map/dot_general | solution.py:905
  663.5 5.5 convolution_convert_fusion.5
  670.3 7.8 convolution_convert_fusion.4.part
  680.5 4.5 pad_maximum_fusion.5
  685.1 23.9 %collective-permute-done.9 = bf16[2112,512]{1,0:T(8,128)(2,1)} collective-permute-done((bf16[2112,512]{1,0:T(8,128)(2,1)}, bf16[2112,512]{1,0:T(8,128)(2,1)}, u32[]{:S(2)}, u32[]{:S(2)}) %collective-permute-start.9) | collective-permute-done | bytes 2162720 | tf_op jit(solution)/shard_map/ppermute | solution.py:1228
  709.0 44.9 %shard_map.249 = (bf16[128,2048]{1,0:T(8,128)(2,1)}, f32[1,2048]{1,0:T(1,128)}) custom-call(bf16[1024,2048]{1,0:T(8,128)(2,1)} %convolution_convert_fusion.4.part, bf16[128,2048]{1,0:T(8,128)(2,1)} %hidden.3, f32[1,2048]{1,0:T(1,128)} %get-tuple-element.154.gain, f32[128,2048]{1,0:T(8,128)} %get-tuple-element.63.grad_middle), custom_call_target="tpu_custom_call" | custom-call | flops 40000000000 | bytes 5775360 | tf_op jit(solution)/shard_map/pallas_call | solution.py:881
  758.9 3.2 broadcast_select_fusion.3
  764.6 6.0 copy.238
  770.6 6.4 reshape.491
  777.0 4.9 all-to-all-start.4
  781.9 65.9 %shard_map.250 = bf16[128,2048]{1,0:T(8,128)(2,1)} custom-call(bf16[2048,2048]{1,0:T(8,128)(2,1)} %convolution_convert_fusion.1.part, f32[128,2048]{1,0:T(8,128)} %get-tuple-element.58.middle, f32[128,1]{1,0:T(8,128)} %copy.229.valid), custom_call_target="tpu_custom_call" | custom-call | flops 54999998464 | bytes 9437696 | tf_op jit(solution)/shard_map/pallas_call | solution.py:881
  847.8 9.4 %convert_add_fusion = f32[528,2048]{1,0:T(8,128)S(1)} fusion(bf16[528,2048]{1,0:T(8,128)(2,1)} %collective-permute-done.8, bf16[2048,2176]{1,0:T(8,128)(2,1)} %get-tuple-element.46, bf16[1056,2048]{1,0:T(8,128)(2,1)} %copy-done.16, s32[]{:T(128)S(6)} %select_n.300), kind=kOutput, calls=%fused_computation.37 | convolution fusion | flops 4431347712 | bytes 17039364 | tf_op jit(solution)/shard_map/dot_general | solution.py:905
  860.3 3.3 fusion.17
  863.6 6.2 copy.240
  872.2 3.5 all-to-all-start.3
  875.7 3.7 slice_bitcast_fusion
  882.9 8.4 reshape.501
  891.3 6.6 copy.239
  898.0 5.5 reshape.498
  (292 shorter events, 136.4 us)
Async XLA Ops:
  14.1 40.9 %all-to-all-start = ((bf16[8,64,896]{2,1,0:T(8,128)(2,1)}), bf16[8,64,896]{2,1,0:T(8,128)(2,1)}, u32[]{:S(2)}, u32[]{:S(2)}) async-start(bf16[8,64,896]{2,1,0:T(8,128)(2,1)} %pad_maximum_fusion.19), calls=%async_computation | async-start | bytes 1835008 | tf_op jit(solution)/shard_map/all_to_all | solution.py:1000
  20.5 210.4 %all-gather.2.cloned.1.call-start = ((), (), s32[]{:S(2)}) async-start(), calls=%async_computation.6 | async-start | bytes 5898240 | tf_op jit(solution)/shard_map/all_gather | solution.py:1003
  27.2 14.5 %copy-start.7 = (bf16[2,2,2,352,512]{4,3,2,1,0:T(8,128)(2,1)}, bf16[2,2,2,352,512]{4,3,2,1,0:T(8,128)(2,1)S(1)}, u32[]{:S(2)}) copy-start(bf16[2,2,2,352,512]{4,3,2,1,0:T(8,128)(2,1)S(1)} %copy.207) | copy-start | bytes 8650756
  27.2 7.5 copy-start.54
  27.2 8.4 copy-start.39
  28.4 124.9 %collective-permute-start = (bf16[1408,512]{1,0:T(8,128)(2,1)}, bf16[1408,512]{1,0:T(8,128)(2,1)}, u32[]{:S(2)}, u32[]{:S(2)}) collective-permute-start(bf16[1408,512]{1,0:T(8,128)(2,1)} %dynamic-slice_bitcast_fusion), channel_id=1, source_target_pairs={{0,8},{8,0},{16,24},{24,16},{1,9},{9,1},{17,25},{25,17},{2,10},{10... | collective-permute-start | bytes 4325384 | tf_op jit(solution)/shard_map/ppermute | solution.py:1020
  33.1 120.3 %collective-permute-start.1 = (bf16[528,2048]{1,0:T(8,128)(2,1)}, bf16[528,2048]{1,0:T(8,128)(2,1)}, u32[]{:S(2)}, u32[]{:S(2)}) collective-permute-start(bf16[528,2048]{1,0:T(8,128)(2,1)} %pad_maximum_fusion.14), channel_id=1, source_target_pairs={{0,16},{8,24},{16,0},{24,8},{1,17},{9,25},{17,1},{25,9},{2,18},{10... | collective-permute-start | bytes 6488072 | tf_op jit(solution)/shard_map/ppermute | solution.py:1011
  41.7 9.1 copy-start.50
  153.4 39.8 %all-to-all-start.1 = ((bf16[8,64,1408]{2,1,0:T(8,128)(2,1)}), bf16[8,64,1408]{2,1,0:T(8,128)(2,1)}, u32[]{:S(2)}, u32[]{:S(2)}) async-start(bf16[8,64,1408]{2,1,0:T(8,128)(2,1)} %reshape.474), calls=%async_computation.1 | async-start | bytes 2883584 | tf_op jit(solution)/shard_map/all_to_all | solution.py:1053
  158.0 711.8 %reduce-scatter.2.cloned.1.call-start = ((), (), s32[]{:S(2)}) async-start(), calls=%async_computation.7 | async-start | bytes 5242880 | tf_op jit(solution)/shard_map/reduce_scatter | solution.py:1272
  164.6 99.4 %copy-start.1 = (pred[1024,1024]{0,1:T(8,128)(4,1)}, pred[1024,1024]{0,1:T(8,128)(4,1)S(1)}, u32[]{:S(2)}) copy-start(pred[1024,1024]{0,1:T(8,128)(4,1)S(1)} %compare_and_fusion) | copy-start | bytes 3145732
  169.0 102.3 %collective-permute-start.3 = (bf16[1408,1024]{1,0:T(8,128)(2,1)}, bf16[1408,1024]{1,0:T(8,128)(2,1)}, u32[]{:S(2)}, u32[]{:S(2)}) collective-permute-start(bf16[1408,1024]{1,0:T(8,128)(2,1)} %pad_maximum_fusion.7), channel_id=1, source_target_pairs={{0,16},{8,24},{16,0},{24,8},{1,17},{9,25},{17,1},{25,9},{2,18},{10... | collective-permute-start | bytes 8650760 | tf_op jit(solution)/shard_map/ppermute | solution.py:1048
  171.7 64.3 %copy-start.48 = (f32[1024]{0:T(1024)}, f32[1024]{0:T(1024)S(1)}, u32[]{:S(2)}) copy-start(f32[1024]{0:T(1024)S(1)} %add_rsqrt_fusion) | copy-start | bytes 12292
  171.7 40.2 %copy-start.24 = (bf16[176,2048]{1,0:T(8,128)(2,1)S(1)}, bf16[176,2048]{1,0:T(8,128)(2,1)}, u32[]{:S(2)}) copy-start(bf16[176,2048]{1,0:T(8,128)(2,1)} %param.27) | copy-start | bytes 2162692
  209.3 17.7 %collective-permute-start.4 = (bf16[704,512]{1,0:T(8,128)(2,1)S(1)}, bf16[704,512]{1,0:T(8,128)(2,1)S(1)}, u32[]{:S(2)}, u32[]{:S(2)}) collective-permute-start(bf16[704,512]{1,0:T(8,128)(2,1)S(1)} %dynamic-slice_bitcast_fusion.1), channel_id=1, source_target_pairs={{0,8},{8,0},{16,24},{24,16},{1,9},{9,1},{17,25},{25,17},{2,10},{10... | collective-permute-start | bytes 2162696 | tf_op jit(solution)/shard_map/ppermute | solution.py:1020
  211.9 15.2 %copy-start.14 = (bf16[2,2,2,176,512]{4,3,2,1,0:T(8,128)(2,1)S(1)}, bf16[2,2,2,176,512]{4,3,2,1,0:T(8,128)(2,1)}, u32[]{:S(2)}) copy-start(bf16[2,2,2,176,512]{4,3,2,1,0:T(8,128)(2,1)} %copy.218) | copy-start | bytes 4325380
  229.4 136.6 %collective-permute-start.5 = (bf16[704,1024]{1,0:T(8,128)(2,1)}, bf16[704,1024]{1,0:T(8,128)(2,1)}, u32[]{:S(2)}, u32[]{:S(2)}) collective-permute-start(bf16[704,1024]{1,0:T(8,128)(2,1)} %pad_maximum_fusion.15), channel_id=1, source_target_pairs={{0,16},{8,24},{16,0},{24,8},{1,17},{9,25},{17,1},{25,9},{2,18},{10... | collective-permute-start | bytes 4325384 | tf_op jit(solution)/shard_map/ppermute | solution.py:1111
  236.0 7.3 copy-start.45
  255.0 11.8 %collective-permute-start.2 = (bf16[2,64,2048]{2,1,0:T(8,128)(2,1)S(1)}, bf16[2,64,2048]{2,1,0:T(8,128)(2,1)S(1)}, u32[]{:S(2)}, u32[]{:S(2)}) collective-permute-start(bf16[2,64,2048]{2,1,0:T(8,128)(2,1)S(1)} %constant_dynamic-slice_fusion.1), channel_id=1, source_target_pairs={{0,1},{1,0},{2,3},{3,2},{4,5},{5,4},{6,7},{7,6},{8,9},{9,8},{10,11... | collective-permute-start | bytes 1572872 | tf_op jit(solution)/shard_map/ppermute | solution.py:1076
  366.0 7.3 copy-start.13
  385.5 25.9 %copy-start.52 = (pred[8]{0:T(512)(128)(4,1)S(1)}, pred[8]{0:T(512)(128)(4,1)}, u32[]{:S(2)}) copy-start(pred[8]{0:T(512)(128)(4,1)} %iota_compare_fusion.8) | copy-start | bytes 28
  385.5 26.9 %copy-start.42 = (f32[2048]{0:T(1024)S(1)}, f32[2048]{0:T(1024)}, u32[]{:S(2)}) copy-start(f32[2048]{0:T(1024)} %convert_reduce_fusion.1) | copy-start | bytes 24580
  385.5 26.9 %copy-start.25 = (bf16[528,2048]{1,0:T(8,128)(2,1)S(1)}, bf16[528,2048]{1,0:T(8,128)(2,1)}, u32[]{:S(2)}) copy-start(bf16[528,2048]{1,0:T(8,128)(2,1)} %get-tuple-element.159) | copy-start | bytes 6488068
  385.5 26.9 %copy-start.44 = (pred[1056]{0:T(1024)(128)(4,1)S(1)}, pred[1056]{0:T(1024)(128)(4,1)}, u32[]{:S(2)}) copy-start(pred[1056]{0:T(1024)(128)(4,1)} %fusion.61) | copy-start | bytes 3172
  435.6 5.4 copy-start.11
  435.6 30.9 %slice-start.2 = ((s8[8388608]{0:T(1024)(128)(4,1)}), s8[4194304]{0:T(1024)(128)(4,1)S(1)}, s32[]{:S(2)}) async-start(s8[8388608]{0:T(1024)(128)(4,1)} %bitcast.217), calls=%async_computation.10 | async-start | bytes 8388608
  435.6 30.9 %slice-start.4 = ((s8[4325376]{0:T(1024)(128)(4,1)}), s8[4194304]{0:T(1024)(128)(4,1)S(1)}, s32[]{:S(2)}) async-start(s8[4325376]{0:T(1024)(128)(4,1)} %bitcast.227), calls=%async_computation.12 | async-start | bytes 8388608
  439.1 39.6 %copy-start.16 = (bf16[1056,2048]{1,0:T(8,128)(2,1)}, bf16[1056,2048]{1,0:T(8,128)(2,1)S(1)}, u32[]{:S(2)}) copy-start(bf16[1056,2048]{1,0:T(8,128)(2,1)S(1)} %fusion) | copy-start | bytes 12976132
  441.0 25.5 %slice-start.3 = ((s8[8388608]{0:T(1024)(128)(4,1)}), s8[4194304]{0:T(1024)(128)(4,1)S(1)}, s32[]{:S(2)}) async-start(s8[8388608]{0:T(1024)(128)(4,1)} %bitcast.217), calls=%async_computation.11 | async-start | bytes 8388608
  441.0 25.5 %slice-start.5 = ((s8[4325376]{0:T(1024)(128)(4,1)}), s8[131072]{0:T(1024)(128)(4,1)S(1)}, s32[]{:S(2)}) async-start(s8[4325376]{0:T(1024)(128)(4,1)} %bitcast.227), calls=%async_computation.13 | async-start | bytes 262144
  478.1 11.2 %copy-start.53 = (pred[16]{0:T(512)(128)(4,1)S(1)}, pred[16]{0:T(512)(128)(4,1)}, u32[]{:S(2)}) copy-start(pred[16]{0:T(512)(128)(4,1)} %iota_compare_fusion.7) | copy-start | bytes 52
  478.1 149.0 %collective-permute-start.6 = (bf16[2112,1024]{1,0:T(8,128)(2,1)}, bf16[2112,1024]{1,0:T(8,128)(2,1)}, u32[]{:S(2)}, u32[]{:S(2)}) collective-permute-start(bf16[2112,1024]{1,0:T(8,128)(2,1)} %convolution_convert_fusion.2), channel_id=1, source_target_pairs={{0,16},{8,24},{16,0},{24,8},{1,17},{9,25},{17,1},{25,9},{2,18},{10... | collective-permute-start | bytes 12976136 | tf_op jit(solution)/shard_map/ppermute | solution.py:1177
  487.8 197.3 %collective-permute-start.8 = (bf16[528,2048]{1,0:T(8,128)(2,1)}, bf16[528,2048]{1,0:T(8,128)(2,1)}, u32[]{:S(2)}, u32[]{:S(2)}) collective-permute-start(bf16[528,2048]{1,0:T(8,128)(2,1)} %fusion.14), channel_id=1, source_target_pairs={{0,16},{8,24},{16,0},{24,8},{1,17},{9,25},{17,1},{25,9},{2,18},{10... | collective-permute-start | bytes 6488072 | tf_op jit(solution)/shard_map/ppermute | solution.py:1159
  500.7 110.6 %copy-start.26 = (bf16[528,2048]{1,0:T(8,128)(2,1)S(1)}, bf16[528,2048]{1,0:T(8,128)(2,1)}, u32[]{:S(2)}) copy-start(bf16[528,2048]{1,0:T(8,128)(2,1)} %get-tuple-element.159) | copy-start | bytes 6488068
  609.2 19.2 %slice-start = ((s8[8388608]{0:T(1024)(128)(4,1)}), s8[4194304]{0:T(1024)(128)(4,1)S(1)}, s32[]{:S(2)}) async-start(s8[8388608]{0:T(1024)(128)(4,1)} %bitcast.176), calls=%async_computation.8 | async-start | bytes 8388608
  611.3 15.8 %copy-start.23 = (bf16[2,2,64,2048]{3,2,1,0:T(8,128)(2,1)S(1)}, bf16[2,2,64,2048]{3,2,1,0:T(8,128)(2,1)}, u32[]{:S(2)}) copy-start(bf16[2,2,64,2048]{3,2,1,0:T(8,128)(2,1)} %copy-done.22) | copy-start | bytes 3145732
  611.3 15.8 %copy-start.55 = (bf16[1024,2048]{1,0:T(8,128)(2,1)S(1)}, bf16[1024,2048]{1,0:T(8,128)(2,1)}, u32[]{:S(2)}) copy-start(bf16[1024,2048]{1,0:T(8,128)(2,1)} %get-tuple-element.60) | copy-start | bytes 12582916
  611.3 17.1 %slice-start.1 = ((s8[8388608]{0:T(1024)(128)(4,1)}), s8[4194304]{0:T(1024)(128)(4,1)S(1)}, s32[]{:S(2)}) async-start(s8[8388608]{0:T(1024)(128)(4,1)} %bitcast.176), calls=%async_computation.9 | async-start | bytes 8388608
  643.4 34.7 %collective-permute-start.7 = (bf16[2,64,2048]{2,1,0:T(8,128)(2,1)}, bf16[2,64,2048]{2,1,0:T(8,128)(2,1)}, u32[]{:S(2)}, u32[]{:S(2)}) collective-permute-start(bf16[2,64,2048]{2,1,0:T(8,128)(2,1)} %select_bitcast_fusion), channel_id=1, source_target_pairs={{0,1},{1,0},{2,3},{3,2},{4,5},{5,4},{6,7},{7,6},{8,9},{9,8},{10,11... | collective-permute-start | bytes 1572872 | tf_op jit(solution)/shard_map/ppermute | solution.py:1264
  659.6 49.4 %collective-permute-start.9 = (bf16[2112,512]{1,0:T(8,128)(2,1)}, bf16[2112,512]{1,0:T(8,128)(2,1)}, u32[]{:S(2)}, u32[]{:S(2)}) collective-permute-start(bf16[2112,512]{1,0:T(8,128)(2,1)} %constant_dynamic-slice_fusion), channel_id=1, source_target_pairs={{0,8},{8,0},{16,24},{24,16},{1,9},{9,1},{17,25},{25,17},{2,10},{10... | collective-permute-start | bytes 6488072 | tf_op jit(solution)/shard_map/ppermute | solution.py:1228
  661.6 7.3 copy-start.35
  663.5 5.5 copy-start.51
  709.0 45.0 %copy-start.38 = (f32[2048,9]{0,1:T(8,128)S(1)}, f32[2048,9]{0,1:T(8,128)}, u32[]{:S(2)}) copy-start(f32[2048,9]{0,1:T(8,128)} %fusion.48) | copy-start | bytes 221188
  709.0 45.0 %copy-start.47 = (f32[1,2048]{1,0:T(1,128)S(1)}, f32[1,2048]{1,0:T(1,128)}, u32[]{:S(2)}) copy-start(f32[1,2048]{1,0:T(1,128)} %get-tuple-element.68) | copy-start | bytes 24580
  755.8 21.2 %all-to-all-start.2 = ((f32[32,1,896]{2,1,0:T(1,128)}), f32[32,1,896]{2,1,0:T(1,128)S(1)}, u32[]{:S(2)}, u32[]{:S(2)}) async-start(f32[32,1,896]{2,1,0:T(1,128)} %reshape.503), calls=%async_computation.2 | async-start | bytes 229376 | tf_op jit(solution)/shard_map/all_to_all | solution.py:1323
  777.0 95.2 %all-to-all-start.4 = ((bf16[8,64,1408]{2,1,0:T(8,128)(2,1)}), bf16[8,64,1408]{2,1,0:T(8,128)(2,1)}, u32[]{:S(2)}, u32[]{:S(2)}) async-start(bf16[8,64,1408]{2,1,0:T(8,128)(2,1)} %reshape.491), calls=%async_computation.5 | async-start | bytes 2883584 | tf_op jit(solution)/shard_map/all_to_all | solution.py:1294
  857.1 6.5 copy-start.17
  872.2 33.3 %all-to-all-start.3 = ((bf16[8,64,768]{2,1,0:T(8,128)(2,1)}), bf16[8,64,768]{2,1,0:T(8,128)(2,1)S(1)}, u32[]{:S(2)}, u32[]{:S(2)}) async-start(bf16[8,64,768]{2,1,0:T(8,128)(2,1)} %bitcast.58), calls=%async_computation.4 | async-start | bytes 1572864 | tf_op jit(solution)/shard_map/all_to_all | solution.py:1307
  (32 other events, 83.1 us)
Sparse Core Ops, SparseCore 0:
  57.7 85.3 all-gather.1
  709.1 50.5 reduce-scatter.1

commit v4 on v3

--- a/solution.py
+++ b/solution.py
@@ -480,10 +480,10 @@
         return self.out.at[pl.ds(place * self.rows, self.rows)]
 
     def mine(self, chip, which):
-        return self.block(self.line.x, chip, which)
+        return self.block(0, chip, which)
 
     def theirs(self, chip, which):
-        return self.block(1 - self.line.x, chip, which)
+        return self.block(1, chip, which)
 
     def origin(self, step, up):
         return self.line.z - step if up else self.line.z + step
@@ -542,7 +542,7 @@
         core = self.line.core
         self.across(index, source, self.mine(origin, core), 0).start()
         if self.wide:
-            self.across(index, source, self.mine(origin, core), 1).start()
+            self.across(index, source, self.theirs(origin, core), 1).start()
 
     def begin(self):
         line = self.line
@@ -602,7 +602,7 @@
         pltpu.make_async_copy(self.own, self.mine(line.z, core), self.local).wait()
 
 
-def gather_lines(*gathers):
+def gather_lines(*gathers, late=None):
     chips = gathers[0].line.chips
     for one in gathers:
         one.begin()
@@ -611,6 +611,8 @@
             one.push(step)
         for one in gathers:
             one.pull(step)
+    if late is not None:
+        late()
     for one in gathers:
         one.end()
 
@@ -651,7 +653,7 @@
     def start_of(other, chip, which):
         place = 2 * chip + which
         if wide:
-            place = place + (1 - line.x if other else line.x) * (2 * chips)
+            place = place + other * (2 * chips)
         return place * rows
 
     def across(other, chip):
@@ -780,17 +782,59 @@
     settle(z)
 
 
-def gather_kernel(chips, near, far, near_all, far_all, *scratch):
+def gather_kernel(chips, near, near_all, *scratch):
+    line = Line(chips, False)
+    line.meet()
+    gather_lines(Gather(line, near, near_all, scratch))
+
+
+def aside_scratch(chips):
+    return [pltpu.SemaphoreType.DMA((chips,)) for _ in range(4)]
+
+
+class Aside:
+    def __init__(self, line, own, out, scratch):
+        self.line, self.own, self.out = line, own, out
+        self.sems = scratch
+        self.rows = own.shape[0] // (2 * line.chips)
+
+    def copy(self, chip, kind, which):
+        line = self.line
+        place = pl.ds((2 * chip + which) * self.rows, self.rows)
+        source = self.out if kind else self.own
+        return pltpu.make_async_remote_copy(
+            src_ref=source.at[place],
+            dst_ref=self.out.at[place],
+            send_sem=self.sems[2 * kind].at[chip],
+            recv_sem=self.sems[2 * kind + 1].at[chip],
+            device_id=line.at(line.z, 1 - line.core) if kind else line.beside(),
+            device_id_type=MESH_IDS,
+        )
+
+    def begin(self):
+        for chip in range(self.line.chips):
+            self.copy(chip, 0, self.line.core).start()
+
+    def turn(self):
+        for chip in range(self.line.chips):
+            self.copy(chip, 0, self.line.core).wait_recv()
+            self.copy(chip, 1, self.line.core).start()
+
+    def end(self):
+        core = self.line.core
+        for chip in range(self.line.chips):
+            self.copy(chip, 0, core).wait_send()
+            self.copy(chip, 1, core).wait_send()
+            self.copy(chip, 1, 1 - core).wait_recv()
+
+
+def middle_kernel(
+    chips, part, hidden, gain, near, middle, normed_all, far, total, normed, *scratch
+):
     line = Line(chips, True)
     line.meet()
-    gather_lines(
-        Gather(line, near, near_all, scratch[:5]), Gather(line, far, far_all, scratch[5:])
-    )
-
-
-def middle_kernel(chips, part, hidden, gain, middle, normed_all, total, normed, *scratch):
-    line = Line(chips, True)
-    line.meet()
+    aside = Aside(line, near, far, scratch[15:])
+    aside.begin()
     scatter_line(line, part, total, scratch[:6])
 
     def body(strip):
@@ -799,7 +843,8 @@
         normed[strip, :] = (rows * rms_scale(rows) * gain[...]).astype(jnp.bfloat16)
 
     strips(hidden.shape[0], body)
-    gather_lines(Gather(line, normed, normed_all, scratch[6:]))
+    gather_lines(Gather(line, normed, normed_all, scratch[6:15]), late=aside.turn)
+    aside.end()
 
 
 def branch_kernel(
@@ -864,26 +909,15 @@
     strips(hidden.shape[0], body)
 
 
-def output_kernel(chips, part, middle, valid, output, total, *scratch):
-    line = Line(chips, True)
-    line.meet()
-    scatter_line(line, part, total, scratch)
-
-    def body(strip):
-        rows = valid[strip, :] * (middle[strip, :] + total[strip, :])
-        output[strip, :] = rows.astype(jnp.bfloat16)
-
-    strips(middle.shape[0], body)
-
-
-def remote_call(kernel, chips, inputs, outputs, scratch, number, micros):
+def remote_call(kernel, chips, inputs, outputs, scratch, number, micros, far=0):
     moved = sum(a.size * a.dtype.itemsize for a in inputs)
     return pl.pallas_call(
         functools.partial(kernel, chips),
         out_shape=[jax.ShapeDtypeStruct(shape, kind) for shape, kind, _ in outputs],
-        in_specs=[pl.BlockSpec(memory_space=pltpu.VMEM)] * len(inputs),
+        in_specs=[pl.BlockSpec(memory_space=pltpu.VMEM)] * (len(inputs) - far)
+        + [pl.BlockSpec(memory_space=pl.ANY)] * far,
         out_specs=[
-            pl.BlockSpec(memory_space=pl.ANY if far else pltpu.VMEM) for _, _, far in outputs
+            pl.BlockSpec(memory_space=pl.ANY if kept else pltpu.VMEM) for _, _, kept in outputs
         ],
         scratch_shapes=scratch,
         compiler_params=pltpu.CompilerParams(collective_id=number, has_side_effects=True),
@@ -1026,34 +1060,26 @@
     valid_rows = rows_of(valid_all, me)
     grad_own = bf16(out_grad.astype(jnp.float32) * valid_rows)
     side = jnp.pad(bf16(routes), ((0, 0), (0, extra - top)))
-    far = jnp.concatenate([grad_own, side], axis=1)
-    far, first = lax.optimization_barrier((far, first))
-    hidden_all, far_all = remote_call(
+    near, first = lax.optimization_barrier((hidden_in, first))
+    (hidden_all,) = remote_call(
         gather_kernel,
         chips,
-        [hidden_in, far],
-        [
-            ((group, width), jnp.bfloat16, True),
-            ((2 * group, width + extra), jnp.bfloat16, True),
-        ],
-        gather_scratch(chips, False) + gather_scratch(chips, True),
+        [near],
+        [((group, width), jnp.bfloat16, True)],
+        gather_scratch(chips, False),
         0,
-        75,
-    )
-    hidden_all, far_all, routed_came, down_came = lax.optimization_barrier(
-        (hidden_all, far_all, routed_came, down_came)
-    )
-    weight_down = ordered(above, down, down_came, 0)
-    routed_up = ordered(side_by, routed_kept, routed_came, 1)
-    routed_came = lax.ppermute(routed_up, "dp", swap_above)
+        40,
+    )
+    far = jnp.concatenate([grad_own, side], axis=1)
+    far, qkv_full = lax.optimization_barrier((far, qkv_full))
+    near_rows = lax.all_gather(far, "expert", axis=0, tiled=True)
 
     cut = shared_in.reshape(block, 2, parts, size, shared_block)
     cut = cut.transpose(3, 0, 1, 2, 4).reshape(size, block, 2 * own_shared)
     cut, hidden_all = lax.optimization_barrier((cut, hidden_all))
     cut = lax.all_to_all(cut, "expert", split_axis=0, concat_axis=0, tiled=True)
+    shared_kept, shared_came = aside(units(cut.reshape(size * block, 2 * own_shared), shared_block))
     hidden_all = hidden_all.astype(jnp.float32)
-    grad_rows = far_all[:, :width]
-    routes_all = far_all[:, width : width + top].astype(jnp.int32)
 
     weight_qkv = qkv_full[:, :own_qkv]
     small = qkv_full[:, own_qkv : own_qkv + extra]
@@ -1105,23 +1131,41 @@
             "hqk,khd->qhd", weights_low, value_low, preferred_element_type=jnp.float32
         ).reshape(group, own_heads * HD)
     )
-    part, routed_came = lax.optimization_barrier((bf16(mm(attended, weight_out)), routed_came))
-    shared_kept, shared_came = aside(units(cut.reshape(size * block, 2 * own_shared), shared_block))
+    part = bf16(mm(attended, weight_out))
+    part, near_rows, routed_came, shared_came = lax.optimization_barrier(
+        (part, near_rows, routed_came, shared_came)
+    )
+    routed_up = ordered(side_by, routed_kept, routed_came, 1)
+    routed_came = lax.ppermute(routed_up, "dp", swap_above)
     shared_up = ordered(side_by, shared_kept, shared_came, 1)
     shared_came = lax.ppermute(shared_up, "dp", swap_above)
-    middle, normed_all = remote_call(
+    part, routed_up, shared_up = lax.optimization_barrier((part, routed_up, shared_up))
+    middle, normed_all, far_rows = remote_call(
         middle_kernel,
         chips,
-        [part, hidden_in, gain_two[None, :]],
-        [((rows, width), jnp.float32, False), ((2 * group, width), jnp.bfloat16, True)],
+        [part, hidden_in, gain_two[None, :], near_rows],
+        [
+            ((rows, width), jnp.float32, False),
+            ((2 * group, width), jnp.bfloat16, True),
+            ((group, width + extra), jnp.bfloat16, True),
+        ],
         [pltpu.VMEM((rows, width), jnp.float32), pltpu.VMEM((rows, width), jnp.bfloat16)]
         + scatter_scratch(chips, rows, width, False)
-        + gather_scratch(chips, True),
+        + gather_scratch(chips, True)
+        + aside_scratch(chips),
         1,
         85,
-    )
-
-    normed_all, shared_came = lax.optimization_barrier((normed_all, shared_came))
+        1,
+    )
+
+    normed_all, routed_came, shared_came, down_came = lax.optimization_barrier(
+        (normed_all, routed_came, shared_came, down_came)
+    )
+    weight_down = ordered(above, down, down_came, 0)
+    grad_rows = jnp.concatenate([near_rows[:, :width], far_rows[:, :width]], axis=0)
+    routes_all = jnp.concatenate(
+        [near_rows[:, width : width + top], far_rows[:, width : width + top]], axis=0
+    ).astype(jnp.int32)
     weight_up = jnp.concatenate(
         [
             ordered(above, routed_up, routed_came, 1).reshape(2, half, expert_block, width),
@@ -1157,7 +1201,11 @@
     sent_down = bf16(mm(half_rows(scaled_hidden, 1 - above), grad_rows))
     term_down = mm(half_rows(scaled_hidden, above), grad_rows)
     came_down = lax.ppermute(sent_down, "dp", swap_above)
-    combined = bf16(mm_tn(scaled_hidden, weight_down))
+    near_part = bf16(mm_tn(scaled_hidden[:, :group], weight_down))
+    far_part = bf16(mm_tn(scaled_hidden[:, group:], weight_down))
+    near_sum = lax.psum_scatter(near_part, "expert", scatter_dimension=0, tiled=True)
+    far_sum = lax.psum_scatter(far_part, "expert", scatter_dimension=0, tiled=True)
+    far_came = lax.ppermute(far_sum, "dp", swap_side)
 
     grad_hidden = mm_nt(weight_down, grad_rows)
     product = hidden.astype(jnp.float32) * grad_hidden
@@ -1188,7 +1236,9 @@
     )
     riders = jnp.pad(riders, ((0, 0), (0, extra - riders.shape[1])))
     part = jnp.concatenate([bf16(mm_tn(grad_both_up, weight_up)), riders], axis=1)
-    part, sent_up, sent_down = lax.optimization_barrier((part, sent_up, sent_down))
+    part, sent_up, sent_down, near_part, far_part = lax.optimization_barrier(
+        (part, sent_up, sent_down, near_part, far_part)
+    )
 
     rider = jnp.arange(extra, dtype=jnp.int32)[:, None]
     lane = jnp.arange(128, dtype=jnp.int32)[None, :]
@@ -1197,7 +1247,7 @@
         | ((rider >= 2 * slots) & (rider < 4 * slots) & (lane == 1 + rider % size))
     )
     probs = jnp.pad(
-        rows_of(jnp.concatenate([opener_all, probs_all], axis=1), slot),
+        rows_of(jnp.concatenate([opener_all, probs_all], axis=1), me),
         ((0, 0), (0, 127 - experts)),
     )
     grad_middle, grad_branch, grad_heads, term_norm_two = remote_call(
@@ -1220,7 +1270,7 @@
         90,
     )
     grad_branch, came_up = lax.optimization_barrier((grad_branch, came_up))
-    term_router = mm_tn(rows_of(normed_all, slot), grad_heads)[:, : 1 + experts]
+    term_router = mm_tn(rows_of(normed_all, me), grad_heads)[:, : 1 + experts]
 
     up = bf16(term_up + came_up.astype(jnp.float32))
     quarter = half_width // 2
@@ -1268,7 +1318,9 @@
     back = jnp.concatenate(
         [bf16(mm_tn(normed_one, grad_projected)), out_blocks.reshape(width, out_cols)], axis=1
     )
-    part, back, came_down, side_came = lax.optimization_barrier((part, back, came_down, side_came))
+    part, back, came_down, near_sum, far_sum = lax.optimization_barrier(
+        (part, back, came_down, near_sum, far_sum)
+    )
     back = lax.psum_scatter(back, "dp", scatter_dimension=0, tiled=True)
     grad_out_weight = back[:, own_qkv:].reshape(block, width).astype(jnp.float32)
     input_grad, term_norm_one = remote_call(
@@ -1328,15 +1380,8 @@
         tiled=True,
     )
     small_sum = jnp.sum(small_terms, axis=0)
-    combined, input_grad = lax.optimization_barrier((combined, input_grad))
-    (output,) = remote_call(
-        output_kernel,
-        chips,
-        [combined, middle, valid_rows],
-        [((rows, width), jnp.bfloat16, False)],
-        [pltpu.VMEM((rows, width), jnp.float32)] + scatter_scratch(chips, rows, width, True),
-        4,
-        55,
+    output = bf16(
+        valid_rows * (middle + near_sum.astype(jnp.float32) + far_came.astype(jnp.float32))
     )
     grad_norm1 = small_sum[0]
     grad_norm2 = small_sum[1]

time: 930 us -> 840 us (0.903)
  Pallas kernels: 410 us -> 320 us
  local copies, waits for them, and re-layouts: 141 us -> 125 us
    pallas_call x5 -> x4, Pallas kernels: 410 us -> 320 us  [remote_call(): pl.pallas_call(functools.partial(kernel, chips), out_shape=[jax.ShapeDtyp...]
    all_gather x1, waiting for transfers between devices: 0.01 us -> 23.2 us  [group_device(): lax.all_gather(jnp.concatenate([first, out_weight.reshape(size * block, o...]
    all_to_all x1, waiting for transfers between devices: 21.4 us -> 0.01 us  [group_device(): cut = lax.all_to_all(cut, 'expert', split_axis=0, concat_axis=0, tiled=True)]
    all_to_all x1, waiting for transfers between devices: 0.01 us -> 18.6 us  [group_device(): lax.all_to_all(first, 'expert', split_axis=0, concat_axis=0, tiled=True)]
    ppermute x2, waiting for transfers between devices: 9.63 us -> 0.01 us  [aside(): return (kept, lax.ppermute(given, 'dp', swap_side))]
    unnamed x134 -> x137, local copies, waits for them, and re-layouts: 30.2 us -> 23.1 us
    dot_general x5 -> x6, matrix products: 50.1 us -> 50.9 us  [mm_tn(): lax.dot_general(left, right, (((0,), (0,)), ((), ())), preferred_element_...]
  transfers between devices with their start and end apart: 17 -> 21, of which waited for: 3 -> 4; matrix products, arithmetic and copies ran while one was open for 29% -> 34% of each run, Pallas kernels for 45% -> 39%
where the time goes in v4:
time: 840 us; the launch traced here: 832 us
  Pallas kernels  320 us (38%)
  matrix products  190 us (23%)
  local copies, waits for them, and re-layouts  125 us (15%)
  other arithmetic  81.2 us (10%)
  waiting for transfers between devices  64.3 us (8%)
  starting transfers between devices  36.1 us (4%)
  between operations  15.5 us (2%)
    pallas_call x4, Pallas kernels, remote_call(): pl.pallas_call(functools.partial(kernel, chips), out_shape=[jax.ShapeDtyp...  320 us
    dot_general x5, matrix products, mm_nt(): lax.dot_general(left, right, (((1,), (1,)), ((), ())), preferred_element_...  65 us
    dot_general x6, matrix products, mm(): return jnp.dot(left, right, preferred_element_type=jnp.float32)  59.7 us
    dot_general x6, matrix products, mm_tn(): lax.dot_general(left, right, (((0,), (0,)), ((), ())), preferred_element_...  50.9 us
    all_gather x1, waiting for transfers between devices, group_device(): lax.all_gather(jnp.concatenate([first, out_weight.reshape(size * block, o...  23.2 us
    unnamed x137, local copies, waits for them, and re-layouts  23.1 us
    convert_element_type x3, local copies, waits for them, and re-layouts, group_device(): grad_shared_in = cut.reshape(size, block, 2, parts, shared_block).transpo...  20.4 us
    all_to_all x1, waiting for transfers between devices, group_device(): lax.all_to_all(first, 'expert', split_axis=0, concat_axis=0, tiled=True)  18.6 us
  transfers between devices with their start and end apart: 21, of which 4 were waited for; matrix products, arithmetic and copies ran while one was open for 34% of the time, Pallas kernels for 39%

profile of v4, /device:TPU:0, one launch (start us, length us, event | category | flops | bytes accessed | tf_op | source)
XLA Modules:
  0.0 831.6 jit_solution(14461455253407498816)
XLA Ops:
  14.1 6.6 all-to-all-start
  26.0 18.6 %all-to-all-done = bf16[8,64,896]{2,1,0:T(8,128)(2,1)} async-done(((bf16[8,64,896]{2,1,0:T(8,128)(2,1)}), bf16[8,64,896]{2,1,0:T(8,128)(2,1)}, u32[]{:S(2)}, u32[]{:S(2)}) %all-to-all-start) | async-done | bytes 917536 | tf_op jit(solution)/shard_map/all_to_all | solution.py:1034
  56.7 5.8 reshape.468
  65.0 3.2 reshape.469
  69.0 42.5 %shard_map.246 = bf16[1024,2048]{1,0:T(8,128)(2,1)} custom-call(bf16[128,2048]{1,0:T(8,128)(2,1)} %hidden.3), custom_call_target="tpu_custom_call" | custom-call | flops 40000000000 | bytes 524288 | tf_op jit(solution)/shard_map/pallas_call | solution.py:914
  111.5 4.3 all-to-all-start.1
  118.5 23.2 %all-gather.3.cloned.1.call-done = bf16[2048,1152]{0,1:T(8,128)(2,1)} async-done(((bf16[512,1152]{0,1:T(8,128)(2,1)}), bf16[2048,1152]{0,1:T(8,128)(2,1)}) %all-gather.3.cloned.1.call-update) | async-done | bytes 4718608 | tf_op jit(solution)/shard_map/all_gather | solution.py:1037
  148.1 3.9 fusion.1
  152.0 8.3 %reshape_reshape.10 = bf16[512,2,2,2,176]{4,3,2,1,0:T(2,128)(2,1)S(1)} reshape(bf16[8,64,1408]{2,1,0:T(8,128)(2,1)} %all-to-all-done.1) | data formatting | bytes 2883584 | tf_op jit(solution)/shard_map/reshape;reshape | solution.py:1048
  160.3 4.0 copy.218
  171.4 7.4 fusion.18
  192.7 3.3 convolution_convert_fusion.2.part
  202.8 102.1 %shard_map.247 = (f32[128,2048]{1,0:T(8,128)}, bf16[2048,2048]{1,0:T(8,128)(2,1)}, bf16[1024,2176]{1,0:T(8,128)(2,1)}) custom-call(bf16[1024,2048]{1,0:T(8,128)(2,1)} %convolution_convert_fusion.2.part, bf16[128,2048]{1,0:T(8,128)(2,1)} %hidden.3, f32[1,2048]{1,0:T(1,128)} %get-tuple-element.159.gain, bf16[1024,2176]{1,0:T(8,128)(2,1)} %all-gather.5.cloned.1.call-done.near), custom_call_target="tpu_custom_call" | custom-call | flops 85000003584 | bytes 9183232 | tf_op jit(solution)/shard_map/pallas_call | solution.py:914
  306.0 5.0 slice.149
  314.0 6.2 fusion.46
  322.9 3.8 broadcast_select_fusion.1
  329.2 4.1 pad_maximum_fusion.1
  333.4 25.0 %fusion.86 = f32[2112,2048]{1,0:T(8,128)} fusion(bf16[2112,2048]{1,0:T(8,128)(2,1)} %bitcast.188, bf16[2048,2048]{1,0:T(8,128)(2,1)} %get-tuple-element.59), kind=kOutput, calls=%fused_computation.230 | convolution fusion | flops 17716740096 | bytes 34340864 | tf_op jit(solution)/shard_map/dot_general | solution.py:943
  358.4 5.0 broadcast_select_fusion.5
  364.5 27.0 %multiply_convert_fusion.2 = (bf16[1056,2048]{1,0:T(8,128)(2,1)}, bf16[1056,2048]{1,0:T(8,128)(2,1)}, f32[2048]{0:T(1024)S(1)}, f32[2048]{0:T(1024)S(1)}, bf16[1056,2048]{1,0:T(8,128)(2,1)S(1)}) fusion(f32[2112,2048]{1,0:T(8,128)} %fusion.86, f32[2048]{0:T(1024)S(1)} %bitcast.219, f32[2048]{0:T(1024)S(1)} %mul.243, pred[1056]{0:T(1024)(128)(4,1)S(1)} %copy-done.38, ...), kind=kOutput, calls=%fused_computation.14 | convolution fusion | flops 8935698432 | bytes 43025440 | tf_op jit(solution)/shard_map/dot_general | solution.py:943
  394.7 7.4 convolution_convert_fusion.4
  402.2 15.7 %convolution_convert_fusion.1 = bf16[2112,1024]{1,0:T(8,128)(2,1)} fusion(bf16[2048,2048]{1,0:T(8,128)(2,1)} %get-tuple-element.59, s32[]{:T(128)S(6)} %select_n.282, bf16[1056,2048]{1,0:T(8,128)(2,1)} %get-tuple-element.150, bf16[1056,2048]{1,0:T(8,128)(2,1)} %get-tuple-element.149), kind=kOutput, calls=%fused_computation.28 | convolution fusion | flops 8877834240 | bytes 17170436 | tf_op jit(solution)/shard_map/dot_general | solution.py:939
  419.0 8.5 %convolution_convert_fusion.7 = bf16[528,2048]{1,0:T(8,128)(2,1)} fusion(bf16[1024,2048]{1,0:T(8,128)(2,1)S(1)} %copy-done.13, bf16[1024,2048]{1,0:T(8,128)(2,1)} %slice.148, bf16[1056,2048]{1,0:T(8,128)(2,1)S(1)} %bitcast.202, s32[]{:T(128)S(6)} %select_n.283), kind=kOutput, calls=%fused_computation.43 | convolution fusion | flops 4447043584 | bytes 12713988 | tf_op jit(solution)/shard_map/dot_general | solution.py:939
  431.2 24.3 %convolution_convert_fusion = bf16[2048,2048]{1,0:T(8,128)(2,1)} fusion(bf16[2112,2048]{1,0:T(8,128)(2,1)S(1)} %bitcast.191, bf16[1056,2048]{1,0:T(8,128)(2,1)} %get-tuple-element.150, bf16[1056,2048]{1,0:T(8,128)(2,1)} %get-tuple-element.149), kind=kOutput, calls=%fused_computation.25 | convolution fusion | flops 17738235904 | bytes 25690112 | tf_op jit(solution)/shard_map/dot_general | solution.py:949
  455.5 8.0 pad_maximum_fusion.part
  463.5 9.2 %convolution_convert_fusion.5 = bf16[1024,2048]{1,0:T(8,128)(2,1)} fusion(bf16[1056,2048]{1,0:T(8,128)(2,1)} %copy-done.10, bf16[528,2048]{1,0:T(8,128)(2,1)} %get-tuple-element.162, bf16[528,2048]{1,0:T(8,128)(2,1)S(1)} %copy-done.19), kind=kOutput, calls=%fused_computation.39 | convolution fusion | flops 4439932928 | bytes 10682368 | tf_op jit(solution)/shard_map/dot_general | solution.py:949
  473.6 130.2 %shard_map.248 = (f32[128,2048]{1,0:T(8,128)}, bf16[1024,2048]{1,0:T(8,128)(2,1)}, bf16[128,128]{1,0:T(8,128)(2,1)}, f32[1,2048]{1,0:T(1,128)}) custom-call(bf16[2048,2176]{1,0:T(8,128)(2,1)} %pad_maximum_fusion.part, f32[128,2048]{1,0:T(8,128)} %get-tuple-element.55.middle, f32[1,2048]{1,0:T(1,128)} %get-tuple-element.159.gain, ...), custom_call_target="tpu_custom_call" | custom-call | flops 89999998976 | bytes 11116544 | tf_op jit(solution)/shard_map/pallas_call | solution.py:914
  605.1 3.6 convolution_convert_fusion.8
  611.7 4.2 multiply_reduce_fusion
  625.8 5.0 convolution_convert_fusion.6
  630.9 5.5 convolution_convert_fusion.3.part
  637.8 4.5 pad_maximum_fusion.6
  642.4 15.6 %add_convert_fusion = bf16[2112,1024]{1,0:T(8,128)(2,1)} fusion(bf16[2112,1024]{1,0:T(8,128)(2,1)} %collective-permute-done.6, bf16[2048,2048]{1,0:T(8,128)(2,1)} %get-tuple-element.59, s32[]{:T(128)S(6)} %select_n.295, bf16[1056,2048]{1,0:T(8,128)(2,1)} %get-tuple-element.150, bf16[1056,2048]{1,0:T(8,128)(2,1)} %get-tuple-element.149), kind=kOutput, calls=%fused_computation.9 | convolution fusion | flops 8882159616 | bytes 21495812 | tf_op jit(solution)/shard_map/dot_general | solution.py:939
  661.3 3.5 collective-permute-start.10
  664.8 45.7 %shard_map.249 = (bf16[128,2048]{1,0:T(8,128)(2,1)}, f32[1,2048]{1,0:T(1,128)}) custom-call(bf16[1024,2048]{1,0:T(8,128)(2,1)} %convolution_convert_fusion.3.part, bf16[128,2048]{1,0:T(8,128)(2,1)} %hidden.3, f32[1,2048]{1,0:T(1,128)} %get-tuple-element.158.gain, f32[128,2048]{1,0:T(8,128)} %get-tuple-element.69.grad_middle), custom_call_target="tpu_custom_call" | custom-call | flops 40000000000 | bytes 5775360 | tf_op jit(solution)/shard_map/pallas_call | solution.py:914
  712.3 3.7 all-to-all-start.2
  716.0 15.2 %collective-permute-done.10 = bf16[2112,512]{1,0:T(8,128)(2,1)} collective-permute-done((bf16[2112,512]{1,0:T(8,128)(2,1)S(1)}, bf16[2112,512]{1,0:T(8,128)(2,1)}, u32[]{:S(2)}, u32[]{:S(2)}) %collective-permute-start.10) | collective-permute-done | bytes 2162720 | tf_op jit(solution)/shard_map/ppermute | solution.py:1278
  736.8 6.0 copy.239
  742.9 6.4 reshape.491
  749.2 4.7 all-to-all-start.4
  753.9 4.7 fusion.8
  758.6 6.2 copy.241
  764.9 9.3 %convert_add_fusion = f32[528,2048]{1,0:T(8,128)S(1)} fusion(bf16[528,2048]{1,0:T(8,128)(2,1)} %collective-permute-done.8, bf16[1024,2048]{1,0:T(8,128)(2,1)} %slice.149, bf16[1024,2048]{1,0:T(8,128)(2,1)} %slice.148, bf16[1056,2048]{1,0:T(8,128)(2,1)} %copy-done.10, s32[]{:T(128)S(6)} %select_n.300), kind=kOutput, calls=%fused_computation.31 | convolution fusion | flops 4448124928 | bytes 17039364 | tf_op jit(solution)/shard_map/dot_general | solution.py:939
  781.9 7.2 all-to-all-done.4
  789.1 3.8 all-to-all-start.3
  796.8 8.4 %reshape.501 = f32[8,64,2,4,176]{4,3,2,1,0:T(4,128)} reshape(bf16[8,64,1408]{2,1,0:T(8,128)(2,1)} %all-to-all-done.4) | data formatting | bytes 4325376 | tf_op jit(solution)/shard_map/convert_element_type | solution.py:1357
  805.2 6.6 copy.240
  811.8 5.5 reshape.498
  (316 shorter events, 128.4 us)
Async XLA Ops:
  8.0 12.8 %copy-start.34 = (bf16[64,2048]{1,0:T(8,128)(2,1)S(1)}, bf16[64,2048]{1,0:T(8,128)(2,1)}, u32[]{:S(2)}) copy-start(bf16[64,2048]{1,0:T(8,128)(2,1)} %param.22) | copy-start | bytes 786436
  14.1 30.5 %all-to-all-start = ((bf16[8,64,896]{2,1,0:T(8,128)(2,1)}), bf16[8,64,896]{2,1,0:T(8,128)(2,1)}, u32[]{:S(2)}, u32[]{:S(2)}) async-start(bf16[8,64,896]{2,1,0:T(8,128)(2,1)} %pad_maximum_fusion.26), calls=%async_computation | async-start | bytes 1835008 | tf_op jit(solution)/shard_map/all_to_all | solution.py:1034
  20.7 121.0 %all-gather.3.cloned.1.call-start = ((), (), s32[]{:S(2)}) async-start(), calls=%async_computation.8 | async-start | bytes 5898240 | tf_op jit(solution)/shard_map/all_gather | solution.py:1037
  25.9 29.1 %copy-start.4 = (bf16[2,2,2,352,512]{4,3,2,1,0:T(8,128)(2,1)}, bf16[2,2,2,352,512]{4,3,2,1,0:T(8,128)(2,1)S(1)}, u32[]{:S(2)}) copy-start(bf16[2,2,2,352,512]{4,3,2,1,0:T(8,128)(2,1)S(1)} %copy.217) | copy-start | bytes 8650756
  49.1 7.4 copy-start.50
  50.4 145.6 %collective-permute-start.1 = (bf16[1408,512]{1,0:T(8,128)(2,1)}, bf16[1408,512]{1,0:T(8,128)(2,1)}, u32[]{:S(2)}, u32[]{:S(2)}) collective-permute-start(bf16[1408,512]{1,0:T(8,128)(2,1)} %dynamic-slice_bitcast_fusion), channel_id=1, source_target_pairs={{0,8},{8,0},{16,24},{24,16},{1,9},{9,1},{17,25},{25,17},{2,10},{10... | collective-permute-start | bytes 4325384 | tf_op jit(solution)/shard_map/ppermute | solution.py:1054
  55.0 258.9 %collective-permute-start.5 = (bf16[528,2048]{1,0:T(8,128)(2,1)}, bf16[528,2048]{1,0:T(8,128)(2,1)}, u32[]{:S(2)}, u32[]{:S(2)}) collective-permute-start(bf16[528,2048]{1,0:T(8,128)(2,1)} %pad_maximum_fusion.18), channel_id=1, source_target_pairs={{0,16},{8,24},{16,0},{24,8},{1,17},{9,25},{17,1},{25,9},{2,18},{10... | collective-permute-start | bytes 6488072 | tf_op jit(solution)/shard_map/ppermute | solution.py:1045
  69.0 47.4 %copy-start.44 = (s32[128,4]{0,1:T(4,128)S(1)}, s32[128,4]{0,1:T(4,128)}, u32[]{:S(2)}) copy-start(s32[128,4]{0,1:T(4,128)} %param.18) | copy-start | bytes 6148
  69.0 47.6 %copy-start.32 = (bf16[128,2048]{1,0:T(8,128)(2,1)S(1)}, bf16[128,2048]{1,0:T(8,128)(2,1)}, u32[]{:S(2)}) copy-start(bf16[128,2048]{1,0:T(8,128)(2,1)} %param.16) | copy-start | bytes 1572868
  111.5 40.5 %all-to-all-start.1 = ((bf16[8,64,1408]{2,1,0:T(8,128)(2,1)}), bf16[8,64,1408]{2,1,0:T(8,128)(2,1)}, u32[]{:S(2)}, u32[]{:S(2)}) async-start(bf16[8,64,1408]{2,1,0:T(8,128)(2,1)} %reshape.469), calls=%async_computation.1 | async-start | bytes 2883584 | tf_op jit(solution)/shard_map/all_to_all | solution.py:1080
  115.8 80.2 %all-gather.5.cloned.1.call-start = ((), (), s32[]{:S(2)}) async-start(), calls=%async_computation.9 | async-start | bytes 5013504 | tf_op jit(solution)/shard_map/all_gather | solution.py:1075
  116.6 30.3 %copy-start.45 = (f32[128]{0:T(128)}, f32[128]{0:T(128)S(1)}, u32[]{:S(2)}) copy-start(f32[128]{0:T(128)S(1)} %dynamic-slice.3) | copy-start | bytes 1540
  141.7 500.6 %reduce-scatter.6.cloned.1.call-start = ((), (), s32[]{:S(2)}) async-start(), calls=%async_computation.11 | async-start | bytes 4718592 | tf_op jit(solution)/shard_map/reduce_scatter | solution.py:1207
  148.1 37.7 %copy-start.1 = (pred[1024,1024]{0,1:T(8,128)(4,1)}, pred[1024,1024]{0,1:T(8,128)(4,1)S(1)}, u32[]{:S(2)}) copy-start(pred[1024,1024]{0,1:T(8,128)(4,1)S(1)} %compare_and_fusion) | copy-start | bytes 3145732
  151.9 19.5 %copy-start.42 = (f32[1024]{0:T(1024)}, f32[1024]{0:T(1024)S(1)}, u32[]{:S(2)}) copy-start(f32[1024]{0:T(1024)S(1)} %add_rsqrt_fusion) | copy-start | bytes 12292
  166.4 29.6 %collective-permute-start.2 = (bf16[704,512]{1,0:T(8,128)(2,1)}, bf16[704,512]{1,0:T(8,128)(2,1)}, u32[]{:S(2)}, u32[]{:S(2)}) collective-permute-start(bf16[704,512]{1,0:T(8,128)(2,1)} %dynamic-slice_bitcast_fusion.1), channel_id=1, source_target_pairs={{0,8},{8,0},{16,24},{24,16},{1,9},{9,1},{17,25},{25,17},{2,10},{10... | collective-permute-start | bytes 2162696 | tf_op jit(solution)/shard_map/ppermute | solution.py:1054
  169.8 21.6 %collective-permute-start = (bf16[2,64,2048]{2,1,0:T(8,128)(2,1)S(1)}, bf16[2,64,2048]{2,1,0:T(8,128)(2,1)S(1)}, u32[]{:S(2)}, u32[]{:S(2)}) collective-permute-start(bf16[2,64,2048]{2,1,0:T(8,128)(2,1)S(1)} %constant_dynamic-slice_fusion.1), channel_id=1, source_target_pairs={{0,1},{1,0},{2,3},{3,2},{4,5},{5,4},{6,7},{7,6},{8,9},{9,8},{10,11... | collective-permute-start | bytes 1572872 | tf_op jit(solution)/shard_map/ppermute | solution.py:1102
  171.4 7.4 copy-start.39
  178.8 6.9 copy-start.6
  199.4 114.5 %collective-permute-start.3 = (bf16[1408,1024]{1,0:T(8,128)(2,1)S(1)}, bf16[1408,1024]{1,0:T(8,128)(2,1)}, u32[]{:S(2)}, u32[]{:S(2)}) collective-permute-start(bf16[1408,1024]{1,0:T(8,128)(2,1)S(1)} %pad_maximum_fusion.8), channel_id=1, source_target_pairs={{0,16},{8,24},{16,0},{24,8},{1,17},{9,25},{17,1},{25,9},{2,18},{10... | collective-permute-start | bytes 8650760 | tf_op jit(solution)/shard_map/ppermute | solution.py:1139
  202.2 111.7 %collective-permute-start.4 = (bf16[704,1024]{1,0:T(8,128)(2,1)}, bf16[704,1024]{1,0:T(8,128)(2,1)}, u32[]{:S(2)}, u32[]{:S(2)}) collective-permute-start(bf16[704,1024]{1,0:T(8,128)(2,1)} %pad_maximum_fusion.19), channel_id=1, source_target_pairs={{0,16},{8,24},{16,0},{24,8},{1,17},{9,25},{17,1},{25,9},{2,18},{10... | collective-permute-start | bytes 4325384 | tf_op jit(solution)/shard_map/ppermute | solution.py:1141
  320.2 38.1 %copy-start.37 = (f32[2048,128]{0,1:T(8,128)}, f32[2048,128]{0,1:T(8,128)S(1)}, u32[]{:S(2)}) copy-start(f32[2048,128]{0,1:T(8,128)S(1)} %fusion.46) | copy-start | bytes 3145732
  333.4 25.0 %copy-start.8 = (bf16[1,352,2048]{2,1,0:T(8,128)(2,1)S(1)}, bf16[1,352,2048]{2,1,0:T(8,128)(2,1)}, u32[]{:S(2)}) copy-start(bf16[1,352,2048]{2,1,0:T(8,128)(2,1)} %param.29) | copy-start | bytes 4325380
  333.4 25.0 %copy-start.18 = (bf16[176,2048]{1,0:T(8,128)(2,1)S(1)}, bf16[176,2048]{1,0:T(8,128)(2,1)}, u32[]{:S(2)}) copy-start(bf16[176,2048]{1,0:T(8,128)(2,1)} %param.27) | copy-start | bytes 2162692
  402.1 16.9 %slice-start.8 = ((s8[4325376]{0:T(1024)(128)(4,1)}), s8[131072]{0:T(1024)(128)(4,1)S(1)}, s32[]{:S(2)}) async-start(s8[4325376]{0:T(1024)(128)(4,1)} %bitcast.201), calls=%async_computation.21 | async-start | bytes 262144
  402.1 240.2 %reduce-scatter.4.cloned.1.call-start = ((), (), s32[]{:S(2)}) async-start(), calls=%async_computation.10 | async-start | bytes 4718592 | tf_op jit(solution)/shard_map/reduce_scatter | solution.py:1206
  402.2 16.8 %slice-start.9 = ((s8[4325376]{0:T(1024)(128)(4,1)}), s8[4194304]{0:T(1024)(128)(4,1)S(1)}, s32[]{:S(2)}) async-start(s8[4325376]{0:T(1024)(128)(4,1)} %bitcast.201), calls=%async_computation.22 | async-start | bytes 8388608
  402.2 16.8 %copy-start.13 = (bf16[1024,2048]{1,0:T(8,128)(2,1)S(1)}, bf16[1024,2048]{1,0:T(8,128)(2,1)}, u32[]{:S(2)}) copy-start(bf16[1024,2048]{1,0:T(8,128)(2,1)} %slice.149) | copy-start | bytes 12582916
  402.2 28.9 %slice-start.2 = ((s8[8650752]{0:T(1024)(128)(4,1)}), s8[262144]{0:T(1024)(128)(4,1)S(1)}, s32[]{:S(2)}) async-start(s8[8650752]{0:T(1024)(128)(4,1)} %bitcast.189), calls=%async_computation.15 | async-start | bytes 524288
  402.2 28.9 %slice-start.3 = ((s8[8650752]{0:T(1024)(128)(4,1)}), s8[4194304]{0:T(1024)(128)(4,1)S(1)}, s32[]{:S(2)}) async-start(s8[8650752]{0:T(1024)(128)(4,1)} %bitcast.189), calls=%async_computation.16 | async-start | bytes 8388608
  417.9 10.7 %copy-start.49 = (pred[16]{0:T(512)(128)(4,1)S(1)}, pred[16]{0:T(512)(128)(4,1)}, u32[]{:S(2)}) copy-start(pred[16]{0:T(512)(128)(4,1)} %iota_compare_fusion.7) | copy-start | bytes 52
  417.9 13.3 %slice-start.4 = ((s8[8650752]{0:T(1024)(128)(4,1)}), s8[4194304]{0:T(1024)(128)(4,1)S(1)}, s32[]{:S(2)}) async-start(s8[8650752]{0:T(1024)(128)(4,1)} %bitcast.189), calls=%async_computation.17 | async-start | bytes 8388608
  417.9 187.2 %collective-permute-start.6 = (bf16[2112,1024]{1,0:T(8,128)(2,1)}, bf16[2112,1024]{1,0:T(8,128)(2,1)}, u32[]{:S(2)}, u32[]{:S(2)}) collective-permute-start(bf16[2112,1024]{1,0:T(8,128)(2,1)} %convolution_convert_fusion.1), channel_id=1, source_target_pairs={{0,16},{8,24},{16,0},{24,8},{1,17},{9,25},{17,1},{25,9},{2,18},{10... | collective-permute-start | bytes 12976136 | tf_op jit(solution)/shard_map/ppermute | solution.py:1225
  427.5 214.8 %collective-permute-start.8 = (bf16[528,2048]{1,0:T(8,128)(2,1)}, bf16[528,2048]{1,0:T(8,128)(2,1)}, u32[]{:S(2)}, u32[]{:S(2)}) collective-permute-start(bf16[528,2048]{1,0:T(8,128)(2,1)} %convolution_convert_fusion.7), channel_id=1, source_target_pairs={{0,16},{8,24},{16,0},{24,8},{1,17},{9,25},{17,1},{25,9},{2,18},{10... | collective-permute-start | bytes 6488072 | tf_op jit(solution)/shard_map/ppermute | solution.py:1203
  472.9 306.6 %reduce-scatter.8.cloned.1.call-start = ((), (), s32[]{:S(2)}) async-start(), calls=%async_computation.12 | async-start | bytes 5242880 | tf_op jit(solution)/shard_map/reduce_scatter | solution.py:1324
  473.6 131.5 %copy-start.30 = (bf16[2,128,1024]{2,1,0:T(8,128)(2,1)S(1)}, bf16[2,128,1024]{2,1,0:T(8,128)(2,1)}, u32[]{:S(2)}) copy-start(bf16[2,128,1024]{2,1,0:T(8,128)(2,1)} %copy-done.29) | copy-start | bytes 1572868
  608.8 27.6 %collective-permute-start.7 = (bf16[2,64,2048]{2,1,0:T(8,128)(2,1)S(1)}, bf16[2,64,2048]{2,1,0:T(8,128)(2,1)S(1)}, u32[]{:S(2)}, u32[]{:S(2)}) collective-permute-start(bf16[2,64,2048]{2,1,0:T(8,128)(2,1)S(1)} %select_bitcast_fusion), channel_id=1, source_target_pairs={{0,1},{1,0},{2,3},{3,2},{4,5},{5,4},{6,7},{7,6},{8,9},{9,8},{10,11... | collective-permute-start | bytes 1572872 | tf_op jit(solution)/shard_map/ppermute | solution.py:1314
  622.7 8.1 slice-start.12
  642.4 15.6 %copy-start.47 = (pred[4,2]{0,1:T(4,128)(4,1)S(1)}, pred[4,2]{0,1:T(4,128)(4,1)}, u32[]{:S(2)}) copy-start(pred[4,2]{0,1:T(4,128)(4,1)} %add_compare_fusion) | copy-start | bytes 28
  661.3 69.9 %collective-permute-start.10 = (bf16[2112,512]{1,0:T(8,128)(2,1)S(1)}, bf16[2112,512]{1,0:T(8,128)(2,1)}, u32[]{:S(2)}, u32[]{:S(2)}) collective-permute-start(bf16[2112,512]{1,0:T(8,128)(2,1)S(1)} %constant_dynamic-slice_fusion), channel_id=1, source_target_pairs={{0,8},{8,0},{16,24},{24,16},{1,9},{9,1},{17,25},{25,17},{2,10},{10... | collective-permute-start | bytes 6488072 | tf_op jit(solution)/shard_map/ppermute | solution.py:1278
  664.8 45.7 %copy-start.41 = (f32[1,2048]{1,0:T(1,128)S(1)}, f32[1,2048]{1,0:T(1,128)}, u32[]{:S(2)}) copy-start(f32[1,2048]{1,0:T(1,128)} %get-tuple-element.72) | copy-start | bytes 24580
  712.3 37.0 %all-to-all-start.2 = ((f32[32,1,896]{2,1,0:T(1,128)}), f32[32,1,896]{2,1,0:T(1,128)S(1)}, u32[]{:S(2)}, u32[]{:S(2)}) async-start(f32[32,1,896]{2,1,0:T(1,128)} %reshape.503), calls=%async_computation.4 | async-start | bytes 229376 | tf_op jit(solution)/shard_map/all_to_all | solution.py:1375
  749.2 39.8 %all-to-all-start.4 = ((bf16[8,64,1408]{2,1,0:T(8,128)(2,1)}), bf16[8,64,1408]{2,1,0:T(8,128)(2,1)}, u32[]{:S(2)}, u32[]{:S(2)}) async-start(bf16[8,64,1408]{2,1,0:T(8,128)(2,1)} %reshape.491), calls=%async_computation.7 | async-start | bytes 2883584 | tf_op jit(solution)/shard_map/all_to_all | solution.py:1346
  775.4 19.4 %copy-start.31 = (f32[128,2048]{1,0:T(8,128)S(1)}, f32[128,2048]{1,0:T(8,128)}, u32[]{:S(2)}) copy-start(f32[128,2048]{1,0:T(8,128)} %get-tuple-element.55.middle) | copy-start | bytes 3145732
  775.4 19.4 %copy-start.33 = (bf16[128,2048]{1,0:T(8,128)(2,1)S(1)}, bf16[128,2048]{1,0:T(8,128)(2,1)}, u32[]{:S(2)}) copy-start(bf16[128,2048]{1,0:T(8,128)(2,1)} %reduce-scatter.4.cloned.1.call-done) | copy-start | bytes 1572868
  775.4 19.4 %copy-start.46 = (f32[128]{0:T(128)S(1)}, f32[128]{0:T(128)}, u32[]{:S(2)}) copy-start(f32[128]{0:T(128)} %copy-done.45) | copy-start | bytes 1540
  775.4 19.4 %collective-permute-start.9 = (bf16[128,2048]{1,0:T(8,128)(2,1)}, bf16[128,2048]{1,0:T(8,128)(2,1)}, u32[]{:S(2)}, u32[]{:S(2)}) collective-permute-start(bf16[128,2048]{1,0:T(8,128)(2,1)} %reduce-scatter.6.cloned.1.call-done), channel_id=1, source_target_pairs={{0,8},{8,0},{16,24},{24,16},{1,9},{9,1},{17,25},{25,17},{2,10},{10... | collective-permute-start | bytes 1572872 | tf_op jit(solution)/shard_map/ppermute | solution.py:1208
  789.1 30.3 %all-to-all-start.3 = ((bf16[8,64,768]{2,1,0:T(8,128)(2,1)}), bf16[8,64,768]{2,1,0:T(8,128)(2,1)S(1)}, u32[]{:S(2)}, u32[]{:S(2)}) async-start(bf16[8,64,768]{2,1,0:T(8,128)(2,1)} %bitcast.57), calls=%async_computation.6 | async-start | bytes 1572864 | tf_op jit(solution)/shard_map/all_to_all | solution.py:1359
  (40 other events, 139.6 us)
Sparse Core Ops, SparseCore 0:
  49.3 92.3 all-gather.2
  143.3 47.9 all-gather.4
  402.3 48.8 reduce-scatter.5
  473.0 71.2 reduce-scatter.3
  642.5 76.2 reduce-scatter.7

commit v5 on v2

--- a/solution.py
+++ b/solution.py
@@ -553,7 +553,7 @@
         body(pl.ds(pl.multiple_of(index * STRIP, STRIP), STRIP))
 
 
-def scatter_line(line, part, total, held, come, pair_send, pair_recv, send, recv):
+def scatter_line(line, part, total, held, come, pair_send, pair_recv, send, recv, aside=None):
     chips, z, core = line.chips, line.z, line.core
     rows = total.shape[0]
 
@@ -585,6 +585,8 @@
         first = start_of(chip, core)
         mine = part[pl.ds(pl.multiple_of(first + strip.start, STRIP), STRIP), :]
         summed = mine.astype(jnp.float32) + held[chip, strip, :].astype(jnp.float32)
+        if aside is not None:
+            summed = summed + aside[chip, strip, :].astype(jnp.float32)
         for way in ways:
             summed = summed + come[way, chip, strip, :].astype(jnp.float32)
         return summed
@@ -594,14 +596,6 @@
             held[chip, strip, :] = value(chip, strip, ways).astype(jnp.bfloat16)
 
         strips(rows, body)
-
-    order = []
-    for near in range((chips + 1) // 2):
-        for chip in (chips - 1 - near, near):
-            if chip not in order:
-                order.append(chip)
-    for chip in order:
-        across(chip).start()
 
     def forward(chip, up):
         across(chip).wait_recv()
@@ -628,10 +622,14 @@
     def down_sends(step):
         return (step >= chips - 1 - z) & line.below
 
-    for step in range(chips - 1):
-        pl.when(up_sends(step))(lambda step=step: forward(up_chip(step), True))
-        pl.when(down_sends(step))(lambda step=step: forward(down_chip(step), False))
-
+    def each(act):
+        for step in range(chips - 1):
+            pl.when(up_sends(step))(lambda step=step: act(up_chip(step), True))
+            pl.when(down_sends(step))(lambda step=step: act(down_chip(step), False))
+
+    each(lambda chip, up: across(chip).start())
+    across(z).start()
+    each(forward)
     across(z).wait_recv()
     pl.when(line.below)(lambda: hop(z, True, z).wait_recv())
     pl.when(line.above)(lambda: hop(z, False, z).wait_recv())
@@ -646,15 +644,13 @@
     pl.when(inner)(lambda: last((0, 1)))
     pl.when(jnp.logical_not(line.below))(lambda: last((1,)))
     pl.when(jnp.logical_not(line.above))(lambda: last((0,)))
-    for chip in order:
+
+    def settle(chip, up):
         across(chip).wait_send()
-    for step in range(chips - 1):
-        pl.when(up_sends(step))(
-            lambda step=step: hop(up_chip(step), True, z + 1).wait_send()
-        )
-        pl.when(down_sends(step))(
-            lambda step=step: hop(down_chip(step), False, z - 1).wait_send()
-        )
+        hop(chip, up, z + 1 if up else z - 1).wait_send()
+
+    each(settle)
+    across(z).wait_send()
 
 
 def gather_kernel(chips, own, out, *scratch):
@@ -678,12 +674,12 @@
 
 
 def branch_kernel(
-    chips, part, middle, gain, out_grad, probs, collect, router,
+    chips, part, aside, middle, gain, out_grad, probs, collect, router,
     grad_middle, grad_all, heads, term, total, turned, *scratch
 ):
     line = Line(chips)
     line.meet()
-    scatter_line(line, part, total, *scratch[:6])
+    scatter_line(line, part, total, *scratch[:6], aside=aside)
     width = middle.shape[1]
     term[...] = jnp.zeros_like(term)
 
@@ -739,16 +735,191 @@
     strips(hidden.shape[0], body)
 
 
-def output_kernel(chips, part, middle, valid, output, total, *scratch):
-    line = Line(chips)
-    line.meet()
-    scatter_line(line, part, total, *scratch)
-
-    def body(strip):
-        rows = valid[strip, :] * (middle[strip, :] + total[strip, :])
-        output[strip, :] = rows.astype(jnp.bfloat16)
-
-    strips(middle.shape[0], body)
+UNIT_STRIP = 16
+
+
+def nt_dot(left, right):
+    return lax.dot_general(
+        left, right, (((1,), (1,)), ((), ())), preferred_element_type=jnp.float32
+    )
+
+
+def experts_kernel(experts, top, split, near, place, normed, grads, side, router, down, *rest):
+    if near:
+        routed, routed_came, shared, shared_came = rest[:4]
+        hidden, grad_up, heads, dots, weight, up, back, scale, sums = rest[4:]
+    else:
+        weight, hidden, grad_up, heads, dots, up, back, scale, sums = rest
+    step = pl.program_id(0)
+    above, me = place[0], place[1]
+    rows = normed.shape[0]
+    units = down.shape[1]
+    width = down.shape[2]
+    chunk = min(256, rows)
+
+    @pl.when(step == 0)
+    def _():
+        logits = nt_dot(router[...], normed[...])
+        row = lax.broadcasted_iota(jnp.int32, logits.shape, 0)
+        opener = jax.nn.sigmoid(logits)
+        choice = jnp.where((row >= 1) & (row <= experts), logits, NEG_FILL)
+        peak = jnp.max(choice, axis=0, keepdims=True)
+        total = peak + jnp.log(jnp.sum(jnp.exp(choice - peak), axis=0, keepdims=True))
+        probs = jnp.exp(choice - total)
+        heads[...] = jnp.where(row == 0, opener, probs)
+        names = side[...].astype(jnp.float32)
+        lane = lax.broadcasted_iota(jnp.int32, names.shape, 1)
+        match = jnp.where(
+            (lane < top) & (names == me.astype(jnp.float32)), 1.0, 0.0
+        ).astype(jnp.bfloat16)
+        named = nt_dot(jnp.ones((16, names.shape[1]), jnp.bfloat16), match)[0:1]
+        own = jnp.sum(jnp.where(row == me + 1, probs, 0.0), axis=0, keepdims=True)
+        scale[0:1, :] = named * own
+        scale[1:2, :] = opener[0:1]
+        scale[2:3, :] = named
+        sums[...] = jnp.zeros_like(sums)
+
+    if near:
+        first = pl.multiple_of(above * (width // 2), 128)
+        second = pl.multiple_of((1 - above) * (width // 2), 128)
+        cut = routed.shape[2]
+        for kind in range(2):
+            weight[kind, 0, :cut, pl.ds(first, width // 2)] = routed[kind, 0]
+            weight[kind, 0, :cut, pl.ds(second, width // 2)] = routed_came[kind, 0]
+            weight[kind, 0, cut:, pl.ds(first, width // 2)] = shared[kind, 0]
+            weight[kind, 0, cut:, pl.ds(second, width // 2)] = shared_came[kind, 0]
+
+    @pl.loop(0, rows // chunk)
+    def _(index):
+        span = pl.ds(pl.multiple_of(index * chunk, chunk), chunk)
+        for kind in range(2):
+            up[kind, :, span] = nt_dot(weight[kind, 0], normed[span, :])
+        back[:, span] = nt_dot(down[0], grads[span, :])
+
+    def part(first, last, which):
+        @pl.loop(first // UNIT_STRIP, last // UNIT_STRIP)
+        def _(index):
+            strip = pl.ds(pl.multiple_of(index * UNIT_STRIP, UNIT_STRIP), UNIT_STRIP)
+            gate = up[0, strip, :]
+            value = up[1, strip, :]
+            grad = back[strip, :]
+            sigmoid = jax.nn.sigmoid(gate)
+            act = gate * sigmoid
+            unit = (act * value).astype(jnp.bfloat16)
+            wide = unit.astype(jnp.float32)
+            factor = scale[which : which + 1, :]
+            hidden[0, strip, :] = (wide * factor).astype(jnp.bfloat16)
+            product = wide * grad
+            sums[which, :, :] += product[:8] + product[8:]
+            grad = grad * factor
+            slope = grad * value * sigmoid * (1.0 + gate * (1.0 - sigmoid))
+            grad_up[0, 0, strip, :] = slope.astype(jnp.bfloat16)
+            grad_up[1, 0, strip, :] = (grad * act).astype(jnp.bfloat16)
+
+    part(0, split, 0)
+    part(split, units, 1)
+
+    @pl.when(step == pl.num_programs(0) - 1)
+    def _():
+        routed_dot = scale[2:3, :] * jnp.sum(sums[0], axis=0, keepdims=True)
+        shared_dot = jnp.sum(sums[1], axis=0, keepdims=True)
+        row = lax.broadcasted_iota(jnp.int32, (16, rows), 0)
+        both = jnp.where(row < 2, shared_dot, routed_dot)
+        high = both.astype(jnp.bfloat16).astype(jnp.float32)
+        value = jnp.where((row == 0) | (row == 2), high, both - high)
+        dots[...] = jnp.where(row < 4, value, 0.0).astype(jnp.bfloat16)
+
+
+def experts_call(place, normed, grads, side, router, down, weights, experts, top, split):
+    rows, width = normed.shape
+    steps, units = down.shape[:2]
+    near = len(weights) == 4
+
+    def whole(shape):
+        return pl.BlockSpec(
+            shape, lambda i, place: (0,) * len(shape), pipeline_mode=pl.Buffered(1)
+        )
+
+    def piece(array):
+        return pl.BlockSpec(
+            (2, 1) + array.shape[2:],
+            lambda i, place: (0, place[0] + i - 2 * place[0] * i, 0, 0),
+        )
+
+    full = pl.BlockSpec((2, 1, units, width), lambda i, place: (0, i, 0, 0))
+    outs = [
+        jax.ShapeDtypeStruct((steps, units, rows), jnp.bfloat16),
+        jax.ShapeDtypeStruct((2, steps, units, rows), jnp.bfloat16),
+        jax.ShapeDtypeStruct((16, rows), jnp.float32),
+        jax.ShapeDtypeStruct((16, rows), jnp.bfloat16),
+    ]
+    out_specs = [
+        pl.BlockSpec((1, units, rows), lambda i, place: (i, 0, 0)),
+        pl.BlockSpec((2, 1, units, rows), lambda i, place: (0, i, 0, 0)),
+        pl.BlockSpec((16, rows), lambda i, place: (0, 0)),
+        pl.BlockSpec((16, rows), lambda i, place: (0, 0)),
+    ]
+    if near:
+        outs.append(jax.ShapeDtypeStruct((2, steps, units, width), jnp.bfloat16))
+        out_specs.append(full)
+    return pl.pallas_call(
+        functools.partial(experts_kernel, experts, top, split, near),
+        out_shape=outs,
+        grid_spec=pltpu.PrefetchScalarGridSpec(
+            num_scalar_prefetch=1,
+            grid=(steps,),
+            in_specs=[
+                whole(normed.shape),
+                whole(grads.shape),
+                whole(side.shape),
+                whole(router.shape),
+                pl.BlockSpec((1, units, width), lambda i, place: (i, 0, 0)),
+            ]
+            + ([piece(array) for array in weights] if near else [full]),
+            out_specs=out_specs,
+            scratch_shapes=[
+                pltpu.VMEM((2, units, rows), jnp.float32),
+                pltpu.VMEM((units, rows), jnp.float32),
+                pltpu.VMEM((8, rows), jnp.float32),
+                pltpu.VMEM((2, 8, rows), jnp.float32),
+            ],
+        ),
+        cost_estimate=pl.CostEstimate(
+            flops=int(4e9), bytes_accessed=int(1e6), transcendentals=0
+        ),
+    )(place, normed, grads, side, router, down, *weights)
+
+
+def weight_grad_kernel(place, left, right, *rest):
+    *plus, out = rest
+    total = jnp.dot(left[...], right[...], preferred_element_type=jnp.float32)
+    if plus:
+        total = total + plus[0][...].astype(jnp.float32)
+    out[...] = total.astype(jnp.bfloat16)
+
+
+def weight_grad(column, left, right, plus=None):
+    count, rows = left.shape
+    width = right.shape[1] // 2
+    tile = count // 6
+    tiled = pl.BlockSpec((tile, width), lambda i, column: (i, 0))
+    return pl.pallas_call(
+        weight_grad_kernel,
+        out_shape=jax.ShapeDtypeStruct((count, width), jnp.bfloat16),
+        grid_spec=pltpu.PrefetchScalarGridSpec(
+            num_scalar_prefetch=1,
+            grid=(6,),
+            in_specs=[
+                pl.BlockSpec((tile, rows), lambda i, column: (i, 0)),
+                pl.BlockSpec((rows, width), lambda i, column: (0, column[0])),
+            ]
+            + ([tiled] if plus is not None else []),
+            out_specs=tiled,
+        ),
+        cost_estimate=pl.CostEstimate(
+            flops=int(3e9), bytes_accessed=int(1e6), transcendentals=0
+        ),
+    )(column, left, right, *([plus] if plus is not None else []))
 
 
 def remote_call(kernel, chips, inputs, outputs, scratch, number, micros):
@@ -829,10 +1000,17 @@
     shared_block = shared_out.shape[0]
     expert_block = expert_out.shape[1]
     pair_block = expert_block + shared_block
-    hidden_units = parts * pair_block
-    padded = -(-hidden_units // 128) * 128
+    hidden_units = half * pair_block
     own_shared = parts * shared_block
     chips = places
+    data = lax.axis_index("dp")
+    side_by = data % 2
+    above = data // 2
+    slots = 2 * size
+    slot = side_by * size + me
+    swap = [(i, i ^ 1) for i in range(size)]
+    swap_side = [(g, g ^ 1) for g in range(parts)]
+    swap_above = [(g, g ^ 2) for g in range(parts)]
     own_qkv = 3 * own_heads * HD
 
     def by_head(columns):
@@ -845,22 +1023,36 @@
         cut = pieces.reshape(places, 2, count, 3, half, HD)
         return cut.transpose(2, 3, 1, 4, 0, 5).reshape(count, 3 * width)
 
-    side = jnp.pad(bf16(routes), ((0, 0), (0, extra - top)))
-    (gathered,) = remote_call(
-        gather_kernel,
-        chips,
-        [jnp.concatenate([hidden_in, out_grad, side], axis=1)],
-        [((group, 2 * width + extra), jnp.bfloat16, True)],
-        gather_scratch(chips),
-        0,
-        70,
-    )
-    hidden_all = gathered[:, :width].astype(jnp.float32)
-    routes_all = gathered[:, 2 * width : 2 * width + top].astype(jnp.int32)
-
-    weight_down = lax.all_gather(
-        jnp.concatenate([expert_out[0], shared_out], axis=0), "dp", axis=0, tiled=True
-    )
+    def ordered(which, own, other, axis):
+        first = jnp.where(which == 0, own, other)
+        second = jnp.where(which == 0, other, own)
+        return jnp.concatenate([first, second], axis=axis)
+
+    def by_core(values, which):
+        blocks = values.reshape(chips, 2, rows, values.shape[1])
+        blocks = lax.dynamic_index_in_dim(blocks, which, 1, keepdims=False)
+        return blocks.reshape(chips * rows, values.shape[1])
+
+    def beside(values):
+        came = lax.ppermute(by_core(values, core), "dp", swap_side)
+        return jnp.concatenate([came, lax.ppermute(came, "expert", swap)], axis=0)
+
+    def rows_of(values, first):
+        return lax.dynamic_slice_in_dim(values, first * rows, rows, 0)
+
+    down = jnp.concatenate([expert_out[0], shared_out], axis=0)
+    down_came = lax.ppermute(down, "dp", swap_above)
+
+    def units(values, count):
+        cut = values.reshape(size * block, 2, half, 2, count)
+        return cut.transpose(3, 1, 2, 4, 0).reshape(2, 2 * half * count, size * block)
+
+    def aside(values):
+        kept = lax.dynamic_index_in_dim(values, side_by, 0, keepdims=False)
+        given = lax.dynamic_index_in_dim(values, 1 - side_by, 0, keepdims=False)
+        return kept, lax.ppermute(given, "dp", swap_side)
+
+    routed_kept, routed_came = aside(units(expert_in[0], expert_block))
 
     small = jnp.concatenate(
         [
@@ -873,19 +1065,52 @@
         axis=1,
     )
     small = jnp.pad(small, ((0, 0), (0, extra - small.shape[1])))
+    first = jnp.concatenate(
+        [by_head(qkv_weight), jnp.broadcast_to(small[None], (size, block, extra))], axis=2
+    )
+    first = lax.all_to_all(first, "expert", split_axis=0, concat_axis=0, tiled=True)
+    first = first.reshape(size * block, own_qkv + extra)
+    out_cols = width * block // (size * block)
+    qkv_full = lax.all_gather(
+        jnp.concatenate([first, out_weight.reshape(size * block, out_cols)], axis=1),
+        "dp",
+        axis=0,
+        tiled=True,
+    )
+
+    segment, position = segment_table(lengths[0], group)
+    valid_all = (segment < lengths.shape[1] - 1).astype(jnp.float32)[:, None]
+    valid_rows = rows_of(valid_all, me)
+    grad_own = bf16(out_grad.astype(jnp.float32) * valid_rows)
+    side = jnp.pad(bf16(routes), ((0, 0), (0, extra - top)))
     cut = shared_in.reshape(block, 2, parts, size, shared_block)
     cut = cut.transpose(3, 0, 1, 2, 4).reshape(size, block, 2 * own_shared)
-    sent = jnp.concatenate(
-        [by_head(qkv_weight), jnp.broadcast_to(small[None], (size, block, extra)), cut], axis=2
-    )
-    sent = lax.all_to_all(sent, "expert", split_axis=0, concat_axis=0, tiled=True)
-    sent = sent.reshape(size * block, own_qkv + extra + 2 * own_shared)
-    out_cols = width * block // (size * block)
-    first = jnp.concatenate(
-        [sent[:, : own_qkv + extra], out_weight.reshape(size * block, out_cols)], axis=1
-    )
-    first, weight_down = lax.optimization_barrier((first, weight_down))
-    qkv_full = lax.all_gather(first, "dp", axis=0, tiled=True)
+    cut, first = lax.optimization_barrier((cut, first))
+    cut = lax.all_to_all(cut, "expert", split_axis=0, concat_axis=0, tiled=True)
+
+    near = jnp.concatenate([hidden_in, side], axis=1)
+    near, first = lax.optimization_barrier((near, first))
+    (gathered,) = remote_call(
+        gather_kernel,
+        chips,
+        [near],
+        [((group, width + extra), jnp.bfloat16, True)],
+        gather_scratch(chips),
+        0,
+        40,
+    )
+    near_grad, qkv_full = lax.optimization_barrier((grad_own, qkv_full))
+    near_grad = lax.all_gather(near_grad, "expert", axis=0, tiled=True)
+
+    cut, gathered = lax.optimization_barrier((cut, gathered))
+    shared_kept, shared_came = aside(units(cut.reshape(size * block, 2 * own_shared), shared_block))
+    hidden_all = gathered[:, :width].astype(jnp.float32)
+    near_side = gathered[:, width:]
+    far_side = beside(near_side)
+    routed_came, qkv_full = lax.optimization_barrier((routed_came, qkv_full))
+    routed_up = ordered(side_by, routed_kept, routed_came, 1)
+    routed_came = lax.ppermute(routed_up, "dp", swap_above)
+
     weight_qkv = qkv_full[:, :own_qkv]
     small = qkv_full[:, own_qkv : own_qkv + extra]
     gain_one = small[:, 0].astype(jnp.float32)
@@ -894,16 +1119,6 @@
     bias_all = by_head(small[:, 3 + experts : 3 + experts + bias_cols].reshape(1, 3 * width))
     bias_own = lax.dynamic_index_in_dim(bias_all, me, 0, keepdims=False).astype(jnp.float32)
 
-    cut = sent[:, own_qkv + extra :].reshape(size * block, 2, parts, shared_block)
-    up = expert_in[0].reshape(size * block, 2, parts, expert_block)
-    up = jnp.concatenate([up, cut], axis=3).reshape(size * block, 2, hidden_units)
-    up = jnp.pad(up, ((0, 0), (0, 0), (0, padded - hidden_units)))
-    up = up.reshape(size * block, 2 * padded)
-    up, qkv_full = lax.optimization_barrier((up, qkv_full))
-    weight_up = lax.all_gather(up, "dp", axis=0, tiled=True)
-
-    swap = [(i, i ^ 1) for i in range(size)]
-
     def own_half(values):
         return lax.dynamic_slice_in_dim(values, core * half, half, 0)
 
@@ -917,8 +1132,6 @@
         [jnp.where(core == 0, kept, came), jnp.where(core == 0, came, kept)], axis=1
     ).reshape(own_heads * HD, width)
 
-    segment, position = segment_table(lengths[0], group)
-    valid_all = (segment < lengths.shape[1] - 1).astype(jnp.float32)[:, None]
     cosine, sine = rotary_tables(position, HD)
     allowed = (
         (segment[:, None] == segment[None, :]) & (position[:, None] >= position[None, :])
@@ -946,112 +1159,120 @@
             "hqk,khd->qhd", weights_low, value_low, preferred_element_type=jnp.float32
         ).reshape(group, own_heads * HD)
     )
-    middle, normed_all = remote_call(
+    part = bf16(mm(attended, weight_out))
+    far_grad = by_core(near_grad, core)
+    part, far_grad, shared_came = lax.optimization_barrier((part, far_grad, shared_came))
+    far_grad = lax.ppermute(far_grad, "dp", swap_side)
+    shared_up = ordered(side_by, shared_kept, shared_came, 1)
+    shared_came = lax.ppermute(shared_up, "dp", swap_above)
+    part, routed_up, shared_up = lax.optimization_barrier((part, routed_up, shared_up))
+    middle, normed = remote_call(
         middle_kernel,
         chips,
-        [bf16(mm(attended, weight_out)), hidden_in, gain_two[None, :]],
+        [part, hidden_in, gain_two[None, :]],
         [((rows, width), jnp.float32, False), ((group, width), jnp.bfloat16, True)],
         [pltpu.VMEM((rows, width), jnp.float32), pltpu.VMEM((rows, width), jnp.bfloat16)]
         + scatter_scratch(chips, rows, width)
         + gather_scratch(chips),
         1,
-        70,
-    )
-
-    gate_logits = mm_nt(normed_all, router_rows)
-    logits = gate_logits[:, 1 : 1 + experts]
-    opener_all = jax.nn.sigmoid(gate_logits[:, :1])
-    peak_logit = jnp.max(logits, axis=-1, keepdims=True)
-    router_total = peak_logit + jnp.log(
-        jnp.sum(jnp.exp(logits - peak_logit), axis=-1, keepdims=True)
-    )
-    probs_all = jnp.exp(logits - router_total)
-    expert_ids = jnp.arange(experts, dtype=jnp.int32)
-    mine = expert_ids[None, :] == me
-    named = jnp.sum((routes_all == me).astype(jnp.float32), axis=1, keepdims=True)
-    gate_own = named * jnp.sum(jnp.where(mine, probs_all, 0.0), axis=1, keepdims=True)
-
-    routed_unit = (jnp.arange(hidden_units, dtype=jnp.int32) % pair_block < expert_block)[None, :]
-    unit_scale = jnp.where(routed_unit, gate_own, opener_all)
-    grad_rows = bf16(
-        gathered[:, width : 2 * width].astype(jnp.float32) * valid_all
-    )
-    both_up = mm(normed_all, weight_up)
-
-    gate_part = both_up[:, :hidden_units]
-    up_part = both_up[:, padded : padded + hidden_units]
-    hidden = bf16(jax.nn.silu(gate_part) * up_part)
-    scaled_hidden = bf16(unit_scale * hidden.astype(jnp.float32))
-    term_down = bf16(mm_tn(scaled_hidden, grad_rows))
-    grad_down = lax.psum_scatter(term_down, "dp", scatter_dimension=0, tiled=True).astype(
-        jnp.float32
-    )
-    grad_shared_out = grad_down[expert_block:]
-    grad_expert_out = grad_down[None, :expert_block]
-    combined = bf16(mm(scaled_hidden, weight_down))
-
-    grad_hidden = mm_nt(grad_rows, weight_down)
-    product = hidden.astype(jnp.float32) * grad_hidden
-    dot_expert = named * jnp.sum(jnp.where(routed_unit, product, 0.0), axis=1, keepdims=True)
-    dot_shared = jnp.sum(jnp.where(routed_unit, 0.0, product), axis=1, keepdims=True)
-    grad_hidden = grad_hidden * unit_scale
-    sigmoid_gate = jax.nn.sigmoid(gate_part)
-    grad_gate = grad_hidden * up_part * sigmoid_gate * (1.0 + gate_part * (1.0 - sigmoid_gate))
-    grad_up = grad_hidden * gate_part * sigmoid_gate
-    wide = ((0, 0), (0, padded - hidden_units))
-    grad_both_up = jnp.concatenate(
-        [jnp.pad(bf16(grad_gate), wide), jnp.pad(bf16(grad_up), wide)], axis=1
-    )
-    term_up = bf16(mm_tn(normed_all, grad_both_up))
-    up = lax.psum_scatter(term_up, "dp", scatter_dimension=0, tiled=True)
-    up = up.reshape(size * block, 2, padded)[:, :, :hidden_units]
-    up = up.reshape(size * block, 2, parts, pair_block)
-    grad_expert_in = (
-        up[:, :, :, :expert_block]
-        .reshape(1, size * block, 2 * parts * expert_block)
-        .astype(jnp.float32)
-    )
-    cut = lax.all_to_all(
-        up[:, :, :, expert_block:].reshape(size, block, 2 * own_shared),
-        "expert",
-        split_axis=0,
-        concat_axis=0,
-        tiled=True,
-    )
-    grad_shared_in = (
-        cut.reshape(size, block, 2, parts, shared_block)
-        .transpose(1, 2, 3, 0, 4)
-        .reshape(block, 2 * parts * size * shared_block)
-        .astype(jnp.float32)
-    )
-
-    zero = jnp.zeros((), jnp.bfloat16)
-    riders = jnp.concatenate(
+        75,
+    )
+    far_normed = beside(normed)
+    far_grad = jnp.concatenate([far_grad, lax.ppermute(far_grad, "expert", swap)], axis=0)
+    normed, routed_came, shared_came, down_came = lax.optimization_barrier(
+        (normed, routed_came, shared_came, down_came)
+    )
+    weight_down = jnp.stack([down, down_came])
+    place = jnp.stack([above, me]).astype(jnp.int32)
+    cell = jnp.arange(16, dtype=jnp.int32)[:, None]
+    spot = bf16((cell < 4) & (jnp.arange(extra)[None, :] == cell * slots + slot))
+    router_few = router_rows[:16]
+    near_hidden, near_up, near_heads, near_dots, weight_up = experts_call(
+        place,
+        normed,
+        near_grad,
+        near_side,
+        router_few,
+        weight_down,
         [
-            jnp.where(mine, column, zero)
-            for column in two_parts(dot_shared) + two_parts(dot_expert)
+            piece.reshape(2, half, piece.shape[0] // 4, width // 2)
+            for piece in (routed_up, routed_came, shared_up, shared_came)
         ],
-        axis=1,
-    )
-    riders = jnp.pad(riders, ((0, 0), (0, extra - riders.shape[1])))
-    part = jnp.concatenate([bf16(mm_nt(grad_both_up, weight_up)), riders], axis=1)
-
-    def rows_of(values):
-        return lax.dynamic_slice_in_dim(values, me * rows, rows, 0)
+        experts,
+        top,
+        expert_block,
+    )
+    column = place[:1]
+    near_up = near_up.reshape(2 * hidden_units, group)
+    near_hidden = near_hidden.reshape(hidden_units, group)
+    flat_up = weight_up.reshape(2 * hidden_units, width)
+    flat_down = weight_down.reshape(hidden_units, width)
+    near_sent = weight_grad(1 - column, near_up, normed)
+    part = jnp.concatenate([bf16(mm_tn(near_up, flat_up)), bf16(mm_tn(near_dots, spot))], axis=1)
+    near_output = bf16(mm_tn(near_hidden, flat_down))
+    far_normed, far_grad, near_sent, part, near_output = lax.optimization_barrier(
+        (far_normed, far_grad, near_sent, part, near_output)
+    )
+    far_hidden, far_up, _, far_dots = experts_call(
+        place,
+        far_normed,
+        far_grad,
+        far_side,
+        router_few,
+        weight_down,
+        [weight_up],
+        experts,
+        top,
+        expert_block,
+    )
+    far_up = far_up.reshape(2 * hidden_units, group)
+    far_hidden = far_hidden.reshape(hidden_units, group)
+
+    def pair_sum(values):
+        came = lax.ppermute(values[group // 2 :], "expert", swap)
+        return bf16(values[: group // 2].astype(jnp.float32) + came.astype(jnp.float32))
+
+    far_part = jnp.concatenate(
+        [bf16(mm_tn(far_up, flat_up)), bf16(mm_tn(far_dots, spot))], axis=1
+    )
+    far_sum = pair_sum(far_part)
+    sent_up = weight_grad(1 - column, far_up, far_normed, near_sent)
+    far_sum, sent_up, far_hidden, near_hidden, near_up, far_up = lax.optimization_barrier(
+        (far_sum, sent_up, far_hidden, near_hidden, near_up, far_up)
+    )
+    aside_part = lax.ppermute(far_sum, "dp", swap_side)
+    came_up = lax.ppermute(sent_up, "dp", swap_above)
+    far_output = pair_sum(bf16(mm_tn(far_hidden, flat_down)))
+    far_came = lax.ppermute(far_output, "dp", swap_side)
+    sent_down = bf16(mm(near_hidden[pair_block:], near_grad) + mm(far_hidden[pair_block:], far_grad))
+    came_down = lax.ppermute(sent_down, "dp", swap_above)
+    term_up = weight_grad(column, far_up, far_normed, weight_grad(column, near_up, normed))
+    term_down = mm(near_hidden[:pair_block], near_grad) + mm(far_hidden[:pair_block], far_grad)
 
     rider = jnp.arange(extra, dtype=jnp.int32)[:, None]
     lane = jnp.arange(128, dtype=jnp.int32)[None, :]
     collect = bf16(
-        ((rider < 2 * experts) & (lane == 0))
-        | ((rider >= 2 * experts) & (rider < 4 * experts) & (lane == 1 + rider % experts))
-    )
-    probs = jnp.pad(
-        rows_of(jnp.concatenate([opener_all, probs_all], axis=1)), ((0, 0), (0, 127 - experts))
+        ((rider < 2 * slots) & (lane == 0))
+        | ((rider >= 2 * slots) & (rider < 4 * slots) & (lane == 1 + rider % size))
+    )
+    probs = lax.dynamic_slice_in_dim(near_heads, me * rows, rows, 1).T
+    probs = jnp.pad(probs, ((0, 0), (0, 128 - probs.shape[1])))
+    part, aside_part, term_up, term_down, sent_down, far_output = lax.optimization_barrier(
+        (part, aside_part, term_up, term_down, sent_down, far_output)
     )
     grad_middle, grad_branch, grad_heads, term_norm_two = remote_call(
         branch_kernel,
         chips,
-        [part, middle, gain_two[None, :], rows_of(grad_rows), probs, collect, router_rows],
+        [
+            part,
+            aside_part.reshape(chips, rows, width + extra),
+            middle,
+            gain_two[None, :],
+            grad_own,
+            probs,
+            collect,
+            router_rows,
+        ],
         [
             ((rows, width), jnp.float32, False),
             ((group, width), jnp.bfloat16, True),
@@ -1065,9 +1286,31 @@
         + scatter_scratch(chips, rows, width + extra)
         + gather_scratch(chips),
         2,
-        75,
-    )
-    term_router = mm_tn(rows_of(normed_all), grad_heads)[:, : 1 + experts]
+        80,
+    )
+    grad_branch, came_up, far_came = lax.optimization_barrier((grad_branch, came_up, far_came))
+    term_router = mm_tn(rows_of(normed, me), grad_heads)[:, : 1 + experts]
+
+    which = (jnp.arange(2) == core)[None, :, None, None]
+    combined = near_output.reshape(chips, 2, rows, width).astype(jnp.float32)
+    combined = combined + jnp.where(
+        which, far_came.reshape(chips, 1, rows, width).astype(jnp.float32), 0.0
+    )
+    summed_part = bf16(combined).reshape(group, width)
+
+    shape = (2, half, pair_block, width // 2)
+    up = term_up.reshape(shape).astype(jnp.float32) + came_up.reshape(shape)[:, ::-1].astype(
+        jnp.float32
+    )
+    up = bf16(up).reshape(2 * hidden_units, width // 2)
+    quarter = width // 4
+    side_kept = lax.dynamic_slice_in_dim(up, side_by * quarter, quarter, 1)
+    side_given = lax.dynamic_slice_in_dim(up, (1 - side_by) * quarter, quarter, 1)
+    grad_branch, side_given, summed_part = lax.optimization_barrier(
+        (grad_branch, side_given, summed_part)
+    )
+    summed = lax.psum_scatter(summed_part, "expert", scatter_dimension=0, tiled=True)
+    side_came = lax.ppermute(side_given, "dp", swap_side)
 
     grad_attended = bf16(mm_nt(grad_branch, weight_out)).reshape(group, own_heads, HD)
     weights_again = jnp.exp(score_rows() - log_total)
@@ -1097,21 +1340,7 @@
             axis=1,
         ).reshape(group, own_qkv)
     )
-    input_grad, term_norm_one = remote_call(
-        input_kernel,
-        chips,
-        [
-            bf16(mm_nt(grad_projected, weight_qkv)),
-            hidden_in,
-            gain_one[None, :],
-            grad_middle,
-        ],
-        [((rows, width), jnp.bfloat16, False), ((1, width), jnp.float32, False)],
-        [pltpu.VMEM((rows, width), jnp.float32)] + scatter_scratch(chips, rows, width),
-        3,
-        40,
-    )
-
+    part = bf16(mm_nt(grad_projected, weight_qkv))
     term_out = bf16(mm_tn(attended, grad_branch)).reshape(half, 2, block, width)
     kept = jnp.where(core == 0, term_out[:, 0], term_out[:, 1])
     given = jnp.where(core == 0, term_out[:, 1], term_out[:, 0])
@@ -1119,7 +1348,55 @@
     out_blocks = jnp.concatenate(
         [jnp.where(core == 0, kept, came), jnp.where(core == 0, came, kept)], axis=0
     )
-    term_qkv = mm_tn(normed_one, grad_projected)
+    back = jnp.concatenate(
+        [bf16(mm_tn(normed_one, grad_projected)), out_blocks.reshape(width, out_cols)], axis=1
+    )
+    part, back, summed = lax.optimization_barrier((part, back, summed))
+    back = lax.psum_scatter(back, "dp", scatter_dimension=0, tiled=True)
+    grad_out_weight = back[:, own_qkv:].reshape(block, width).astype(jnp.float32)
+    input_grad, term_norm_one = remote_call(
+        input_kernel,
+        chips,
+        [part, hidden_in, gain_one[None, :], grad_middle],
+        [((rows, width), jnp.bfloat16, False), ((1, width), jnp.float32, False)],
+        [pltpu.VMEM((rows, width), jnp.float32)] + scatter_scratch(chips, rows, width),
+        3,
+        40,
+    )
+    grad_down = term_down + came_down.astype(jnp.float32)
+    grad_shared_out = grad_down[expert_block:]
+    grad_expert_out = grad_down[None, :expert_block]
+    up = ordered(side_by, side_kept[None], side_came[None], 0)
+    up = up.reshape(2, 2, half, pair_block, quarter)
+    up = ordered(above, up[:, :, :1], up[:, :, 1:], 2)
+    grad_expert_in = (
+        up[:, :, :, :expert_block]
+        .transpose(4, 1, 2, 0, 3)
+        .reshape(1, quarter, 2 * parts * expert_block)
+        .astype(jnp.float32)
+    )
+    cut = lax.all_to_all(
+        up[:, :, :, expert_block:].transpose(4, 1, 2, 0, 3).reshape(size, block, 2 * own_shared),
+        "expert",
+        split_axis=0,
+        concat_axis=0,
+        tiled=True,
+    )
+    grad_shared_in = (
+        cut.reshape(size, block, 2, parts, shared_block)
+        .transpose(1, 2, 3, 0, 4)
+        .reshape(block, 2 * parts * size * shared_block)
+        .astype(jnp.float32)
+    )
+    back = lax.all_to_all(
+        back[:, :own_qkv].reshape(size, block, own_qkv),
+        "expert",
+        split_axis=0,
+        concat_axis=0,
+        tiled=True,
+    )
+    grad_qkv = from_head(back).astype(jnp.float32)
+
     term_bias = jnp.sum(grad_projected.astype(jnp.float32), axis=0)
     bias_slots = jnp.where(jnp.arange(size)[:, None] == me, term_bias[None, :], 0.0)
     bias_rows = from_head(bias_slots[:, None, :]).reshape(width, bias_cols)
@@ -1127,38 +1404,20 @@
         [term_norm_one[0][:, None], term_norm_two[0][:, None], term_router, bias_rows], axis=1
     )
     count = small_terms.shape[1]
-    small_high, small_low = two_parts(small_terms)
-    small_terms = jnp.concatenate([small_high, small_low], axis=1)
-    small_terms = jnp.pad(small_terms, ((0, 0), (0, extra - 2 * count)))
-    back = lax.psum_scatter(
-        jnp.concatenate(
-            [bf16(term_qkv), small_terms, out_blocks.reshape(width, out_cols)], axis=1
-        ),
-        "dp",
-        scatter_dimension=0,
+    small_terms = lax.all_to_all(
+        small_terms.T.reshape(count, parts * size, block).transpose(1, 0, 2),
+        ("dp", "expert"),
+        split_axis=0,
+        concat_axis=0,
         tiled=True,
     )
-    grad_out_weight = back[:, own_qkv + extra :].reshape(block, width).astype(jnp.float32)
-    back = lax.all_to_all(
-        back[:, : own_qkv + extra].reshape(size, block, own_qkv + extra), "expert", split_axis=0, concat_axis=0, tiled=True
-    ).astype(jnp.float32)
-    grad_qkv = from_head(back[:, :, :own_qkv])
-    small_sum = jnp.sum(back[:, :, own_qkv:], axis=0)
-    small_sum = small_sum[:, :count] + small_sum[:, count : 2 * count]
-    (output,) = remote_call(
-        output_kernel,
-        chips,
-        [combined, middle, rows_of(valid_all)],
-        [((rows, width), jnp.bfloat16, False)],
-        [pltpu.VMEM((rows, width), jnp.float32)] + scatter_scratch(chips, rows, width),
-        4,
-        40,
-    )
-    grad_norm1 = small_sum[:, 0]
-    grad_norm2 = small_sum[:, 1]
-    grad_shared_gate = small_sum[:, 2]
-    grad_router = small_sum[:, 3 : 3 + experts]
-    grad_bias = small_sum[:, 3 + experts :].reshape(block * bias_cols)
+    small_sum = jnp.sum(small_terms, axis=0)
+    output = bf16(valid_rows * (middle + summed.astype(jnp.float32)))
+    grad_norm1 = small_sum[0]
+    grad_norm2 = small_sum[1]
+    grad_shared_gate = small_sum[2]
+    grad_router = small_sum[3 : 3 + experts].T
+    grad_bias = small_sum[3 + experts :].T.reshape(block * bias_cols)
     return (
         output,
         input_grad,
@@ -1181,7 +1440,7 @@
 
     def device(*arrays):
         block = arrays[5].shape[0]
-        whole_heads = 2 * block == HD and parts % 2 == 0 and size % 2 == 0
+        whole_heads = 2 * block == HD and parts == 4 and size % 2 == 0
         one_expert = arrays[13].shape[0] == 1
         if whole_heads and one_expert and arrays[5].shape[1] % (3 * size * HD) == 0:
             return group_device(*arrays)

time: 1000 us -> 924 us (0.924)
  waiting for transfers between devices: 265 us -> 105 us
  matrix products: 187 us -> 109 us
  other arithmetic: 43.8 us -> 99.7 us
  Pallas kernels: 361 us -> 412 us
  local copies, waits for them, and re-layouts: 104 us -> 130 us
  starting transfers between devices: 16.7 us -> 41.3 us
    reduce_scatter x3 -> x2, waiting for transfers between devices: 153 us -> 10 us  [the longest x1 10 us: group_device(): lax.psum_scatter(summed_part, 'expert', scatter_dimension=0, tiled=True)]
    pallas_call x0 -> x6, Pallas kernels: none -> 96.3 us  [the longest x2 57.4 us: experts_call(): pl.pallas_call(functools.partial(experts_kernel, experts, top, split, nea...]
    ppermute x0 -> x18, waiting for transfers between devices: none -> 71.2 us  [the longest x1 67.4 us: group_device(): side_came = lax.ppermute(side_given, 'dp', swap_side)]
    dot_general x5 -> x2, matrix products: 63.5 us -> 6.4 us  [mm_nt(): lax.dot_general(left, right, (((1,), (1,)), ((), ())), preferred_element_...]
    all_gather x3 -> x2, waiting for transfers between devices: 57.9 us -> 3.55 us  [the longest x1 3.55 us: group_device(): near_grad = lax.all_gather(near_grad, 'expert', axis=0, tiled=True)]
    pallas_call x5 -> x4, Pallas kernels: 361 us -> 316 us  [remote_call(): pl.pallas_call(functools.partial(kernel, chips), out_shape=[jax.ShapeDtyp...]
    all_to_all x3 -> x5, waiting for transfers between devices: 54.4 us -> 20.4 us  [the longest x1 14.4 us: group_device(): lax.all_to_all(back[:, :own_qkv].reshape(size, block, own_qkv), 'expert',...]
    dot_general x4 -> x6, matrix products: 52.6 us -> 31.1 us  [mm(): return jnp.dot(left, right, preferred_element_type=jnp.float32)]
  transfers between devices with their start and end apart: 11 -> 29, of which waited for: 5 -> 7; matrix products, arithmetic and copies ran while one was open for 20% -> 30% of each run, Pallas kernels for 28% -> 42%
where the time goes in v5:
time: 924 us; the launch traced here: 914 us
  Pallas kernels  412 us (45%)
  local copies, waits for them, and re-layouts  130 us (14%)
  matrix products  109 us (12%)
  waiting for transfers between devices  105 us (11%)
  other arithmetic  99.7 us (11%)
  starting transfers between devices  41.3 us (4%)
  between operations  15.5 us (2%)
    pallas_call x4, Pallas kernels, remote_call(): pl.pallas_call(functools.partial(kernel, chips), out_shape=[jax.ShapeDtyp...  316 us
    ppermute x1, waiting for transfers between devices, group_device(): side_came = lax.ppermute(side_given, 'dp', swap_side)  67.4 us
    pallas_call x2, Pallas kernels, experts_call(): pl.pallas_call(functools.partial(experts_kernel, experts, top, split, nea...  57.4 us
    dot_general x9, matrix products, mm_tn(): lax.dot_general(left, right, (((0,), (0,)), ((), ())), preferred_element_...  57.2 us
    pallas_call x4, Pallas kernels, weight_grad(): pl.pallas_call(weight_grad_kernel, out_shape=jax.ShapeDtypeStruct((count,...  38.9 us
    dot_general x6, matrix products, mm(): return jnp.dot(left, right, preferred_element_type=jnp.float32)  31.1 us
    unnamed x142, local copies, waits for them, and re-layouts  24.8 us
    convert_element_type x10, other arithmetic, bf16(): return values.astype(jnp.bfloat16)  21.3 us
  transfers between devices with their start and end apart: 29, of which 7 were waited for; matrix products, arithmetic and copies ran while one was open for 30% of the time, Pallas kernels for 42%

profile of v5, /device:TPU:0, one launch (start us, length us, event | category | flops | bytes accessed | tf_op | source)
XLA Modules:
  0.0 913.6 jit_solution(7040978088981665667)
XLA Ops:
  12.2 6.3 all-to-all-start
  18.6 4.5 copy.211
  28.1 4.2 fusion.60
  36.4 6.0 all-to-all-done
  45.0 5.0 reshape.482
  65.7 75.9 %shard_map.246 = bf16[1024,2176]{1,0:T(8,128)(2,1)} custom-call(bf16[128,2176]{1,0:T(8,128)(2,1)} %fusion.31.own), custom_call_target="tpu_custom_call" | custom-call | flops 40000000000 | bytes 557056 | tf_op jit(solution)/shard_map/pallas_call | solution.py:927
  148.3 8.3 reshape_reshape.10
  156.7 4.0 copy.222
  177.9 6.7 fusion.13
  189.4 13.2 %exponential_reduce_fusion = f32[2,1024]{1,0:T(2,128)S(1)} fusion(f32[2,1024,1024]{1,2,0:T(8,128)S(1)} %get-tuple-element.237, f32[2,1024]{1,0:T(2,128)S(1)} %get-tuple-element.236, pred[1024,1024]{0,1:T(8,128)(4,1)S(1)} %compare_and_fusion), kind=kLoop, calls=%fused_computation.16 | loop fusion | flops 8386560 | bytes 9453568 | tf_op jit(solution)/shard_map/reduce_sum | solution.py:1155
  224.8 86.8 %shard_map.247 = (f32[128,2048]{1,0:T(8,128)}, bf16[1024,2048]{1,0:T(8,128)(2,1)}) custom-call(bf16[1024,2048]{1,0:T(8,128)(2,1)} %convolution_convert_fusion.part, bf16[128,2048]{1,0:T(8,128)(2,1)} %hidden.3, f32[1,2048]{1,0:T(1,128)} %get-tuple-element.197.gain), custom_call_target="tpu_custom_call" | custom-call | flops 74999996416 | bytes 4726784 | tf_op jit(solution)/shard_map/pallas_call | solution.py:927
  315.6 4.0 pad_maximum_fusion.1.down
  319.6 29.9 %shard_map.248 = (bf16[2,528,1024]{2,1,0:T(8,128)(2,1)}, bf16[2,2,528,1024]{3,2,1,0:T(8,128)(2,1)}, f32[16,1024]{1,0:T(8,128)}, bf16[16,1024]{1,0:T(8,128)(2,1)}, bf16[2,2,528,2048]{3,2,1,0:T(8,128)(2,1)}) custom-call(s32[2]{0:T(128)} %pad_add_fusion.place, bf16[1024,2048]{1,0:T(8,128)(2,1)} %get-tuple-element.83.normed.right, ...), custom_call_target="tpu_custom_call" | custom-call | flops 4000000000 | bytes 1000000 | tf_op jit(solution)/shard_map/pallas_call | solution.py:865
  350.5 13.9 %bitcast_convert_fusion.1 = bf16[1024,2048]{1,0:T(8,128)(2,1)S(1)} fusion(bf16[2,2,528,1024]{3,2,1,0:T(8,128)(2,1)} %get-tuple-element.89, bf16[2,2,528,2048]{3,2,1,0:T(8,128)(2,1)} %get-tuple-element.90.rest_0_), kind=kOutput, calls=%fused_computation.8 | convolution fusion | flops 8860467200 | bytes 17170432 | tf_op jit(solution)/shard_map/dot_general | solution.py:962
  367.5 9.2 %shard_map.249.rest_0_ = bf16[2112,1024]{1,0:T(8,128)(2,1)} custom-call(s32[1]{0:T(128)S(6)} %sub.71.place, bf16[2112,1024]{1,0:T(8,128)(2,1)} %bitcast.226, bf16[1024,2048]{1,0:T(8,128)(2,1)} %get-tuple-element.83.normed.right), custom_call_target="tpu_custom_call" | custom-call | flops 3000000000 | bytes 1000000 | tf_op jit(solution)/shard_map/pallas_call | solution.py:906
  376.7 9.6 %bitcast_convert_fusion.2 = bf16[1024,2048]{1,0:T(8,128)(2,1)} fusion(bf16[2,528,1024]{2,1,0:T(8,128)(2,1)} %get-tuple-element.92, bf16[1,528,2048]{2,1,0:T(8,128)(2,1)} %bitcast.40, bf16[1,528,2048]{2,1,0:T(8,128)(2,1)S(1)} %copy-done.10), kind=kOutput, calls=%fused_computation.12 | convolution fusion | flops 4433444864 | bytes 10682368 | tf_op jit(solution)/shard_map/dot_general | solution.py:962
  386.3 4.8 pad_maximum_fusion.3.grads
  391.1 4.8 pad_maximum_fusion.2.normed.right
  395.9 27.5 %shard_map.250 = (bf16[2,528,1024]{2,1,0:T(8,128)(2,1)}, bf16[2,2,528,1024]{3,2,1,0:T(8,128)(2,1)}, f32[16,1024]{1,0:T(8,128)}, bf16[16,1024]{1,0:T(8,128)(2,1)}) custom-call(s32[2]{0:T(128)} %pad_add_fusion.place, bf16[1024,2048]{1,0:T(8,128)(2,1)} %pad_maximum_fusion.2.normed.right, bf16[1024,2048]{1,0:T(8,128)(2,1)} %pad_maximum_fusion.3.grads, ...), custom_call_target="tpu_custom_call" | custom-call | flops 4000000000 | bytes 1000000 | tf_op jit(solution)/shard_map/pallas_call | solution.py:865
  423.4 13.9 %bitcast_convert_fusion = bf16[1024,2048]{1,0:T(8,128)(2,1)S(1)} fusion(bf16[2,2,528,1024]{3,2,1,0:T(8,128)(2,1)} %get-tuple-element.96, bf16[2,2,528,2048]{3,2,1,0:T(8,128)(2,1)} %get-tuple-element.90.rest_0_), kind=kOutput, calls=%fused_computation.7 | convolution fusion | flops 8860467200 | bytes 17170432 | tf_op jit(solution)/shard_map/dot_general | solution.py:962
  442.2 10.2 %shard_map.251 = bf16[2112,1024]{1,0:T(8,128)(2,1)} custom-call(s32[1]{0:T(128)S(6)} %sub.71.place, bf16[2112,1024]{1,0:T(8,128)(2,1)} %bitcast.231, bf16[1024,2048]{1,0:T(8,128)(2,1)} %pad_maximum_fusion.2.normed.right, bf16[2112,1024]{1,0:T(8,128)(2,1)} %shard_map.249.rest_0_), custom_call_target="tpu_custom_call" | custom-call | flops 3000000000 | bytes 1000000 | tf_op jit(solution)/shard_map/pallas_call | solution.py:906
  455.4 8.3 convolution_convert_fusion.2
  468.1 4.5 fusion.18
  472.6 4.5 fusion.21
  477.1 9.2 %shard_map.252.rest_0_ = bf16[2112,1024]{1,0:T(8,128)(2,1)} custom-call(s32[1]{0:T(128)} %bitcast.35.place, bf16[2112,1024]{1,0:T(8,128)(2,1)} %bitcast.227, bf16[1024,2048]{1,0:T(8,128)(2,1)} %get-tuple-element.83.normed.right), custom_call_target="tpu_custom_call" | custom-call | flops 3000000000 | bytes 1000000 | tf_op jit(solution)/shard_map/pallas_call | solution.py:906
  486.3 10.2 %shard_map.253 = bf16[2112,1024]{1,0:T(8,128)(2,1)} custom-call(s32[1]{0:T(128)} %bitcast.35.place, bf16[2112,1024]{1,0:T(8,128)(2,1)} %bitcast.232, bf16[1024,2048]{1,0:T(8,128)(2,1)} %pad_maximum_fusion.2.normed.right, bf16[2112,1024]{1,0:T(8,128)(2,1)} %shard_map.252.rest_0_), custom_call_target="tpu_custom_call" | custom-call | flops 3000000000 | bytes 1000000 | tf_op jit(solution)/shard_map/pallas_call | solution.py:906
  496.6 7.7 add_convert_fusion.1
  504.3 4.5 convolution_add_fusion
  516.3 87.4 %shard_map.254 = (f32[128,2048]{1,0:T(8,128)}, bf16[1024,2048]{1,0:T(8,128)(2,1)}, bf16[128,128]{1,0:T(8,128)(2,1)}, f32[1,2048]{1,0:T(1,128)}) custom-call(bf16[1024,2176]{1,0:T(8,128)(2,1)} %pad_maximum_fusion.part, bf16[4,128,2176]{2,1,0:T(8,128)(2,1)} %bitcast.57.aside, f32[128,2048]{1,0:T(8,128)} %get-tuple-element.80.middle, ...), custom_call_target="tpu_custom_call" | custom-call | flops 80000000000 | bytes 8888320 | tf_op jit(solution)/shard_map/pallas_call | solution.py:927
  605.9 5.7 fusion
  620.0 3.9 convolution_convert_fusion.4
  626.5 4.6 multiply_reduce_fusion
  641.0 5.1 convolution_convert_fusion.3
  646.1 5.1 convolution_convert_fusion.1.part
  652.8 4.6 pad_maximum_fusion.4
  657.4 10.0 %reduce-scatter.3.cloned.1.call-done = bf16[128,2048]{1,0:T(8,128)(2,1)} async-done(((bf16[1024,2048]{1,0:T(8,128)(2,1)}), bf16[128,2048]{1,0:T(8,128)(2,1)}) %reduce-scatter.3.cloned.1.call-update) | async-done | bytes 524304 | tf_op jit(solution)/shard_map/reduce_scatter | solution.py:1312
  678.4 67.4 %collective-permute-done.18 = bf16[2112,512]{1,0:T(8,128)(2,1)} collective-permute-done((bf16[2112,512]{1,0:T(8,128)(2,1)S(1)}, bf16[2112,512]{1,0:T(8,128)(2,1)}, u32[]{:S(2)}, u32[]{:S(2)}) %collective-permute-start.18) | collective-permute-done | bytes 2162720 | tf_op jit(solution)/shard_map/ppermute | solution.py:1313
  751.9 6.1 copy.242
  758.0 6.4 reshape.520
  764.4 4.3 all-to-all-start.4
  768.7 66.0 %shard_map.255 = (bf16[128,2048]{1,0:T(8,128)(2,1)}, f32[1,2048]{1,0:T(1,128)}) custom-call(bf16[1024,2048]{1,0:T(8,128)(2,1)} %convolution_convert_fusion.1.part, bf16[128,2048]{1,0:T(8,128)(2,1)} %hidden.3, f32[1,2048]{1,0:T(1,128)} %get-tuple-element.196.gain, f32[128,2048]{1,0:T(8,128)} %get-tuple-element.119.grad_middle), custom_call_target="tpu_custom_call" | custom-call | flops 40000000000 | bytes 5775360 | tf_op jit(solution)/shard_map/pallas_call | solution.py:927
  836.5 4.4 all-to-all-start.2
  846.1 6.2 copy.245
  852.4 8.4 reshape.532
  860.8 6.7 copy.243
  867.5 5.6 reshape.529
  875.4 5.0 all-to-all-start.3
  887.0 14.4 %all-to-all-done.3 = bf16[8,64,768]{2,1,0:T(8,128)(2,1)S(1)} async-done(((bf16[8,64,768]{2,1,0:T(8,128)(2,1)}), bf16[8,64,768]{2,1,0:T(8,128)(2,1)S(1)}, u32[]{:S(2)}, u32[]{:S(2)}) %all-to-all-start.3) | async-done | bytes 786464 | tf_op jit(solution)/shard_map/all_to_all | solution.py:1391
  (337 shorter events, 173.3 us)
Async XLA Ops:
  12.2 30.2 %all-to-all-start = ((bf16[8,64,896]{2,1,0:T(8,128)(2,1)}), bf16[8,64,896]{2,1,0:T(8,128)(2,1)}, u32[]{:S(2)}, u32[]{:S(2)}) async-start(bf16[8,64,896]{2,1,0:T(8,128)(2,1)} %pad_maximum_fusion.14), calls=%async_computation | async-start | bytes 1835008 | tf_op jit(solution)/shard_map/all_to_all | solution.py:1071
  18.5 147.9 %all-gather.3.cloned.1.call-start = ((), (), s32[]{:S(2)}) async-start(), calls=%async_computation.7 | async-start | bytes 5898240 | tf_op jit(solution)/shard_map/all_gather | solution.py:1074
  26.6 139.8 %collective-permute-start = (bf16[1408,512]{1,0:T(8,128)(2,1)}, bf16[1408,512]{1,0:T(8,128)(2,1)}, u32[]{:S(2)}, u32[]{:S(2)}) collective-permute-start(bf16[1408,512]{1,0:T(8,128)(2,1)} %dynamic-slice_bitcast_fusion), channel_id=1, source_target_pairs={{0,8},{8,0},{16,24},{24,16},{1,9},{9,1},{17,25},{25,17},{2,10},{10... | collective-permute-start | bytes 4325384 | tf_op jit(solution)/shard_map/ppermute | solution.py:1053
  32.4 12.7 %copy-start.28 = (bf16[64,11264]{1,0:T(8,128)(2,1)S(1)}, bf16[64,11264]{1,0:T(8,128)(2,1)}, u32[]{:S(2)}) copy-start(bf16[64,11264]{1,0:T(8,128)(2,1)} %param.26) | copy-start | bytes 4325380
  32.4 283.2 %collective-permute-start.9 = (bf16[528,2048]{1,0:T(8,128)(2,1)}, bf16[528,2048]{1,0:T(8,128)(2,1)}, u32[]{:S(2)}, u32[]{:S(2)}) collective-permute-start(bf16[528,2048]{1,0:T(8,128)(2,1)} %get-tuple-element.208), channel_id=1, source_target_pairs={{0,16},{8,24},{16,0},{24,8},{1,17},{9,25},{17,1},{25,9},{2,18},{10... | collective-permute-start | bytes 6488072 | tf_op jit(solution)/shard_map/ppermute | solution.py:1044
  56.0 85.5 %copy-start.45 = (f32[128]{0:T(128)}, f32[128]{0:T(128)S(1)}, u32[]{:S(2)}) copy-start(f32[128]{0:T(128)S(1)} %dynamic-slice.3) | copy-start | bytes 1540
  62.0 142.2 %copy-start.1 = (pred[1024,1024]{0,1:T(8,128)(4,1)}, pred[1024,1024]{0,1:T(8,128)(4,1)S(1)}, u32[]{:S(2)}) copy-start(pred[1024,1024]{0,1:T(8,128)(4,1)S(1)} %compare_and_fusion) | copy-start | bytes 3145732
  62.0 80.5 %all-to-all-start.1 = ((bf16[8,64,1408]{2,1,0:T(8,128)(2,1)}), bf16[8,64,1408]{2,1,0:T(8,128)(2,1)S(1)}, u32[]{:S(2)}, u32[]{:S(2)}) async-start(bf16[8,64,1408]{2,1,0:T(8,128)(2,1)} %reshape.483), calls=%async_computation.1 | async-start | bytes 2883584 | tf_op jit(solution)/shard_map/all_to_all | solution.py:1089
  65.6 75.9 %copy-start.34 = (bf16[128,2048]{1,0:T(8,128)(2,1)S(1)}, bf16[128,2048]{1,0:T(8,128)(2,1)}, u32[]{:S(2)}) copy-start(bf16[128,2048]{1,0:T(8,128)(2,1)} %param.16) | copy-start | bytes 1572868
  65.6 150.6 %all-gather.5.cloned.1.call-start = ((), (), s32[]{:S(2)}) async-start(), calls=%async_computation.8 | async-start | bytes 4718592 | tf_op jit(solution)/shard_map/all_gather | solution.py:1103
  143.7 17.0 %copy-start.27 = (bf16[1024,128]{1,0:T(8,128)(2,1)}, bf16[1024,128]{1,0:T(8,128)(2,1)S(1)}, u32[]{:S(2)}) copy-start(bf16[1024,128]{1,0:T(8,128)(2,1)S(1)} %slice.158.side) | copy-start | bytes 786436
  143.7 19.5 %collective-permute-start.10 = (bf16[512,128]{1,0:T(8,128)(2,1)S(1)}, bf16[512,128]{1,0:T(8,128)(2,1)}, u32[]{:S(2)}, u32[]{:S(2)}) collective-permute-start(bf16[512,128]{1,0:T(8,128)(2,1)S(1)} %bitcast.267), channel_id=1, source_target_pairs={{0,8},{8,0},{16,24},{24,16},{1,9},{9,1},{17,25},{25,17},{2,10},{10... | collective-permute-start | bytes 393224 | tf_op jit(solution)/shard_map/ppermute | solution.py:1037
  162.7 56.7 %collective-permute-start.2 = (bf16[704,512]{1,0:T(8,128)(2,1)}, bf16[704,512]{1,0:T(8,128)(2,1)}, u32[]{:S(2)}, u32[]{:S(2)}) collective-permute-start(bf16[704,512]{1,0:T(8,128)(2,1)} %dynamic-slice_bitcast_fusion.1), channel_id=1, source_target_pairs={{0,8},{8,0},{16,24},{24,16},{1,9},{9,1},{17,25},{25,17},{2,10},{10... | collective-permute-start | bytes 2162696 | tf_op jit(solution)/shard_map/ppermute | solution.py:1053
  163.2 1.6 collective-permute-start.11
  163.2 14.7 %copy-start.43 = (f32[1024]{0:T(1024)}, f32[1024]{0:T(1024)S(1)}, u32[]{:S(2)}) copy-start(f32[1024]{0:T(1024)S(1)} %add_rsqrt_fusion) | copy-start | bytes 12292
  169.6 497.8 %reduce-scatter.3.cloned.1.call-start = ((), (), s32[]{:S(2)}) async-start(), calls=%async_computation.9 | async-start | bytes 4718592 | tf_op jit(solution)/shard_map/reduce_scatter | solution.py:1312
  169.7 37.1 %collective-permute-start.1 = (bf16[2,64,2048]{2,1,0:T(8,128)(2,1)S(1)}, bf16[2,64,2048]{2,1,0:T(8,128)(2,1)}, u32[]{:S(2)}, u32[]{:S(2)}) collective-permute-start(bf16[2,64,2048]{2,1,0:T(8,128)(2,1)S(1)} %constant_dynamic-slice_fusion.4), channel_id=1, source_target_pairs={{0,1},{1,0},{2,3},{3,2},{4,5},{5,4},{6,7},{7,6},{8,9},{9,8},{10,11... | collective-permute-start | bytes 1572872 | tf_op jit(solution)/shard_map/ppermute | solution.py:1130
  174.9 140.6 %collective-permute-start.7 = (bf16[1408,1024]{1,0:T(8,128)(2,1)}, bf16[1408,1024]{1,0:T(8,128)(2,1)}, u32[]{:S(2)}, u32[]{:S(2)}) collective-permute-start(bf16[1408,1024]{1,0:T(8,128)(2,1)} %pad_maximum_fusion.6), channel_id=1, source_target_pairs={{0,16},{8,24},{16,0},{24,8},{1,17},{9,25},{17,1},{25,9},{2,18},{10... | collective-permute-start | bytes 8650760 | tf_op jit(solution)/shard_map/ppermute | solution.py:1112
  184.6 19.5 %copy-start.9 = (f32[1024,768]{0,1:T(8,128)}, f32[1024,768]{0,1:T(8,128)S(1)}, u32[]{:S(2)}) copy-start(f32[1024,768]{0,1:T(8,128)S(1)} %fusion.13) | copy-start | bytes 9437188
  189.4 14.8 %copy-start = (f32[2,1024,1024]{1,2,0:T(8,128)}, f32[2,1024,1024]{1,2,0:T(8,128)S(1)}, u32[]{:S(2)}) copy-start(f32[2,1024,1024]{1,2,0:T(8,128)S(1)} %get-tuple-element.237) | copy-start | bytes 25165828
  209.3 10.0 %copy-start.12 = (bf16[2,2,2,176,512]{4,3,2,1,0:T(8,128)(2,1)S(1)}, bf16[2,2,2,176,512]{4,3,2,1,0:T(8,128)(2,1)}, u32[]{:S(2)}) copy-start(bf16[2,2,2,176,512]{4,3,2,1,0:T(8,128)(2,1)} %copy.222) | copy-start | bytes 4325380
  221.9 93.7 %collective-permute-start.8 = (bf16[704,1024]{1,0:T(8,128)(2,1)}, bf16[704,1024]{1,0:T(8,128)(2,1)}, u32[]{:S(2)}, u32[]{:S(2)}) collective-permute-start(bf16[704,1024]{1,0:T(8,128)(2,1)} %pad_maximum_fusion.10), channel_id=1, source_target_pairs={{0,16},{8,24},{16,0},{24,8},{1,17},{9,25},{17,1},{25,9},{2,18},{10... | collective-permute-start | bytes 4325384 | tf_op jit(solution)/shard_map/ppermute | solution.py:1167
  223.4 141.1 %collective-permute-start.5 = (bf16[512,2048]{1,0:T(8,128)(2,1)}, bf16[512,2048]{1,0:T(8,128)(2,1)}, u32[]{:S(2)}, u32[]{:S(2)}) collective-permute-start(bf16[512,2048]{1,0:T(8,128)(2,1)} %bitcast.26), channel_id=1, source_target_pairs={{0,8},{8,0},{16,24},{24,16},{1,9},{9,1},{17,25},{25,17},{2,10},{10... | collective-permute-start | bytes 6291464 | tf_op jit(solution)/shard_map/ppermute | solution.py:1165
  315.0 52.1 %collective-permute-start.3 = (bf16[512,2048]{1,0:T(8,128)(2,1)}, bf16[512,2048]{1,0:T(8,128)(2,1)}, u32[]{:S(2)}, u32[]{:S(2)}) collective-permute-start(bf16[512,2048]{1,0:T(8,128)(2,1)} %bitcast.34), channel_id=1, source_target_pairs={{0,8},{8,0},{16,24},{24,16},{1,9},{9,1},{17,25},{25,17},{2,10},{10... | collective-permute-start | bytes 6291464 | tf_op jit(solution)/shard_map/ppermute | solution.py:1037
  319.6 29.9 %copy-start.47 = (pred[16]{0:T(512)(128)(4,1)S(1)}, pred[16]{0:T(512)(128)(4,1)}, u32[]{:S(2)}) copy-start(pred[16]{0:T(512)(128)(4,1)} %iota_compare_fusion.8) | copy-start | bytes 52
  319.6 29.9 %copy-start.48 = (s32[16]{0:T(128)S(1)}, s32[16]{0:T(128)}, u32[]{:S(2)}) copy-start(s32[16]{0:T(128)} %multiply_add_fusion) | copy-start | bytes 196
  364.4 21.9 %collective-permute-start.6 = (bf16[512,2048]{1,0:T(8,128)(2,1)}, bf16[512,2048]{1,0:T(8,128)(2,1)}, u32[]{:S(2)}, u32[]{:S(2)}) collective-permute-start(bf16[512,2048]{1,0:T(8,128)(2,1)} %collective-permute-done.5), channel_id=1, source_target_pairs={{0,1},{1,0},{2,3},{3,2},{4,5},{5,4},{6,7},{7,6},{8,9},{9,8},{10,11... | collective-permute-start | bytes 6291464 | tf_op jit(solution)/shard_map/ppermute | solution.py:1181
  367.1 24.0 %collective-permute-start.4 = (bf16[512,2048]{1,0:T(8,128)(2,1)}, bf16[512,2048]{1,0:T(8,128)(2,1)}, u32[]{:S(2)}, u32[]{:S(2)}) collective-permute-start(bf16[512,2048]{1,0:T(8,128)(2,1)} %collective-permute-done.3), channel_id=1, source_target_pairs={{0,1},{1,0},{2,3},{3,2},{4,5},{5,4},{6,7},{7,6},{8,9},{9,8},{10,11... | collective-permute-start | bytes 6291464 | tf_op jit(solution)/shard_map/ppermute | solution.py:1038
  423.4 13.9 %copy-start.39 = (bf16[16,1024]{1,0:T(8,128)(2,1)S(1)}, bf16[16,1024]{1,0:T(8,128)(2,1)}, u32[]{:S(2)}) copy-start(bf16[16,1024]{1,0:T(8,128)(2,1)} %get-tuple-element.97) | copy-start | bytes 98308
  439.5 12.9 %collective-permute-start.12 = (bf16[512,2176]{1,0:T(8,128)(2,1)S(1)}, bf16[512,2176]{1,0:T(8,128)(2,1)}, u32[]{:S(2)}, u32[]{:S(2)}) collective-permute-start(bf16[512,2176]{1,0:T(8,128)(2,1)S(1)} %pad_maximum_fusion.7), channel_id=1, source_target_pairs={{0,1},{1,0},{2,3},{3,2},{4,5},{5,4},{6,7},{7,6},{8,9},{9,8},{10,11... | collective-permute-start | bytes 6684680 | tf_op jit(solution)/shard_map/ppermute | solution.py:1232
  455.4 12.3 %copy-start.55 = (bf16[2,528,1024]{2,1,0:T(8,128)(2,1)S(1)}, bf16[2,528,1024]{2,1,0:T(8,128)(2,1)}, u32[]{:S(2)}) copy-start(bf16[2,528,1024]{2,1,0:T(8,128)(2,1)} %get-tuple-element.92) | copy-start | bytes 6488068
  465.2 43.6 %collective-permute-start.14 = (bf16[512,2048]{1,0:T(8,128)(2,1)}, bf16[512,2048]{1,0:T(8,128)(2,1)}, u32[]{:S(2)}, u32[]{:S(2)}) collective-permute-start(bf16[512,2048]{1,0:T(8,128)(2,1)} %slice.200), channel_id=1, source_target_pairs={{0,1},{1,0},{2,3},{3,2},{4,5},{5,4},{6,7},{7,6},{8,9},{9,8},{10,11... | collective-permute-start | bytes 6291464 | tf_op jit(solution)/shard_map/ppermute | solution.py:1232
  465.6 50.6 %collective-permute-start.13 = (bf16[512,2176]{1,0:T(8,128)(2,1)S(1)}, bf16[512,2176]{1,0:T(8,128)(2,1)}, u32[]{:S(2)}, u32[]{:S(2)}) collective-permute-start(bf16[512,2176]{1,0:T(8,128)(2,1)S(1)} %add_convert_fusion), channel_id=1, source_target_pairs={{0,8},{8,0},{16,24},{24,16},{1,9},{9,1},{17,25},{25,17},{2,10},{10... | collective-permute-start | bytes 6684680 | tf_op jit(solution)/shard_map/ppermute | solution.py:1243
  467.1 136.6 %collective-permute-start.15 = (bf16[2112,1024]{1,0:T(8,128)(2,1)}, bf16[2112,1024]{1,0:T(8,128)(2,1)}, u32[]{:S(2)}, u32[]{:S(2)}) collective-permute-start(bf16[2112,1024]{1,0:T(8,128)(2,1)} %shard_map.251), channel_id=1, source_target_pairs={{0,16},{8,24},{16,0},{24,8},{1,17},{9,25},{17,1},{25,9},{2,18},{10... | collective-permute-start | bytes 12976136 | tf_op jit(solution)/shard_map/ppermute | solution.py:1244
  486.3 18.0 %slice-start.6 = ((s8[4325376]{0:T(1024)(128)(4,1)}), s8[131072]{0:T(1024)(128)(4,1)S(1)}, s32[]{:S(2)}) async-start(s8[4325376]{0:T(1024)(128)(4,1)} %bitcast.282), calls=%async_computation.17 | async-start | bytes 262144
  512.6 91.1 %collective-permute-start.16 = (bf16[512,2048]{1,0:T(8,128)(2,1)}, bf16[512,2048]{1,0:T(8,128)(2,1)}, u32[]{:S(2)}, u32[]{:S(2)}) collective-permute-start(bf16[512,2048]{1,0:T(8,128)(2,1)} %add_convert_fusion.2), channel_id=1, source_target_pairs={{0,8},{8,0},{16,24},{24,16},{1,9},{9,1},{17,25},{25,17},{2,10},{10... | collective-permute-start | bytes 6291464 | tf_op jit(solution)/shard_map/ppermute | solution.py:1246
  619.0 254.1 %reduce-scatter.5.cloned.1.call-start = ((), (), s32[]{:S(2)}) async-start(), calls=%async_computation.10 | async-start | bytes 5242880 | tf_op jit(solution)/shard_map/reduce_scatter | solution.py:1355
  619.0 50.0 %collective-permute-start.19 = (bf16[528,2048]{1,0:T(8,128)(2,1)}, bf16[528,2048]{1,0:T(8,128)(2,1)}, u32[]{:S(2)}, u32[]{:S(2)}) collective-permute-start(bf16[528,2048]{1,0:T(8,128)(2,1)} %add_convert_fusion.1), channel_id=1, source_target_pairs={{0,16},{8,24},{16,0},{24,8},{1,17},{9,25},{17,1},{25,9},{2,18},{10... | collective-permute-start | bytes 6488072 | tf_op jit(solution)/shard_map/ppermute | solution.py:1248
  624.0 27.3 %collective-permute-start.17 = (bf16[2,64,2048]{2,1,0:T(8,128)(2,1)S(1)}, bf16[2,64,2048]{2,1,0:T(8,128)(2,1)S(1)}, u32[]{:S(2)}, u32[]{:S(2)}) collective-permute-start(bf16[2,64,2048]{2,1,0:T(8,128)(2,1)S(1)} %select_bitcast_fusion), channel_id=1, source_target_pairs={{0,1},{1,0},{2,3},{3,2},{4,5},{5,4},{6,7},{7,6},{8,9},{9,8},{10,11... | collective-permute-start | bytes 1572872 | tf_op jit(solution)/shard_map/ppermute | solution.py:1347
  657.4 10.1 %copy-start.19 = (bf16[2112,512]{1,0:T(8,128)(2,1)S(1)}, bf16[2112,512]{1,0:T(8,128)(2,1)}, u32[]{:S(2)}) copy-start(bf16[2112,512]{1,0:T(8,128)(2,1)} %constant_dynamic-slice_fusion) | copy-start | bytes 6488068
  667.5 78.4 %collective-permute-start.18 = (bf16[2112,512]{1,0:T(8,128)(2,1)S(1)}, bf16[2112,512]{1,0:T(8,128)(2,1)}, u32[]{:S(2)}, u32[]{:S(2)}) collective-permute-start(bf16[2112,512]{1,0:T(8,128)(2,1)S(1)} %copy-done.19), channel_id=1, source_target_pairs={{0,8},{8,0},{16,24},{24,16},{1,9},{9,1},{17,25},{25,17},{2,10},{10... | collective-permute-start | bytes 6488072 | tf_op jit(solution)/shard_map/ppermute | solution.py:1313
  764.4 72.1 %all-to-all-start.4 = ((bf16[8,64,1408]{2,1,0:T(8,128)(2,1)}), bf16[8,64,1408]{2,1,0:T(8,128)(2,1)}, u32[]{:S(2)}, u32[]{:S(2)}) async-start(bf16[8,64,1408]{2,1,0:T(8,128)(2,1)} %reshape.520), calls=%async_computation.6 | async-start | bytes 2883584 | tf_op jit(solution)/shard_map/all_to_all | solution.py:1378
  768.7 66.0 %copy-start.42 = (f32[1,2048]{1,0:T(1,128)S(1)}, f32[1,2048]{1,0:T(1,128)}, u32[]{:S(2)}) copy-start(f32[1,2048]{1,0:T(1,128)} %get-tuple-element.122) | copy-start | bytes 24580
  836.5 38.9 %all-to-all-start.2 = ((f32[32,1,896]{2,1,0:T(1,128)}), f32[32,1,896]{2,1,0:T(1,128)S(1)}, u32[]{:S(2)}, u32[]{:S(2)}) async-start(f32[32,1,896]{2,1,0:T(1,128)} %reshape.537), calls=%async_computation.3 | async-start | bytes 229376 | tf_op jit(solution)/shard_map/all_to_all | solution.py:1407
  867.5 12.9 %copy-start.31 = (f32[128,2048]{1,0:T(8,128)S(1)}, f32[128,2048]{1,0:T(8,128)}, u32[]{:S(2)}) copy-start(f32[128,2048]{1,0:T(8,128)} %get-tuple-element.80.middle) | copy-start | bytes 3145732
  867.5 13.0 %copy-start.32 = (bf16[128,2048]{1,0:T(8,128)(2,1)S(1)}, bf16[128,2048]{1,0:T(8,128)(2,1)}, u32[]{:S(2)}) copy-start(bf16[128,2048]{1,0:T(8,128)(2,1)} %reduce-scatter.3.cloned.1.call-done) | copy-start | bytes 1572868
  867.5 13.0 %copy-start.46 = (f32[128]{0:T(128)S(1)}, f32[128]{0:T(128)}, u32[]{:S(2)}) copy-start(f32[128]{0:T(128)} %copy-done.45) | copy-start | bytes 1540
  875.4 26.0 %all-to-all-start.3 = ((bf16[8,64,768]{2,1,0:T(8,128)(2,1)}), bf16[8,64,768]{2,1,0:T(8,128)(2,1)S(1)}, u32[]{:S(2)}, u32[]{:S(2)}) async-start(bf16[8,64,768]{2,1,0:T(8,128)(2,1)} %bitcast.84), calls=%async_computation.5 | async-start | bytes 1572864 | tf_op jit(solution)/shard_map/all_to_all | solution.py:1391
  (49 other events, 200.1 us)
Sparse Core Ops, SparseCore 0:
  45.1 74.6 all-gather.2
  169.7 46.4 all-gather.4
  619.1 48.3 reduce-scatter.2
  670.3 79.0 reduce-scatter.4
